TPU v7x, 32 devices: a whole 2x2x4 slice. The times are simulated.
32 devices in a mesh: fsdp: 8 (over z, y), seq: 4 (over x, core).
Axes of the slice: x: 2, y: 2, z: 4, core: 2. Of those that a mesh axis runs over, the one named last changes fastest.
Arguments:
- tokens: bfloat16 [16, 1024, 1024], P('fsdp', 'seq'), may hold values from -6 to 6
- cotangent: bfloat16 [16, 1024, 1024], P('fsdp', 'seq'), may hold values from -6 to 6
- lengths: int32 [16], P('fsdp'), may hold values from 256 to 1024, as said below
- first_gain: bfloat16 [1024], P('fsdp'), may hold values from 0.25 to 1.75
- first_shift: bfloat16 [1024], P('fsdp'), may hold values from -3 to 3
- qkv_weight: bfloat16 [1024, 3072], P('fsdp'), may hold values from -0.1875 to 0.1875
- qv_bias: bfloat16 [2, 1024], P(None, 'fsdp'), may hold values from -3 to 3
- out_weight: bfloat16 [1024, 1024], P('fsdp'), may hold values from -0.375 to 0.375
- out_bias: bfloat16 [1024], P('fsdp'), may hold values from -2 to 2
- second_gain: bfloat16 [1024], P('fsdp'), may hold values from 0.25 to 1.75
- second_shift: bfloat16 [1024], P('fsdp'), may hold values from -3 to 3
- up_weight: bfloat16 [1024, 4096], P('fsdp'), may hold values from -0.1875 to 0.1875
- up_bias: bfloat16 [4096], P('fsdp'), may hold values from -3 to 3
- down_weight: bfloat16 [4096, 1024], P('fsdp'), may hold values from -0.09375 to 0.09375
- down_bias: bfloat16 [1024], P('fsdp'), may hold values from -2 to 2
Outputs:
- block_out: bfloat16 [16, 1024, 1024], P('fsdp', 'seq')
- tokens_grad: bfloat16 [16, 1024, 1024], P('fsdp', 'seq')
- first_gain_grad: float32 [1024], P(('fsdp', 'seq'))
- first_shift_grad: float32 [1024], P(('fsdp', 'seq'))
- qkv_weight_grad: float32 [1024, 3072], P(('fsdp', 'seq'))
- qv_bias_grad: float32 [2, 1024], P(None, ('fsdp', 'seq'))
- out_weight_grad: float32 [1024, 1024], P(('fsdp', 'seq'))
- out_bias_grad: float32 [1024], P(('fsdp', 'seq'))
- second_gain_grad: float32 [1024], P(('fsdp', 'seq'))
- second_shift_grad: float32 [1024], P(('fsdp', 'seq'))
- up_weight_grad: float32 [1024, 4096], P(('fsdp', 'seq'))
- up_bias_grad: float32 [4096], P(('fsdp', 'seq'))
- down_weight_grad: float32 [4096, 1024], P(('fsdp', 'seq'))
- down_bias_grad: float32 [1024], P(('fsdp', 'seq'))
Inputs may be any that keep to these rules, and one draw needn't show every extreme that they name: `lengths`: at least a quarter of 1024; in every draw some sequence has all 1024 slots valid.
All inputs are finite; a program needn't handle non-finite values.
Results may differ from a plain program's by a relative error of at most 0.011.
Values may be sent and summed in bfloat16 or wider, within the bound.
No kernel may reach another device: no remote copies, remote signals or barrier semaphores. Data moves between devices by JAX's collectives and lax.ppermute only.
A program may use at most 256 MiB of HBM per device.

v0:
```python
from functools import partial
import math

import jax
import jax.numpy as jnp
from jax import lax
from jax.sharding import PartitionSpec as P

H = 16


epsilon = 1e-05


def layer_norm(values, norm_gain, norm_shift):
    row_mean = jnp.mean(values, axis=-1, keepdims=True)
    centered = values - row_mean
    variance = jnp.mean(centered * centered, axis=-1, keepdims=True)
    return centered * lax.rsqrt(variance + epsilon) * norm_gain + norm_shift


def contract_rows(left_side, right_side):
    return lax.dot_general(
        left_side, right_side, (((0,), (0,)), ((), ())), preferred_element_type=jnp.float32
    )


def against(left_side, right_side):
    return lax.dot_general(
        left_side, right_side, (((1,), (1,)), ((), ())), preferred_element_type=jnp.float32
    )


def head_scores(query_block, key_rows, start_row, slopes, length, score_scale):
    block_size = query_block.shape[1]
    seq_len = key_rows.shape[1]
    row_index = start_row + jnp.arange(block_size)
    columns = jnp.arange(seq_len)
    products = jnp.einsum("hqd,hkd->hqk", query_block, key_rows, preferred_element_type=jnp.float32)
    distance = (columns[None, :] - row_index[:, None]).astype(jnp.float32)
    allowed = (columns[None, :] <= row_index[:, None]) & (columns[None, :] < length)
    return jnp.where(
        allowed[None], products * score_scale + slopes[:, None, None] * distance, -jnp.inf
    )


def attend(queries, key_rows, value_rows, length, slopes, score_scale):
    head_count, seq_len, head_size = queries.shape
    block_size = math.gcd(512, seq_len)

    def one_block(start_row):
        query_block = lax.dynamic_slice_in_dim(queries, start_row, block_size, 1)
        scores = head_scores(query_block, key_rows, start_row, slopes, length, score_scale)
        largest = jnp.max(scores, axis=-1, keepdims=True)
        log_total = largest + jnp.log(jnp.sum(jnp.exp(scores - largest), axis=-1, keepdims=True))
        attention_probs = jnp.exp(scores - log_total).astype(jnp.bfloat16)
        mixed_rows = jnp.einsum(
            "hqk,hkd->hqd", attention_probs, value_rows, preferred_element_type=jnp.float32
        )
        return (mixed_rows.astype(jnp.bfloat16), log_total[..., 0])

    starts = jnp.arange(seq_len // block_size, dtype=jnp.int32) * block_size
    mixed_rows, log_totals = lax.map(one_block, starts)
    return (
        jnp.moveaxis(mixed_rows, 0, 1).reshape(head_count, seq_len, head_size),
        jnp.moveaxis(log_totals, 0, 1).reshape(head_count, seq_len),
    )


def attend_back(queries, key_rows, value_rows, grad_mixed, log_totals, length, slopes, score_scale):
    head_count, seq_len, head_size = queries.shape
    block_size = math.gcd(512, seq_len)

    def one_block(carried, start_row):
        key_sum, value_sum = carried
        query_block = lax.dynamic_slice_in_dim(queries, start_row, block_size, 1)
        grad_block = lax.dynamic_slice_in_dim(grad_mixed, start_row, block_size, 1)
        total_block = lax.dynamic_slice_in_dim(log_totals, start_row, block_size, 1)
        scores = head_scores(query_block, key_rows, start_row, slopes, length, score_scale)
        attention_probs = jnp.exp(scores - total_block[..., None])
        grad_probs = jnp.einsum(
            "hqd,hkd->hqk", grad_block, value_rows, preferred_element_type=jnp.float32
        )
        row_inner = jnp.sum(attention_probs * grad_probs, axis=-1, keepdims=True)
        grad_scores = (attention_probs * (grad_probs - row_inner)).astype(jnp.bfloat16)
        query_grad = (
            jnp.einsum("hqk,hkd->hqd", grad_scores, key_rows, preferred_element_type=jnp.float32)
            * score_scale
        ).astype(jnp.bfloat16)
        key_sum = (
            key_sum
            + jnp.einsum(
                "hqk,hqd->hkd", grad_scores, query_block, preferred_element_type=jnp.float32
            )
            * score_scale
        )
        value_sum = value_sum + jnp.einsum(
            "hqk,hqd->hkd",
            attention_probs.astype(jnp.bfloat16),
            grad_block,
            preferred_element_type=jnp.float32,
        )
        return ((key_sum, value_sum), query_grad)

    starts = jnp.arange(seq_len // block_size, dtype=jnp.int32) * block_size
    empty = jnp.zeros(queries.shape, jnp.float32)
    (key_sum, value_sum), query_grads = lax.scan(one_block, (empty, empty), starts)
    query_grad = jnp.moveaxis(query_grads, 0, 1).reshape(head_count, seq_len, head_size)
    return (query_grad, key_sum.astype(jnp.bfloat16), value_sum.astype(jnp.bfloat16))


def forward_pass(token_rows, length, whole, positions, slopes, score_scale):
    (
        first_gain,
        first_shift,
        qkv_weight,
        qv_bias,
        out_weight,
        out_bias,
        second_gain,
        second_shift,
        up_weight,
        up_bias,
        down_weight,
        down_bias,
    ) = whole
    seq_shards = lax.axis_size("seq")
    row_count, model_width = token_rows.shape
    head_size = model_width // H
    local_heads = H // seq_shards
    seq_len = row_count * seq_shards
    valid_mask = (positions < length).astype(jnp.float32)[:, None]
    row_values = token_rows.astype(jnp.float32)
    normed = layer_norm(
        row_values, first_gain.astype(jnp.float32), first_shift.astype(jnp.float32)
    ).astype(jnp.bfloat16)
    bias_float = qv_bias.astype(jnp.float32)
    bias_columns = jnp.stack(
        [
            bias_float[0].reshape(H, head_size),
            jnp.zeros((H, head_size), jnp.float32),
            bias_float[1].reshape(H, head_size),
        ],
        axis=1,
    ).reshape(3 * model_width)
    projected = (
        jnp.dot(normed, qkv_weight, preferred_element_type=jnp.float32) + bias_columns
    ).astype(jnp.bfloat16)
    by_head = lax.all_to_all(
        projected.reshape(row_count, seq_shards, 3 * local_heads * head_size),
        "seq",
        split_axis=1,
        concat_axis=0,
        tiled=True,
    )
    by_head = jnp.moveaxis(by_head.reshape(seq_len, local_heads, 3, head_size), 0, 2)
    queries, key_rows, value_rows = (by_head[:, 0], by_head[:, 1], by_head[:, 2])
    mixed_heads, log_totals = attend(queries, key_rows, value_rows, length, slopes, score_scale)
    mixed_rows = lax.all_to_all(
        jnp.moveaxis(mixed_heads, 0, 1).reshape(seq_shards, row_count, 1, local_heads * head_size),
        "seq",
        split_axis=0,
        concat_axis=2,
        tiled=True,
    ).reshape(row_count, model_width)
    middle = row_values + (
        jnp.dot(mixed_rows, out_weight, preferred_element_type=jnp.float32)
        + out_bias.astype(jnp.float32)
    )
    normed_two = layer_norm(
        middle, second_gain.astype(jnp.float32), second_shift.astype(jnp.float32)
    ).astype(jnp.bfloat16)
    hidden_pre = jnp.dot(
        normed_two, up_weight, preferred_element_type=jnp.float32
    ) + up_bias.astype(jnp.float32)
    activation = jax.nn.gelu(hidden_pre, approximate=True).astype(jnp.bfloat16)
    block_rows = (
        valid_mask
        * (
            middle
            + jnp.dot(activation, down_weight, preferred_element_type=jnp.float32)
            + down_bias.astype(jnp.float32)
        )
    ).astype(jnp.bfloat16)
    saved = (
        normed,
        queries,
        key_rows,
        value_rows,
        mixed_heads,
        log_totals,
        mixed_rows,
        middle,
        normed_two,
        hidden_pre,
        activation,
    )
    return (block_rows, saved)


def backward_pass(token_rows, grad_rows, length, whole, saved, positions, slopes, score_scale):
    (
        first_gain,
        first_shift,
        qkv_weight,
        qv_bias,
        out_weight,
        out_bias,
        second_gain,
        second_shift,
        up_weight,
        up_bias,
        down_weight,
        down_bias,
    ) = whole
    (
        normed,
        queries,
        key_rows,
        value_rows,
        mixed_heads,
        log_totals,
        mixed_rows,
        middle,
        normed_two,
        hidden_pre,
        activation,
    ) = saved
    seq_shards = lax.axis_size("seq")
    row_count, model_width = token_rows.shape
    head_size = model_width // H
    local_heads = H // seq_shards
    seq_len = row_count * seq_shards
    valid_mask = (positions < length).astype(jnp.float32)[:, None]
    grad_out = valid_mask * grad_rows.astype(jnp.float32)
    grad_out_low = grad_out.astype(jnp.bfloat16)
    down_grad = contract_rows(activation, grad_out_low)
    down_bias_grad = jnp.sum(grad_out, axis=0)
    grad_act = against(grad_out_low, down_weight)
    gelu_pull = jax.vjp(partial(jax.nn.gelu, approximate=True), hidden_pre)[1]
    grad_pre = gelu_pull(grad_act)[0].astype(jnp.bfloat16)
    up_grad = contract_rows(normed_two, grad_pre)
    up_bias_grad = jnp.sum(grad_pre.astype(jnp.float32), axis=0)
    grad_normed_two = against(grad_pre, up_weight)
    norm_pull = jax.vjp(
        layer_norm, middle, second_gain.astype(jnp.float32), second_shift.astype(jnp.float32)
    )[1]
    middle_part, second_gain_grad, second_shift_grad = norm_pull(grad_normed_two)
    grad_middle = grad_out + middle_part
    grad_branch = grad_middle.astype(jnp.bfloat16)
    out_bias_grad = jnp.sum(grad_branch.astype(jnp.float32), axis=0)
    out_grad = contract_rows(mixed_rows, grad_branch)
    grad_mixed_rows = against(grad_branch, out_weight).astype(jnp.bfloat16)
    grad_mixed = lax.all_to_all(
        grad_mixed_rows.reshape(row_count, seq_shards, local_heads * head_size),
        "seq",
        split_axis=1,
        concat_axis=0,
        tiled=True,
    )
    grad_mixed = jnp.moveaxis(grad_mixed.reshape(seq_len, local_heads, head_size), 0, 1)
    query_grad, key_grad, value_grad = attend_back(
        queries, key_rows, value_rows, grad_mixed, log_totals, length, slopes, score_scale
    )
    stacked = jnp.moveaxis(jnp.stack([query_grad, key_grad, value_grad], axis=2), 0, 1)
    grad_qkv = lax.all_to_all(
        stacked.reshape(seq_shards, row_count, 1, local_heads * 3 * head_size),
        "seq",
        split_axis=0,
        concat_axis=2,
        tiled=True,
    ).reshape(row_count, 3 * model_width)
    qkv_grad = contract_rows(normed, grad_qkv)
    column_sums = jnp.sum(grad_qkv.astype(jnp.float32), axis=0).reshape(H, 3, head_size)
    qv_bias_grad = jnp.stack(
        [column_sums[:, 0].reshape(model_width), column_sums[:, 2].reshape(model_width)]
    )
    grad_normed = against(grad_qkv, qkv_weight)
    first_pull = jax.vjp(
        layer_norm,
        token_rows.astype(jnp.float32),
        first_gain.astype(jnp.float32),
        first_shift.astype(jnp.float32),
    )[1]
    token_part, first_gain_grad, first_shift_grad = first_pull(grad_normed)
    row_grad = (grad_middle + token_part).astype(jnp.bfloat16)
    grads = (
        first_gain_grad,
        first_shift_grad,
        qkv_grad,
        qv_bias_grad,
        out_grad,
        out_bias_grad,
        second_gain_grad,
        second_shift_grad,
        up_grad,
        up_bias_grad,
        down_grad,
        down_bias_grad,
    )
    return (row_grad, grads)


def local(
    tokens,
    cotangent,
    lengths,
    first_gain,
    first_shift,
    qkv_weight,
    qv_bias,
    out_weight,
    out_bias,
    second_gain,
    second_shift,
    up_weight,
    up_bias,
    down_weight,
    down_bias,
):
    seq_shards = lax.axis_size("seq")
    micro_count, row_count, model_width = tokens.shape
    local_heads = H // seq_shards
    head_first = lax.axis_index("seq") * local_heads
    slopes = jnp.exp2(-((head_first + jnp.arange(local_heads)).astype(jnp.float32) + 1.0) * 8.0 / H)
    score_scale = (model_width // H) ** (-0.5)
    positions = lax.axis_index("seq") * row_count + jnp.arange(row_count)
    block_list = []
    saved_list = []
    for batch_index in range(micro_count):
        whole = (
            lax.all_gather(first_gain, "fsdp", axis=0, tiled=True),
            lax.all_gather(first_shift, "fsdp", axis=0, tiled=True),
            lax.all_gather(qkv_weight, "fsdp", axis=0, tiled=True),
            lax.all_gather(qv_bias, "fsdp", axis=1, tiled=True),
            lax.all_gather(out_weight, "fsdp", axis=0, tiled=True),
            lax.all_gather(out_bias, "fsdp", axis=0, tiled=True),
            lax.all_gather(second_gain, "fsdp", axis=0, tiled=True),
            lax.all_gather(second_shift, "fsdp", axis=0, tiled=True),
            lax.all_gather(up_weight, "fsdp", axis=0, tiled=True),
            lax.all_gather(up_bias, "fsdp", axis=0, tiled=True),
            lax.all_gather(down_weight, "fsdp", axis=0, tiled=True),
            lax.all_gather(down_bias, "fsdp", axis=0, tiled=True),
        )
        block_rows, saved = forward_pass(
            tokens[batch_index], lengths[batch_index], whole, positions, slopes, score_scale
        )
        block_list.append(block_rows)
        saved_list.append(saved)
    grad_list = [None] * micro_count
    summed = None
    for batch_index in reversed(range(micro_count)):
        whole = (
            lax.all_gather(first_gain, "fsdp", axis=0, tiled=True),
            lax.all_gather(first_shift, "fsdp", axis=0, tiled=True),
            lax.all_gather(qkv_weight, "fsdp", axis=0, tiled=True),
            lax.all_gather(qv_bias, "fsdp", axis=1, tiled=True),
            lax.all_gather(out_weight, "fsdp", axis=0, tiled=True),
            lax.all_gather(out_bias, "fsdp", axis=0, tiled=True),
            lax.all_gather(second_gain, "fsdp", axis=0, tiled=True),
            lax.all_gather(second_shift, "fsdp", axis=0, tiled=True),
            lax.all_gather(up_weight, "fsdp", axis=0, tiled=True),
            lax.all_gather(up_bias, "fsdp", axis=0, tiled=True),
            lax.all_gather(down_weight, "fsdp", axis=0, tiled=True),
            lax.all_gather(down_bias, "fsdp", axis=0, tiled=True),
        )
        row_grad, grads = backward_pass(
            tokens[batch_index],
            cotangent[batch_index],
            lengths[batch_index],
            whole,
            saved_list[batch_index],
            positions,
            slopes,
            score_scale,
        )
        grad_list[batch_index] = row_grad
        if summed is None:
            summed = tuple(grads)
        else:
            summed = tuple((earlier + later for earlier, later in zip(summed, grads)))
    summed = (
        lax.psum_scatter(summed[0], ("fsdp", "seq"), scatter_dimension=0, tiled=True),
        lax.psum_scatter(summed[1], ("fsdp", "seq"), scatter_dimension=0, tiled=True),
        lax.psum_scatter(summed[2], ("fsdp", "seq"), scatter_dimension=0, tiled=True),
        lax.psum_scatter(summed[3], ("fsdp", "seq"), scatter_dimension=1, tiled=True),
        lax.psum_scatter(summed[4], ("fsdp", "seq"), scatter_dimension=0, tiled=True),
        lax.psum_scatter(summed[5], ("fsdp", "seq"), scatter_dimension=0, tiled=True),
        lax.psum_scatter(summed[6], ("fsdp", "seq"), scatter_dimension=0, tiled=True),
        lax.psum_scatter(summed[7], ("fsdp", "seq"), scatter_dimension=0, tiled=True),
        lax.psum_scatter(summed[8], ("fsdp", "seq"), scatter_dimension=0, tiled=True),
        lax.psum_scatter(summed[9], ("fsdp", "seq"), scatter_dimension=0, tiled=True),
        lax.psum_scatter(summed[10], ("fsdp", "seq"), scatter_dimension=0, tiled=True),
        lax.psum_scatter(summed[11], ("fsdp", "seq"), scatter_dimension=0, tiled=True),
    )
    return (jnp.stack(block_list), jnp.stack(grad_list)) + tuple(summed)


def solution(mesh):
    return jax.shard_map(
        local,
        mesh=mesh,
        in_specs=(
            P("fsdp", "seq", None),
            P("fsdp", "seq", None),
            P("fsdp"),
            P("fsdp"),
            P("fsdp"),
            P("fsdp", None),
            P(None, "fsdp"),
            P("fsdp", None),
            P("fsdp"),
            P("fsdp"),
            P("fsdp"),
            P("fsdp", None),
            P("fsdp"),
            P("fsdp", None),
            P("fsdp"),
        ),
        out_specs=(
            P("fsdp", "seq", None),
            P("fsdp", "seq", None),
            P(("fsdp", "seq")),
            P(("fsdp", "seq")),
            P(("fsdp", "seq"), None),
            P(None, ("fsdp", "seq")),
            P(("fsdp", "seq"), None),
            P(("fsdp", "seq")),
            P(("fsdp", "seq")),
            P(("fsdp", "seq")),
            P(("fsdp", "seq"), None),
            P(("fsdp", "seq")),
            P(("fsdp", "seq"), None),
            P(("fsdp", "seq")),
        ),
        check_vma=False,
    )
```

profile of v0, /device:TPU:0, one launch (start us, length us, event | category | flops | bytes accessed | tf_op | source)
XLA Modules:
  0.0 1446.3 jit_solution(1450047404139784561)
XLA Ops:
  9.4 22.5 %all_gather.27 = bf16[2,1024]{1,0:T(2,128)(2,1)S(1)} all-gather(bf16[2,128]{1,0:T(2,128)(2,1)} %param.29), channel_id=1, replica_groups=mesh['fsdp'=8,'seq'=4] {'fsdp'}, dimensions={1}, use_global_device_ids=true | all-gather | bytes 4608 | tf_op jit(solution)/shard_map/all_gather | solution.py:335
  32.3 16.7 %all-gather.1 = bf16[8,1,128]{2,1,0:T(2,128)(2,1)S(1)} all-gather(bf16[1,1,128]{2,1,0:T(2,128)(2,1)} %bitcast.420), channel_id=1, replica_groups=mesh['fsdp'=8,'seq'=4] {'fsdp'}, dimensions={0}, use_global_device_ids=true | all-gather | bytes 2304 | tf_op jit(solution)/shard_map/all_gather | solution.py:333
  49.0 18.6 %all-gather = bf16[8,1,128]{2,1,0:T(2,128)(2,1)S(1)} all-gather(bf16[1,1,128]{2,1,0:T(2,128)(2,1)} %bitcast.421), channel_id=1, replica_groups=mesh['fsdp'=8,'seq'=4] {'fsdp'}, dimensions={0}, use_global_device_ids=true | all-gather | bytes 2304 | tf_op jit(solution)/shard_map/all_gather | solution.py:332
  70.7 41.4 %all-gather.12.cloned.1.call-done = bf16[1024,3072]{1,0:T(8,128)(2,1)} async-done(((bf16[128,3072]{1,0:T(8,128)(2,1)}), bf16[1024,3072]{1,0:T(8,128)(2,1)}) %all-gather.12.cloned.1.call-update) | async-done | bytes 6291472 | tf_op jit(solution)/shard_map/all_gather | solution.py:334
  123.2 5.9 fusion.82
  131.6 10.3 all-to-all-done.2
  154.1 30.5 %while.57 = (s32[]{:T(128)}, bf16[2,4,512,64]{2,3,1,0:T(8,128)(2,1)}, f32[2,4,512]{2,1,0:T(4,128)S(1)}, s32[2]{0:T(128)S(1)}, s32[]{:T(128)}, /*index=5*/bf16[4,...) while((s32[]{:T(128)}, ...), condition=%wide.region_13.14_spmd.clone, body=%wide.region_10.13_spmd.clone.sunk | while | flops 574750208 | bytes 43590964 | solution.py:63
  200.2 30.5 %while.56 = (s32[]{:T(128)}, bf16[2,4,512,64]{2,3,1,0:T(8,128)(2,1)}, f32[2,4,512]{2,1,0:T(4,128)S(1)}, s32[2]{0:T(128)S(1)}, s32[]{:T(128)}, /*index=5*/bf16[4,...) while((s32[]{:T(128)}, ...), condition=%wide.region_5.6_spmd.clone, body=%wide.region_2.5_spmd.clone.sunk | while | flops 574750208 | bytes 43590964 | solution.py:63
  236.8 18.0 %all-gather.2 = bf16[8,1,128]{2,1,0:T(2,128)(2,1)S(1)} all-gather(bf16[1,1,128]{2,1,0:T(2,128)(2,1)S(1)} %bitcast.422), channel_id=1, replica_groups=mesh['fsdp'=8,'seq'=4] {'fsdp'}, dimensions={0}, use_global_device_ids=true | all-gather | bytes 2304 | tf_op jit(solution)/shard_map/all_gather | solution.py:337
  254.8 26.4 %all-gather.5 = bf16[8,1,512]{2,1,0:T(2,128)(2,1)S(1)} all-gather(bf16[1,1,512]{2,1,0:T(2,128)(2,1)S(1)} %reshape.650), channel_id=1, replica_groups=mesh['fsdp'=8,'seq'=4] {'fsdp'}, dimensions={0}, use_global_device_ids=true | all-gather | bytes 9216 | tf_op jit(solution)/shard_map/all_gather | solution.py:341
  281.2 16.2 %all-gather.4 = bf16[8,1,128]{2,1,0:T(2,128)(2,1)S(1)} all-gather(bf16[1,1,128]{2,1,0:T(2,128)(2,1)S(1)} %bitcast.423), channel_id=1, replica_groups=mesh['fsdp'=8,'seq'=4] {'fsdp'}, dimensions={0}, use_global_device_ids=true | all-gather | bytes 2304 | tf_op jit(solution)/shard_map/all_gather | solution.py:339
  297.4 18.7 %all-gather.3 = bf16[8,1,128]{2,1,0:T(2,128)(2,1)S(1)} all-gather(bf16[1,1,128]{2,1,0:T(2,128)(2,1)S(1)} %bitcast.424), channel_id=1, replica_groups=mesh['fsdp'=8,'seq'=4] {'fsdp'}, dimensions={0}, use_global_device_ids=true | all-gather | bytes 2304 | tf_op jit(solution)/shard_map/all_gather | solution.py:338
  324.3 8.0 convolution_add_fusion.3
  336.8 75.9 %all-gather.18.cloned.1.call-done = bf16[4096,1024]{1,0:T(8,128)(2,1)} async-done(((bf16[512,1024]{1,0:T(8,128)(2,1)}), bf16[4096,1024]{1,0:T(8,128)(2,1)}) %all-gather.18.cloned.1.call-update) | async-done | bytes 8388624 | tf_op jit(solution)/shard_map/all_gather | solution.py:342
  412.7 12.2 convert_reduce_fusion.1
  438.7 7.6 multiply_reduce_fusion.2
  455.7 7.2 all-to-all-done.6
  481.3 50.7 %while.58 = (s32[]{:T(128)}, f32[4,1024,64]{1,2,0:T(8,128)S(1)}, f32[4,1024,64]{1,2,0:T(8,128)}, bf16[2,4,512,64]{2,3,1,0:T(8,128)(2,1)}, s32[2]{0:T(128)S(1)}, ...) while((s32[]{:T(128)}, f32[4,1024,64]{1,2,0:T(8,128)S(1)}, ...), condition=%wide.region_20.21_spmd.clone, body=%wide.region_18.20_spmd.clone.sunk | while | flops 1368915456 | bytes 178046000 | solution.py:107
  551.8 49.6 %while.59 = (s32[]{:T(128)}, f32[4,1024,64]{1,2,0:T(8,128)S(1)}, f32[4,1024,64]{1,2,0:T(8,128)S(1)}, bf16[2,4,512,64]{2,3,1,0:T(8,128)(2,1)}, s32[2]{0:T(128)S(1...) while((s32[]{:T(128)}, f32[4,1024,64]{1,2,0:T(8,128)S(1)}, ...), condition=%wide.region_27.28_spmd.clone, body=%wide.region_25.27_spmd.clone.sunk | while | flops 1368915456 | bytes 167560144 | solution.py:107
  618.7 14.9 %all-to-all-done.7 = bf16[4,256,1,768]{1,3,2,0:T(8,128)(2,1)} async-done(((bf16[4,256,1,768]{1,3,2,0:T(8,128)(2,1)}), bf16[4,256,1,768]{1,3,2,0:T(8,128)(2,1)}, u32[]{:S(2)}, u32[]{:S(2)}) %all-to-all-start.7) | async-done | bytes 1572896 | tf_op jit(solution)/shard_map/all_to_all | solution.py:266
  650.6 6.6 convolution_add_fusion.2
  662.3 10.0 convolution_add_fusion.1
  672.9 11.1 fusion.164
  684.1 11.0 convolution_add_fusion
  695.8 17.7 %all-gather.6 = bf16[8,1,128]{2,1,0:T(2,128)(2,1)S(1)} all-gather(bf16[1,1,128]{2,1,0:T(2,128)(2,1)S(1)} %bitcast.425), channel_id=1, replica_groups=mesh['fsdp'=8,'seq'=4] {'fsdp'}, dimensions={0}, use_global_device_ids=true | all-gather | bytes 2304 | tf_op jit(solution)/shard_map/all_gather | solution.py:343
  713.6 7.7 fusion.102
  721.3 6.4 fusion.103
  734.8 37.6 %all-reduce.7 = (f32[1024]{0:T(1024)S(1)}, f32[1024]{0:T(1024)S(1)}, f32[1024]{0:T(1024)S(1)}, f32[1024]{0:T(1024)S(1)}, f32[1024]{0:T(1024)S(1)}, /*index=5*/f32[4096]{0:T(1024)S(1)}, f32[1024]{0:T(1024)S(1)}) all-reduce(f32[1024]{0:T(1024)S(1)} %add.430, ...), channel_id=2, replica_groups=mesh['fsdp'=8,'seq'=4] {'fsdp','seq'}, use_global_device_ids=true, to_apply=%region_32.33.clone | all-reduce | flops 10240 | bytes 81920
  781.0 127.3 %reduce-scatter.10.cloned.1.call-done = f32[32,1024]{1,0:T(8,128)} async-done(((f32[1024,1024]{1,0:T(8,128)}), f32[32,1024]{1,0:T(8,128)}) %reduce-scatter.10.cloned.1.call-update) | async-done | bytes 131088 | tf_op jit(solution)/shard_map/reduce_scatter | solution.py:387
  908.3 159.0 %reduce-scatter.8.cloned.1.call-done = f32[32,3072]{1,0:T(8,128)} async-done(((f32[1024,3072]{1,0:T(8,128)}), f32[32,3072]{1,0:T(8,128)}) %reduce-scatter.8.cloned.1.call-update) | async-done | bytes 393232 | tf_op jit(solution)/shard_map/reduce_scatter | solution.py:385
  1067.3 184.7 %reduce-scatter.12.cloned.1.call-done = f32[32,4096]{1,0:T(8,128)} async-done(((f32[1024,4096]{1,0:T(8,128)}), f32[32,4096]{1,0:T(8,128)}) %reduce-scatter.12.cloned.1.call-update) | async-done | bytes 524304 | tf_op jit(solution)/shard_map/reduce_scatter | solution.py:391
  1252.0 187.5 %reduce-scatter.14.cloned.1.call-done = f32[128,1024]{1,0:T(8,128)} async-done(((f32[4096,1024]{1,0:T(8,128)}), f32[128,1024]{1,0:T(8,128)}) %reduce-scatter.14.cloned.1.call-update) | async-done | bytes 524304 | tf_op jit(solution)/shard_map/reduce_scatter | solution.py:393
  (542 shorter events, 327.4 us)
Async XLA Ops:
  7.2 104.9 %copy-start.6 = (bf16[2,256,1024]{2,1,0:T(8,128)(2,1)S(1)}, bf16[2,256,1024]{2,1,0:T(8,128)(2,1)}, u32[]{:S(2)}) copy-start(bf16[2,256,1024]{2,1,0:T(8,128)(2,1)} %param.23) | copy-start | bytes 3145732
  7.2 104.9 %all-gather.12.cloned.1.call-start = ((), (), s32[]{:S(2)}) async-start(), calls=%async_computation.13 | async-start | bytes 7077888 | tf_op jit(solution)/shard_map/all_gather | solution.py:334
  7.9 312.2 %all-gather.14.cloned.1.call-start = ((), (), s32[]{:S(2)}) async-start(), calls=%async_computation.14 | async-start | bytes 2359296 | tf_op jit(solution)/shard_map/all_gather | solution.py:336
  8.7 315.6 %all-gather.16.cloned.1.call-start = ((), (), s32[]{:S(2)}) async-start(), calls=%async_computation.15 | async-start | bytes 9437184 | tf_op jit(solution)/shard_map/all_gather | solution.py:340
  49.0 74.1 %copy-start.65 = (f32[8,1,128]{2,1,0:T(1,128)}, f32[8,1,128]{2,1,0:T(1,128)S(1)}, u32[]{:S(2)}) copy-start(f32[8,1,128]{2,1,0:T(1,128)S(1)} %convert_element_type.299) | copy-start | bytes 12292
  118.3 23.6 %all-to-all-start.2 = ((bf16[256,4,768]{0,2,1:T(8,128)(2,1)}), bf16[256,4,768]{0,2,1:T(8,128)(2,1)S(1)}, u32[]{:S(2)}, u32[]{:S(2)}) async-start(bf16[256,4,768]{0,2,1:T(8,128)(2,1)} %bitcast.365), calls=%async_computation.2 | async-start | bytes 3145728 | tf_op jit(solution)/shard_map/all_to_all | solution.py:149
  121.9 290.8 %all-gather.18.cloned.1.call-start = ((), (), s32[]{:S(2)}) async-start(), calls=%async_computation.16 | async-start | bytes 9437184 | tf_op jit(solution)/shard_map/all_gather | solution.py:342
  142.0 45.2 %all-to-all-start = ((bf16[256,4,768]{0,2,1:T(8,128)(2,1)}), bf16[256,4,768]{0,2,1:T(8,128)(2,1)}, u32[]{:S(2)}, u32[]{:S(2)}) async-start(bf16[256,4,768]{0,2,1:T(8,128)(2,1)} %bitcast.8), calls=%async_computation | async-start | bytes 3145728 | tf_op jit(solution)/shard_map/all_to_all | solution.py:149
  187.2 46.1 %all-to-all-start.3 = ((bf16[4,256,1,256]{1,3,2,0:T(8,128)(2,1)}), bf16[4,256,1,256]{1,3,2,0:T(8,128)(2,1)}, u32[]{:S(2)}, u32[]{:S(2)}) async-start(bf16[4,256,1,256]{1,3,2,0:T(8,128)(2,1)} %copy.90), calls=%async_computation.3 | async-start | bytes 1048576 | tf_op jit(solution)/shard_map/all_to_all | solution.py:159
  230.6 89.5 %copy-start.15 = (bf16[4,1024,64]{1,2,0:T(8,128)(2,1)}, bf16[4,1024,64]{1,2,0:T(8,128)(2,1)S(1)}, u32[]{:S(2)}) copy-start(bf16[4,1024,64]{1,2,0:T(8,128)(2,1)S(1)} %get-tuple-element.1001) | copy-start | bytes 1572868
  230.7 66.7 %copy-start.109 = (bf16[128]{0:T(256)(128)(2,1)S(1)}, bf16[128]{0:T(256)(128)(2,1)}, u32[]{:S(2)}) copy-start(bf16[128]{0:T(256)(128)(2,1)} %param.32) | copy-start | bytes 772
  230.7 89.5 %copy-start.7 = (bf16[2,256,1024]{2,1,0:T(8,128)(2,1)S(1)}, bf16[2,256,1024]{2,1,0:T(8,128)(2,1)}, u32[]{:S(2)}) copy-start(bf16[2,256,1024]{2,1,0:T(8,128)(2,1)} %param.23) | copy-start | bytes 3145732
  233.3 85.7 %all-to-all-start.1 = ((bf16[4,256,1,256]{1,3,2,0:T(8,128)(2,1)}), bf16[4,256,1,256]{1,3,2,0:T(8,128)(2,1)S(1)}, u32[]{:S(2)}, u32[]{:S(2)}) async-start(bf16[4,256,1,256]{1,3,2,0:T(8,128)(2,1)} %copy.84), calls=%async_computation.1 | async-start | bytes 1048576 | tf_op jit(solution)/shard_map/all_to_all | solution.py:159
  316.1 130.1 %copy-start.61 = (f32[8,1,128]{2,1,0:T(1,128)}, f32[8,1,128]{2,1,0:T(1,128)S(1)}, u32[]{:S(2)}) copy-start(f32[8,1,128]{2,1,0:T(1,128)S(1)} %convert_element_type.301) | copy-start | bytes 12292
  316.8 130.3 %copy-start.85 = (f32[256]{0:T(256)}, f32[256]{0:T(256)S(1)}, u32[]{:S(2)}) copy-start(f32[256]{0:T(256)S(1)} %compare_convert_fusion) | copy-start | bytes 3076
  317.5 129.6 %copy-start.77 = (f32[256]{0:T(256)}, f32[256]{0:T(256)S(1)}, u32[]{:S(2)}) copy-start(f32[256]{0:T(256)S(1)} %compare_convert_fusion.1) | copy-start | bytes 3076
  322.7 123.5 %copy-start.24 = (f32[256,1024]{1,0:T(8,128)}, f32[256,1024]{1,0:T(8,128)S(1)}, u32[]{:S(2)}) copy-start(f32[256,1024]{1,0:T(8,128)S(1)} %get-tuple-element.530) | copy-start | bytes 3145732
  322.8 123.5 %copy-start.71 = (f32[256]{0:T(256)}, f32[256]{0:T(256)S(1)}, u32[]{:S(2)}) copy-start(f32[256]{0:T(256)S(1)} %broadcast_multiply_fusion) | copy-start | bytes 3076
  323.9 122.4 %copy-start.11 = (f32[256,1024]{1,0:T(8,128)}, f32[256,1024]{1,0:T(8,128)S(1)}, u32[]{:S(2)}) copy-start(f32[256,1024]{1,0:T(8,128)S(1)} %get-tuple-element.532) | copy-start | bytes 3145732
  323.9 122.4 %copy-start.79 = (f32[256]{0:T(256)}, f32[256]{0:T(256)S(1)}, u32[]{:S(2)}) copy-start(f32[256]{0:T(256)S(1)} %broadcast_multiply_fusion.2) | copy-start | bytes 3076
  324.2 122.1 %copy-start.81 = (f32[256]{0:T(256)}, f32[256]{0:T(256)S(1)}, u32[]{:S(2)}) copy-start(f32[256]{0:T(256)S(1)} %fusion.177) | copy-start | bytes 3076
  324.2 122.1 %copy-start.91 = (f32[256]{0:T(256)}, f32[256]{0:T(256)S(1)}, u32[]{:S(2)}) copy-start(f32[256]{0:T(256)S(1)} %fusion.175) | copy-start | bytes 3076
  332.3 80.4 %copy-start.29 = (bf16[2,256,1024]{2,1,0:T(8,128)(2,1)S(1)}, bf16[2,256,1024]{2,1,0:T(8,128)(2,1)}, u32[]{:S(2)}) copy-start(bf16[2,256,1024]{2,1,0:T(8,128)(2,1)} %param.24) | copy-start | bytes 3145732
  450.6 12.3 all-to-all-start.6
  462.9 13.2 all-to-all-start.4
  546.4 62.7 %all-to-all-start.5 = ((bf16[4,256,1,768]{1,3,2,0:T(8,128)(2,1)}), bf16[4,256,1,768]{1,3,2,0:T(8,128)(2,1)}, u32[]{:S(2)}, u32[]{:S(2)}) async-start(bf16[4,256,1,768]{1,3,2,0:T(8,128)(2,1)} %copy.97), calls=%async_computation.5 | async-start | bytes 3145728 | tf_op jit(solution)/shard_map/all_to_all | solution.py:266
  609.1 24.5 %all-to-all-start.7 = ((bf16[4,256,1,768]{1,3,2,0:T(8,128)(2,1)}), bf16[4,256,1,768]{1,3,2,0:T(8,128)(2,1)}, u32[]{:S(2)}, u32[]{:S(2)}) async-start(bf16[4,256,1,768]{1,3,2,0:T(8,128)(2,1)} %copy.104), calls=%async_computation.7 | async-start | bytes 3145728 | tf_op jit(solution)/shard_map/all_to_all | solution.py:266
  613.4 166.2 %reduce-scatter.16.cloned.1.call-start = ((), (), s32[]{:S(2)}) async-start(), calls=%async_computation.21 | async-start | bytes 540672
  637.1 271.1 %reduce-scatter.10.cloned.1.call-start = ((), (), s32[]{:S(2)}) async-start(), calls=%async_computation.18 | async-start | bytes 4325376 | tf_op jit(solution)/shard_map/reduce_scatter | solution.py:387
  642.5 424.8 %reduce-scatter.8.cloned.1.call-start = ((), (), s32[]{:S(2)}) async-start(), calls=%async_computation.17 | async-start | bytes 12976128 | tf_op jit(solution)/shard_map/reduce_scatter | solution.py:385
  657.2 594.8 %reduce-scatter.12.cloned.1.call-start = ((), (), s32[]{:S(2)}) async-start(), calls=%async_computation.19 | async-start | bytes 17301504 | tf_op jit(solution)/shard_map/reduce_scatter | solution.py:391
  672.3 767.2 %reduce-scatter.14.cloned.1.call-start = ((), (), s32[]{:S(2)}) async-start(), calls=%async_computation.20 | async-start | bytes 17301504 | tf_op jit(solution)/shard_map/reduce_scatter | solution.py:393
  (123 other events, 1046.7 us)
Sparse Core Ops, SparseCore 0:
  10.2 101.7 all-gather.11
  114.2 47.4 all-gather.13
  163.8 123.5 all-gather.15
  289.4 123.2 all-gather.17
  637.3 131.3 reduce-scatter.15
  771.5 136.7 reduce-scatter.9
  915.9 151.3 reduce-scatter.7
  1070.2 181.7 reduce-scatter.11
  1254.9 184.5 reduce-scatter.13
where the time goes:
time: 1450 us
  waiting for transfers between devices  815 us (56%)
  matrix products  211 us (15%)
  blocking collectives  192 us (13%)
  local copies, waits for them, and re-layouts  105 us (7%)
  other arithmetic  56.9 us (4%)
  starting transfers between devices  33.5 us (2%)
  loops' own time  16.4 us (1%)
  between operations  15.6 us (1%)
    reduce_scatter x1, waiting for transfers between devices, local(): lax.psum_scatter(summed[10], ('fsdp', 'seq'), scatter_dimension=0, tiled=...  188 us
    reduce_scatter x1, waiting for transfers between devices, local(): lax.psum_scatter(summed[8], ('fsdp', 'seq'), scatter_dimension=0, tiled=T...  185 us
    reduce_scatter x1, waiting for transfers between devices, local(): lax.psum_scatter(summed[2], ('fsdp', 'seq'), scatter_dimension=0, tiled=T...  159 us
    reduce_scatter x1, waiting for transfers between devices, local(): lax.psum_scatter(summed[4], ('fsdp', 'seq'), scatter_dimension=0, tiled=T...  127 us
    all_gather x1, waiting for transfers between devices, local(): lax.all_gather(down_weight, 'fsdp', axis=0, tiled=True)  75.9 us
    dot_general x8, matrix products, contract_rows(): lax.dot_general(left_side, right_side, (((0,), (0,)), ((), ())), preferre...  54.7 us
    all_gather x1, waiting for transfers between devices, local(): lax.all_gather(qkv_weight, 'fsdp', axis=0, tiled=True)  41.4 us
    unnamed x1, blocking collectives  37.6 us
  transfers between devices with their start and end apart: 17, of which 10 were waited for; matrix products, arithmetic and copies ran while one was open for 17% of the time, Pallas kernels for 0%

commit v1 on v0

v1 whole, which is shorter than its diff:
```python
from functools import partial
import math

import jax
import jax.numpy as jnp
from jax import lax
from jax.experimental import pallas as pl
from jax.experimental.pallas import tpu as pltpu
from jax.sharding import PartitionSpec as P

H = 16


epsilon = 1e-05
f32 = jnp.float32
bf16 = jnp.bfloat16


def layer_norm(values, norm_gain, norm_shift):
    row_mean = jnp.mean(values, axis=-1, keepdims=True)
    centered = values - row_mean
    variance = jnp.mean(centered * centered, axis=-1, keepdims=True)
    return centered * lax.rsqrt(variance + epsilon) * norm_gain + norm_shift


def product(left_side, right_side):
    return jnp.dot(left_side, right_side, preferred_element_type=f32)


def contract_rows(left_side, right_side):
    return lax.dot_general(
        left_side, right_side, (((0,), (0,)), ((), ())), preferred_element_type=f32
    )


def against(left_side, right_side):
    return lax.dot_general(
        left_side, right_side, (((1,), (1,)), ((), ())), preferred_element_type=f32
    )


def head_scores(query_block, key_rows, start_row, slopes, length, score_scale):
    block_size = query_block.shape[1]
    seq_len = key_rows.shape[1]
    row_index = start_row + jnp.arange(block_size)
    columns = jnp.arange(seq_len)
    products = jnp.einsum("hqd,hkd->hqk", query_block, key_rows, preferred_element_type=f32)
    distance = (columns[None, :] - row_index[:, None]).astype(f32)
    allowed = (columns[None, :] <= row_index[:, None]) & (columns[None, :] < length)
    return jnp.where(
        allowed[None], products * score_scale + slopes[:, None, None] * distance, -jnp.inf
    )


def attend(queries, key_rows, value_rows, length, slopes, score_scale):
    head_count, seq_len, head_size = queries.shape
    block_size = math.gcd(512, seq_len)

    def one_block(start_row):
        query_block = lax.dynamic_slice_in_dim(queries, start_row, block_size, 1)
        scores = head_scores(query_block, key_rows, start_row, slopes, length, score_scale)
        largest = jnp.max(scores, axis=-1, keepdims=True)
        log_total = largest + jnp.log(jnp.sum(jnp.exp(scores - largest), axis=-1, keepdims=True))
        attention_probs = jnp.exp(scores - log_total).astype(bf16)
        mixed_rows = jnp.einsum(
            "hqk,hkd->hqd", attention_probs, value_rows, preferred_element_type=f32
        )
        return (mixed_rows.astype(bf16), log_total[..., 0])

    starts = jnp.arange(seq_len // block_size, dtype=jnp.int32) * block_size
    mixed_rows, log_totals = lax.map(one_block, starts)
    return (
        jnp.moveaxis(mixed_rows, 0, 1).reshape(head_count, seq_len, head_size),
        jnp.moveaxis(log_totals, 0, 1).reshape(head_count, seq_len),
    )


def attend_back(queries, key_rows, value_rows, grad_mixed, log_totals, length, slopes, score_scale):
    head_count, seq_len, head_size = queries.shape
    block_size = math.gcd(512, seq_len)

    def one_block(carried, start_row):
        key_sum, value_sum = carried
        query_block = lax.dynamic_slice_in_dim(queries, start_row, block_size, 1)
        grad_block = lax.dynamic_slice_in_dim(grad_mixed, start_row, block_size, 1)
        total_block = lax.dynamic_slice_in_dim(log_totals, start_row, block_size, 1)
        scores = head_scores(query_block, key_rows, start_row, slopes, length, score_scale)
        attention_probs = jnp.exp(scores - total_block[..., None])
        grad_probs = jnp.einsum(
            "hqd,hkd->hqk", grad_block, value_rows, preferred_element_type=f32
        )
        row_inner = jnp.sum(attention_probs * grad_probs, axis=-1, keepdims=True)
        grad_scores = (attention_probs * (grad_probs - row_inner)).astype(bf16)
        query_grad = (
            jnp.einsum("hqk,hkd->hqd", grad_scores, key_rows, preferred_element_type=f32)
            * score_scale
        ).astype(bf16)
        key_sum = (
            key_sum
            + jnp.einsum("hqk,hqd->hkd", grad_scores, query_block, preferred_element_type=f32)
            * score_scale
        )
        value_sum = value_sum + jnp.einsum(
            "hqk,hqd->hkd",
            attention_probs.astype(bf16),
            grad_block,
            preferred_element_type=f32,
        )
        return ((key_sum, value_sum), query_grad)

    starts = jnp.arange(seq_len // block_size, dtype=jnp.int32) * block_size
    empty = jnp.zeros(queries.shape, f32)
    (key_sum, value_sum), query_grads = lax.scan(one_block, (empty, empty), starts)
    query_grad = jnp.moveaxis(query_grads, 0, 1).reshape(head_count, seq_len, head_size)
    return (query_grad, key_sum.astype(bf16), value_sum.astype(bf16))


ACROSS = ((1,), (1,))
PLAIN = ((1,), (0,))
DOWN = ((0,), (0,))

def mm(left_side, right_side, dims):
    return lax.dot_general(left_side, right_side, (dims, ((), ())), preferred_element_type=f32)


def set_bias(length, head, su):
    rows = su.shape[1]
    u = lax.broadcasted_iota(jnp.int32, (rows, 128), 0)
    for h in range(2):
        power = jnp.full((rows, 128), head + (h + 1), jnp.int32).astype(f32)
        slope = jnp.exp2(power * (-8.0 / H))
        su[h] = jnp.where(u < length, u.astype(f32) * slope, -jnp.inf)


def half(value, h):
    lane = lax.broadcasted_iota(jnp.int32, value.shape, 1)
    return jnp.where((lane // 64) == h, value, jnp.zeros_like(value))


def scores(k_ref, q, h, su, nk, block):
    st = mm(k_ref[:nk], half(q, h) * jnp.asarray(0.125, bf16), ACROSS)
    st = st + jnp.concatenate([su[h, :nk]] * (block // 128), axis=1)
    keep = lax.broadcasted_iota(jnp.int32, (block, block), 0) <= lax.broadcasted_iota(
        jnp.int32, (block, block), 1
    )
    tail = jnp.where(keep, st[nk - block :], -jnp.inf)
    return tail if nk == block else jnp.concatenate([st[: nk - block], tail], axis=0)


def exchange(value, axis, bit):
    return lax.ppermute(value, axis, [(i, i ^ bit) for i in range(lax.axis_size(axis))])


def is_set(axis, bit):
    return (lax.axis_index(axis) // bit) % 2


def place(bit):
    return (0 if bit[0] == "fsdp" else 1, -bit[1])


def powers(size):
    return [1 << i for i in range(size.bit_length() - 1)]


def gather_bits(unit, order):
    held, buffer = [], unit
    for bit in order:
        received = exchange(buffer, *bit)
        second = is_set(*bit) == 1
        at = sum(1 for other in held if place(other) < place(bit))
        buffer = jnp.stack(
            [jnp.where(second, received, buffer), jnp.where(second, buffer, received)], axis=at
        )
        held.append(bit)
    return buffer


def scatter_bits(partial_sum, held, order):
    held, buffer = list(held), partial_sum
    for bit in order:
        at, mine = held.index(bit), is_set(*bit)
        sent = lax.dynamic_index_in_dim(buffer, 1 - mine, at, keepdims=False).astype(bf16)
        kept = lax.dynamic_index_in_dim(buffer, mine, at, keepdims=False).astype(f32)
        buffer = kept + exchange(sent, *bit).astype(f32)
        held.remove(bit)
    return buffer


def in_order(pieces, own):
    pieces = list(pieces)
    for bit in powers(len(pieces)):
        second = (own // bit) % 2 == 1
        pieces = [
            jnp.where(second, pieces[i ^ bit], pieces[i]) for i in range(len(pieces))
        ]
    return pieces


class Team:
    def __init__(self, micro_count):
        self.shards = lax.axis_size("seq")
        self.size = self.shards // micro_count
        self.micro_count = micro_count
        self.member = lax.axis_index("seq") % self.size
        self.which = lax.axis_index("seq") // self.size
        self.team_bits = [("seq", bit) for bit in powers(self.size)]
        self.pair_bits = [("seq", self.size * bit) for bit in powers(micro_count)]

    def to_sequences(self, pieces):
        arrived = []
        for offset in range(self.micro_count):
            sent = lax.dynamic_index_in_dim(pieces, self.which ^ offset, 0, keepdims=False)
            arrived.append(sent if offset == 0 else exchange(sent, "seq", offset * self.size))
        return jnp.stack(in_order(arrived, self.which))

    def share(self, own):
        arrived = [own if e == 0 else exchange(own, "seq", e) for e in range(self.size)]
        return jnp.stack(in_order(arrived, self.member), axis=1)

    def swap(self, pieces, axis, onto):
        arrived = []
        for e in range(self.size):
            sent = lax.dynamic_index_in_dim(pieces, self.member ^ e, axis, keepdims=False)
            arrived.append(sent if e == 0 else exchange(sent, "seq", e))
        return jnp.stack(in_order(arrived, self.member), axis=onto)

    def reduce(self, partial_sum):
        total = lax.dynamic_index_in_dim(partial_sum, self.member, 1, keepdims=False)
        for e in range(1, self.size):
            sent = lax.dynamic_index_in_dim(partial_sum, self.member ^ e, 1, keepdims=False)
            total = total + exchange(sent.astype(bf16), "seq", e).astype(f32)
        return total


def general_program(
    tokens,
    cotangent,
    lengths,
    first_gain,
    first_shift,
    qkv_weight,
    qv_bias,
    out_weight,
    out_bias,
    second_gain,
    second_shift,
    up_weight,
    up_bias,
    down_weight,
    down_bias,
):
    micro_count, block_rows, width = tokens.shape
    team = Team(micro_count)
    size, member, which = team.size, team.member, team.which
    shards = team.shards
    fsdp_shards = lax.axis_size("fsdp")
    seq_len = block_rows * shards
    head_size = width // H
    own_heads = H // size
    own_width = own_heads * head_size
    hidden = up_weight.shape[1]
    own_hidden = hidden // size
    fsdp_bits = [("fsdp", bit) for bit in powers(fsdp_shards)]
    line_bits = fsdp_bits[1:] + fsdp_bits[:1]
    pair_bits, team_bits = team.pair_bits, team.team_bits
    rows_first = lambda bits: sorted(bits, key=place)
    split = lambda bits: (2,) * len(bits)

    packed = jnp.concatenate(
        [
            first_gain,
            first_shift,
            second_gain,
            second_shift,
            out_bias,
            down_bias,
            qv_bias[0],
            qv_bias[1],
            up_bias,
        ]
    )
    packed = gather_bits(packed, line_bits).reshape(fsdp_shards, -1).astype(f32)
    part = width // fsdp_shards
    vectors = [packed[:, i * part : (i + 1) * part].reshape(width) for i in range(8)]
    gain_one, shift_one, gain_two, shift_two, bias_out, bias_down, bias_q, bias_v = vectors
    bias_up = packed[:, 8 * part :].reshape(hidden // (size * (hidden // (fsdp_shards * shards))), size, -1)
    bias_up = lax.dynamic_index_in_dim(bias_up, member, 1, keepdims=False).reshape(own_hidden)

    def part_rows(weight, bits, parts_of):
        rows = weight.shape[0] // parts_of
        index = jnp.int32(0)
        for bit in rows_first(bits):
            index = index * 2 + is_set(*bit)
        return lax.dynamic_slice_in_dim(weight, index * rows, rows, 0)

    qkv_own = lax.dynamic_slice_in_dim(qkv_weight, member * 3 * own_width, 3 * own_width, 1)
    qkv_own = jnp.swapaxes(qkv_own.reshape(-1, own_heads, 3, head_size), 1, 2).reshape(-1, 3 * own_width)
    whole_qkv = gather_bits(
        part_rows(qkv_own, pair_bits, micro_count), line_bits + pair_bits
    ).reshape(width, 3 * own_width)
    whole_out = gather_bits(
        part_rows(out_weight, pair_bits + team_bits, shards), line_bits + pair_bits + team_bits
    ).reshape(width, width)
    unit = hidden // (fsdp_shards * shards)
    up_own = lax.dynamic_index_in_dim(
        up_weight.reshape(width // fsdp_shards, hidden // (size * unit), size, unit),
        member,
        2,
        keepdims=False,
    ).reshape(width // fsdp_shards, own_hidden)
    whole_up = gather_bits(up_own, line_bits).reshape(width, own_hidden)
    down_own = lax.dynamic_index_in_dim(
        down_weight.reshape(micro_count, size, unit, width), member, 1, keepdims=False
    ).reshape(micro_count * unit, width)
    whole_down = gather_bits(
        part_rows(down_own, pair_bits, micro_count), line_bits + pair_bits
    ).reshape(own_hidden, width)

    length = lax.dynamic_index_in_dim(lengths, which, 0, keepdims=False)
    own_tokens = team.to_sequences(tokens)
    all_tokens = team.share(own_tokens).reshape(seq_len, width).astype(f32)
    own_rows = micro_count * block_rows
    own_tokens = own_tokens.reshape(own_rows, width).astype(f32)
    own_positions = (
        (jnp.arange(micro_count)[:, None] * size + member) * block_rows
        + jnp.arange(block_rows)[None, :]
    ).reshape(own_rows)
    valid_mask = (own_positions < length).astype(f32)[:, None]
    slopes = jnp.exp2(-((member * own_heads + jnp.arange(own_heads)).astype(f32) + 1.0) * 8.0 / H)
    score_scale = head_size ** (-0.5)

    by_member = (micro_count, size, block_rows)

    normed = layer_norm(all_tokens, gain_one, shift_one).astype(bf16)
    own_bias = lambda vector: lax.dynamic_slice_in_dim(vector, member * own_width, own_width, 0)
    bias_columns = jnp.concatenate([own_bias(bias_q), jnp.zeros((own_width,), f32), own_bias(bias_v)])
    projected = (product(normed, whole_qkv) + bias_columns).astype(bf16)
    split_heads = lambda value: jnp.moveaxis(value.reshape(seq_len, -1, head_size), 1, 0)
    join_heads = lambda value: jnp.moveaxis(value, 0, 1).reshape(seq_len, -1)
    queries, key_rows, value_rows = [
        split_heads(projected[:, i * own_width : (i + 1) * own_width]) for i in range(3)
    ]
    mixed, log_totals = attend(queries, key_rows, value_rows, length, slopes, score_scale)
    mixed = join_heads(mixed)
    mixed_rows = team.swap(mixed.reshape(by_member + (own_width,)), 1, 2).reshape(own_rows, width)
    middle = own_tokens + (product(mixed_rows, whole_out) + bias_out)
    normed_two_own = layer_norm(middle, gain_two, shift_two).astype(bf16)
    normed_two = team.share(normed_two_own.reshape(micro_count, block_rows, width)).reshape(
        seq_len, width
    )
    hidden_pre = product(normed_two, whole_up) + bias_up
    activation = jax.nn.gelu(hidden_pre, approximate=True).astype(bf16)
    fed = team.reduce(product(activation, whole_down).reshape(by_member + (width,)))
    block_own = (valid_mask * (middle + fed.reshape(own_rows, width) + bias_down)).astype(bf16)
    block_out = team.to_sequences(block_own.reshape(micro_count, block_rows, width))

    own_grad = team.to_sequences(cotangent)
    own_grad = jnp.where(
        (valid_mask > 0).reshape(micro_count, block_rows, 1), own_grad, jnp.zeros_like(own_grad)
    )
    grad_low = team.share(own_grad).reshape(seq_len, width)
    grad_out = own_grad.reshape(own_rows, width).astype(f32)
    down_bias_grad = jnp.sum(grad_out, axis=0)
    down_grad = contract_rows(activation, grad_low)
    grad_act = against(grad_low, whole_down)
    gelu_pull = jax.vjp(partial(jax.nn.gelu, approximate=True), hidden_pre)[1]
    grad_pre = gelu_pull(grad_act)[0].astype(bf16)
    up_grad = contract_rows(normed_two, grad_pre)
    up_bias_grad = jnp.sum(grad_pre.astype(f32), axis=0)
    grad_normed_two = team.reduce(
        against(grad_pre, whole_up).reshape(by_member + (width,))
    ).reshape(own_rows, width)
    norm_pull = jax.vjp(layer_norm, middle, gain_two, shift_two)[1]
    middle_part, second_gain_grad, second_shift_grad = norm_pull(grad_normed_two)
    grad_middle = grad_out + middle_part
    grad_branch = grad_middle.astype(bf16)
    out_bias_grad = jnp.sum(grad_branch.astype(f32), axis=0)
    out_grad = contract_rows(mixed_rows, grad_branch)
    grad_mixed_own = against(grad_branch, whole_out).astype(bf16)
    grad_mixed = team.swap(
        grad_mixed_own.reshape(micro_count, block_rows, size, own_width), 2, 1
    ).reshape(seq_len, own_width)
    backs = attend_back(
        queries,
        key_rows,
        value_rows,
        split_heads(grad_mixed),
        log_totals,
        length,
        slopes,
        score_scale,
    )
    grad_qkv = jnp.concatenate([join_heads(back) for back in backs], axis=1)
    qkv_grad = contract_rows(normed, grad_qkv)
    column_sums = jnp.sum(grad_qkv.astype(f32), axis=0).reshape(3, own_width)
    grad_normed = team.reduce(
        against(grad_qkv, whole_qkv).reshape(by_member + (width,))
    ).reshape(own_rows, width)
    first_pull = jax.vjp(layer_norm, own_tokens, gain_one, shift_one)[1]
    token_part, first_gain_grad, first_shift_grad = first_pull(grad_normed)
    row_grad = (grad_middle + token_part).astype(bf16)
    tokens_grad = team.to_sequences(row_grad.reshape(micro_count, block_rows, width))

    row_bits = rows_first(fsdp_bits + pair_bits)
    pair_first = pair_bits + fsdp_bits[:1] + fsdp_bits[:0:-1]
    pair_second = fsdp_bits[:1] + pair_bits + fsdp_bits[:0:-1]
    down_sum = scatter_bits(
        down_grad.reshape(split(row_bits) + (unit, width)), row_bits, pair_first
    )

    def by_columns(grad, order):
        total = scatter_bits(
            grad.reshape(split(row_bits) + (size, -1) + grad.shape[1:]), row_bits, order
        )
        return team.swap(total, 0, 1)

    up_sum = by_columns(up_grad, pair_second)
    up_sum = jnp.swapaxes(up_sum.reshape(-1, size, hidden // (size * unit), unit), 1, 2)
    up_sum = up_sum.reshape(-1, hidden)
    qkv_sum = by_columns(qkv_grad, pair_first).reshape(-1, size, 3, own_heads, head_size)
    qkv_sum = jnp.swapaxes(qkv_sum, 2, 3).reshape(-1, 3 * width)
    all_bits = rows_first(fsdp_bits + pair_bits + team_bits)
    out_sum = scatter_bits(
        out_grad.reshape(split(all_bits) + (-1, width)), all_bits, team_bits[::-1] + pair_first
    )

    devices = fsdp_shards * shards

    def spread(own, count):
        at_member = jnp.arange(size).reshape(1, size, 1) == member
        return jnp.where(at_member, own.reshape(count, 1, -1), 0.0)

    up_vector = spread(up_bias_grad, hidden // (size * unit)).reshape(devices, unit)
    by_team = lambda own: spread(own.reshape(1, own_width), 1).reshape(width)
    vectors = [
        first_gain_grad,
        first_shift_grad,
        second_gain_grad,
        second_shift_grad,
        out_bias_grad,
        down_bias_grad,
        by_team(column_sums[0]),
        by_team(column_sums[2]),
    ]
    buffer = jnp.concatenate([v.reshape(devices, -1) for v in vectors] + [up_vector], axis=1)
    buffer = buffer.reshape(split(all_bits) + (-1,))
    held = list(all_bits)
    for bit in team_bits + pair_first:
        at, mine = held.index(bit), is_set(*bit)
        sent = lax.dynamic_index_in_dim(buffer, 1 - mine, at, keepdims=False)
        kept = lax.dynamic_index_in_dim(buffer, mine, at, keepdims=False)
        buffer = kept + exchange(sent, *bit)
        held.remove(bit)
    each = width // devices
    sums = [buffer[i * each : (i + 1) * each] for i in range(8)]
    return (
        block_out,
        tokens_grad,
        sums[0],
        sums[1],
        qkv_sum,
        jnp.stack([sums[6], sums[7]]),
        out_sum,
        sums[4],
        sums[2],
        sums[3],
        up_sum,
        buffer[8 * each :],
        down_sum,
        sums[5],
    )


BRIEF = pl.CostEstimate(flops=1, bytes_accessed=1, transcendentals=0)


def whole_block(array):
    return pl.BlockSpec(array.shape, lambda *_: (0,) * array.ndim, pipeline_mode=pl.Buffered(1))


def lanes(ref, block):
    return ref[:, pl.ds(pl.multiple_of(block * 128, 128), 128)]


def member_of(order):
    return order[1] & 1


def pair_of(order):
    return order[1] >> 1


def owner(order, i):
    return order[0] ^ ((i & 3) * 2 + (i >> 2))


def mixed_block(order, i):
    return owner(order, i) ^ (member_of(order) * 4 + pair_of(order) * 2)


def picked(ref, order, first, block_of=owner):
    return jnp.concatenate([lanes(ref, block_of(order, first + i)) for i in range(4)], axis=1)


def flat(ref, start):
    value = ref[start : start + 4, :128]
    return value.reshape(512, value.shape[-1])


class Weight:
    def __init__(self, *parts):
        self.parts = parts

    def slabs(self):
        found = []
        for pair in self.parts:
            for array, _, columns, which in pair:
                if not any(array is a and (columns, which) == b for a, b in found):
                    found.append((array, (columns, which)))
        return found

    def inputs(self):
        result = []
        for array, (columns, which) in self.slabs():
            spec = pl.BlockSpec(
                array.shape[:2] + (columns,),
                lambda *_, which=which: (0, 0, which),
                pipeline_mode=pl.Buffered(1),
            )
            result.append((array, spec))
        return result

    def views(self, refs):
        slabs = self.slabs()

        def find(view):
            array, first, columns, which = view
            at = [array is a and (columns, which) == b for a, b in slabs].index(True)
            return refs[at], first

        return [(find(pair[0]), find(pair[1])) for pair in self.parts]


def grid_call(name, kernel, order, grid, inputs, outputs, scratch=(), limit=48):
    return pl.pallas_call(
        kernel,
        name=name,
        grid_spec=pltpu.PrefetchScalarGridSpec(
            num_scalar_prefetch=1,
            grid=grid,
            in_specs=[spec for _, spec in inputs],
            out_specs=[spec for _, spec in outputs],
            scratch_shapes=list(scratch),
        ),
        out_shape=[shape for shape, _ in outputs],
        compiler_params=pltpu.CompilerParams(vmem_limit_bytes=limit << 20),
        cost_estimate=BRIEF,
    )(order, *[a for a, _ in inputs])


def shape_of(shape, dtype):
    return jax.ShapeDtypeStruct(shape, dtype)


def normalized(values):
    row_mean = jnp.mean(values, axis=-1, keepdims=True)
    centered = values - row_mean
    rstd = lax.rsqrt(jnp.mean(centered * centered, axis=-1, keepdims=True) + epsilon)
    return centered * rstd, rstd


def first_norm(order, tokens, came, other_mine, other_came, vectors):
    _, block, width = tokens.shape

    def kernel(order, mine_ref, came_ref, other_mine_ref, other_came_ref, vec_ref, out_ref):
        def write(ref):
            xhat, _ = normalized(ref[...].astype(f32))
            out_ref[...] = (xhat * vec_ref[0:1] + vec_ref[1:2]).astype(bf16)

        at = pl.program_id(0)
        for i, ref in enumerate((mine_ref.at[0], came_ref, other_mine_ref, other_came_ref)):
            pl.when(at == i)(partial(write, ref))

    def place(i, o):
        return (((i % 2) ^ pair_of(o)) * 2 + ((i // 2) ^ member_of(o)), 0)

    return grid_call(
        "first_norm",
        kernel,
        order,
        (4,),
        [(tokens, pl.BlockSpec((1, block, width), lambda i, o: (pair_of(o), 0, 0)))]
        + [(a, whole_block(a)) for a in (came, other_mine, other_came, vectors)],
        [(shape_of((4 * block, width), bf16), pl.BlockSpec((block, width), place))],
    )[0]


def project(order, normed, bias, part, weight, block=256):
    rows, width = normed.shape
    columns = bias.shape[1]
    step = columns // len(weight.parts)

    def kernel(order, lhs_ref, bias_ref, *rest):
        out_ref = rest[-1]
        left = [picked(lhs_ref, order, 0), picked(lhs_ref, order, 4)]
        for at, views in enumerate(weight.views(rest[:-1])):
            total = sum(mm(l, flat(*view), PLAIN) for l, view in zip(left, views))
            here = slice(at * step, (at + 1) * step)
            out_ref[:, here] = (total + bias_ref[part : part + 1, here]).astype(bf16)

    return grid_call(
        "project",
        kernel,
        order,
        (rows // block,),
        [(normed, pl.BlockSpec((block, width), lambda i, o: (i, 0))), (bias, whole_block(bias))]
        + weight.inputs(),
        [(shape_of((rows, columns), bf16), pl.BlockSpec((block, columns), lambda i, o: (i, 0)))],
    )[0]


def out_and_norm(order, mixed, tokens, vectors, weight, block=256):
    rows, width = mixed.shape

    def kernel(order, lhs_ref, tok_ref, vec_ref, *rest):
        middle_ref, norm_ref = rest[-2:]
        left = [picked(lhs_ref, order, i, mixed_block) for i in (0, 4)]
        for at, views in enumerate(weight.views(rest[:-2])):
            total = sum(mm(l, flat(*view), PLAIN) for l, view in zip(left, views))
            start = pl.multiple_of((member_of(order) ^ at) * (width // 2), 128)
            middle_ref[:, pl.ds(start, width // 2)] = total
        middle = tok_ref[...].astype(f32) + (middle_ref[...] + vec_ref[4:5])
        middle_ref[...] = middle
        xhat, _ = normalized(middle)
        norm_ref[...] = (xhat * vec_ref[2:3] + vec_ref[3:4]).astype(bf16)

    row = pl.BlockSpec((block, width), lambda i, o: (i, 0))
    return grid_call(
        "out_and_norm",
        kernel,
        order,
        (rows // block,),
        [(mixed, row), (tokens, row)]
        + [(vectors, whole_block(vectors))]
        + weight.inputs(),
        [(shape_of((rows, width), f32), row), (shape_of((rows, width), bf16), row)],
    )


def both(block, width):
    return (
        pl.BlockSpec((block, width), lambda i, o: (jnp.minimum(i, 1), 0)),
        pl.BlockSpec((block, width), lambda i, o: (jnp.maximum(i - 2, 0), 0)),
    )


def either(own_ref, other_ref, run):
    at = pl.program_id(0)
    pl.when(at < 2)(lambda: run(own_ref, True))
    pl.when(at >= 2)(lambda: run(other_ref, False))


ROOT = math.sqrt(2.0 / math.pi)


def gelu_and_slope(z):
    inner = jnp.tanh(ROOT * (z + 0.044715 * (z * z * z)))
    half_up = 0.5 * (1.0 + inner)
    slope = half_up + 0.5 * z * (1.0 - inner * inner) * (ROOT * (1.0 + 3 * 0.044715 * (z * z)))
    return z * half_up, slope


def feed_up(order, own, other, bias, part, weight):
    rows, width = own.shape
    block = rows // 2
    columns = bias.shape[1]

    def kernel(order, own_ref, other_ref, bias_ref, *rest):
        act_ref, slope_ref = rest[-2:]

        def run(lhs_ref, _):
            left = [picked(lhs_ref, order, 0), picked(lhs_ref, order, 4)]
            (views,) = weight.views(rest[:-2])
            total = sum(mm(l, flat(*view), PLAIN) for l, view in zip(left, views))
            act, slope = gelu_and_slope(total + bias_ref[part : part + 1])
            act_ref[...] = act.astype(bf16)
            slope_ref[...] = slope.astype(bf16)

        either(own_ref, other_ref, run)

    row = pl.BlockSpec((block, columns), lambda i, o: (i, 0))
    return grid_call(
        "feed_up",
        kernel,
        order,
        (4,),
        list(zip((own, other), both(block, width)))
        + [(bias, whole_block(bias))]
        + weight.inputs(),
        [(shape_of((2 * rows, columns), bf16), row)] * 2,
    )


def own_and_sent(rows, width):
    block = rows // 2
    return list(
        zip(
            (shape_of((rows, width), f32), shape_of((rows, width), bf16)),
            both(block, width),
        )
    )


def feed_down(order, acts, weight):
    rows, columns = acts[0].shape
    width = 1024
    block = rows // 4
    count = len(acts)

    def kernel(order, *rest):
        own_ref, sent_ref = rest[-2:]
        total = 0.0
        for part, views in zip(rest[:count], weight.views(rest[count:-2])):
            for half, view in enumerate(views):
                total = total + mm(picked(part, order, 4 * half), flat(*view), PLAIN)

        def save(ref, _):
            ref[...] = total.astype(ref.dtype)

        either(own_ref, sent_ref, save)

    return grid_call(
        "feed_down",
        kernel,
        order,
        (4,),
        [(act, pl.BlockSpec((block, columns), lambda i, o: (i, 0))) for act in acts]
        + weight.inputs(),
        own_and_sent(rows // 2, width),
    )


def feed_down_back(order, own, other, slope, weight):
    rows, width = own.shape
    columns = slope.shape[1]
    block = rows // 2
    step = columns // len(weight.parts)

    def kernel(order, own_ref, other_ref, slope_ref, *rest):
        out_ref, sum_ref = rest[-2:]

        @pl.when(pl.program_id(0) == 0)
        def _():
            sum_ref[...] = jnp.zeros_like(sum_ref)

        def run(lhs_ref, _):
            left = lhs_ref[...]
            for at, views in enumerate(weight.views(rest[:-2])):
                for half, view in enumerate(views):
                    total = mm(left, flat(*view), ACROSS)
                    for k in range(4):
                        start = at * step + owner(order, 4 * half + k) * 128
                        here = pl.ds(pl.multiple_of(start, 128), 128)
                        value = total[:, 128 * k : 128 * (k + 1)] * slope_ref[:, here].astype(f32)
                        low = value.astype(bf16)
                        out_ref[:, here] = low
                        sum_ref[:, here] += jnp.sum(
                            low.astype(f32).reshape(block // 8, 8, 128), axis=0
                        )

        either(own_ref, other_ref, run)

    row = pl.BlockSpec((block, columns), lambda i, o: (i, 0))
    return grid_call(
        "feed_down_back",
        kernel,
        order,
        (4,),
        list(zip((own, other), both(block, width)))
        + [(slope, row)]
        + weight.inputs(),
        [
            (shape_of((2 * rows, columns), bf16), row),
            (shape_of((8, columns), f32), pl.BlockSpec((8, columns), lambda i, o: (0, 0))),
        ],
    )


def feed_up_back(order, grads, weight):
    rows, columns = grads[0].shape
    width = 1024
    block = rows // 4
    count = len(grads)

    def kernel(order, *rest):
        own_ref, sent_ref = rest[-2:]

        def save(ref, _):
            views = weight.views(rest[count:-2])
            for half in range(2):
                total = 0.0
                for grad_ref, pair in zip(rest[:count], views):
                    total = total + mm(grad_ref[...], flat(*pair[half]), ACROSS)
                for k in range(4):
                    here = pl.ds(pl.multiple_of(owner(order, 4 * half + k) * 128, 128), 128)
                    ref[:, here] = total[:, 128 * k : 128 * (k + 1)].astype(ref.dtype)

        either(own_ref, sent_ref, save)

    return grid_call(
        "feed_up_back",
        kernel,
        order,
        (4,),
        [(grad, pl.BlockSpec((block, columns), lambda i, o: (i, 0))) for grad in grads]
        + weight.inputs(),
        own_and_sent(rows // 2, width),
    )


def rows_of_eight(value):
    return jnp.sum(value.reshape(value.shape[0] // 8, 8, value.shape[1]), axis=0)


def norm_back(xhat, rstd, grad_norm, gain):
    scaled = grad_norm * gain
    return rstd * (
        scaled
        - jnp.mean(scaled, axis=-1, keepdims=True)
        - xhat * jnp.mean(scaled * xhat, axis=-1, keepdims=True)
    )


def middle_back(order, own, came, middle, grad_out, vectors, weight, block=256):
    rows, width = middle.shape
    half_width = width // 2

    def kernel(order, own_ref, came_ref, middle_ref, dy_ref, vec_ref, *rest):
        grad_ref, low_ref, keep_ref, sent_ref, sum_ref, tmp = rest[-6:]

        @pl.when(pl.program_id(0) == 0)
        def _():
            sum_ref[...] = jnp.zeros_like(sum_ref)

        grad_norm = own_ref[...] + came_ref[...].astype(f32)
        xhat, rstd = normalized(middle_ref[...])
        grad_out = dy_ref[...].astype(f32)
        grad_middle = grad_out + norm_back(xhat, rstd, grad_norm, vec_ref[2:3])
        grad_ref[...] = grad_middle
        low = grad_middle.astype(bf16)
        low_ref[...] = low
        sum_ref[0] += rows_of_eight(grad_norm * xhat)
        sum_ref[1] += rows_of_eight(grad_norm)
        sum_ref[2] += rows_of_eight(low.astype(f32))
        sum_ref[3] += rows_of_eight(grad_out)
        views = weight.views(rest[:-6])
        member = member_of(order)
        for half in range(2):
            total = 0.0
            for at, pair in enumerate(views):
                start = pl.multiple_of((member ^ at) * half_width, 128)
                total = total + mm(low_ref[:, pl.ds(start, half_width)], flat(*pair[half]), ACROSS)
            for k in range(4):
                here = pl.ds(pl.multiple_of(mixed_block(order, 4 * half + k) * 128, 128), 128)
                tmp[:, here] = total[:, 128 * k : 128 * (k + 1)].astype(bf16)
        keep_ref[...] = tmp[:, :half_width]
        sent_ref[...] = tmp[:, half_width:]

    row = pl.BlockSpec((block, width), lambda i, o: (i, 0))
    part = pl.BlockSpec((block, half_width), lambda i, o: (i, 0))
    return grid_call(
        "middle_back",
        kernel,
        order,
        (rows // block,),
        [(own, row), (came, row), (middle, row), (grad_out, row), (vectors, whole_block(vectors))]
        + weight.inputs(),
        [
            (shape_of((rows, width), f32), row),
            (shape_of((rows, width), bf16), row),
            (shape_of((rows, half_width), bf16), part),
            (shape_of((rows, half_width), bf16), part),
            (shape_of((4, 8, width), f32), pl.BlockSpec((4, 8, width), lambda i, o: (0, 0, 0))),
        ],
        scratch=[pltpu.VMEM((block, width), bf16)],
    )


def project_back(order, grads, weight):
    rows = grads[0][0].shape[0]
    block = rows // 4
    width = 1024
    given = [g for half in grads for g in half]

    def kernel(order, *rest):
        parts = rest[:6]
        own_ref, sent_ref = rest[-2:]

        def save(ref, _):
            views = weight.views(rest[6:-2])
            lefts = [
                jnp.concatenate([r[...] for r in parts[3 * i : 3 * i + 3]], axis=1) for i in range(2)
            ]
            for half in range(2):
                total = 0.0
                for left, pair in zip(lefts, views):
                    total = total + mm(left, flat(*pair[half]), ACROSS)
                for k in range(4):
                    here = pl.ds(pl.multiple_of(owner(order, 4 * half + k) * 128, 128), 128)
                    ref[:, here] = total[:, 128 * k : 128 * (k + 1)].astype(ref.dtype)

        either(own_ref, sent_ref, save)

    row = pl.BlockSpec(
        (block, given[0].shape[1]), lambda i, o: (((i % 2) ^ pair_of(o)) * 2 + ((i // 2) ^ member_of(o)), 0)
    )
    return grid_call(
        "project_back",
        kernel,
        order,
        (4,),
        [(g, row) for g in given] + weight.inputs(),
        own_and_sent(rows // 2, width),
    )


def first_back(order, own, came, tokens, grad_middle, vectors, block=256):
    rows, width = own.shape

    def kernel(order, own_ref, came_ref, tok_ref, mid_ref, vec_ref, out_ref, sum_ref):
        @pl.when(pl.program_id(0) == 0)
        def _():
            sum_ref[...] = jnp.zeros_like(sum_ref)

        grad_norm = own_ref[...] + came_ref[...].astype(f32)
        xhat, rstd = normalized(tok_ref[...].astype(f32))
        total = mid_ref[...] + norm_back(xhat, rstd, grad_norm, vec_ref[0:1])
        out_ref[...] = total.astype(bf16)
        sum_ref[0] += rows_of_eight(grad_norm * xhat)
        sum_ref[1] += rows_of_eight(grad_norm)

    row = pl.BlockSpec((block, width), lambda i, o: (i, 0))
    return grid_call(
        "first_back",
        kernel,
        order,
        (rows // block,),
        [(own, row), (came, row), (tokens, row), (grad_middle, row), (vectors, whole_block(vectors))],
        [
            (shape_of((rows, width), bf16), row),
            (shape_of((2, 8, width), f32), pl.BlockSpec((2, 8, width), lambda i, o: (0, 0, 0))),
        ],
    )


def weight_grad(order, first, count, lefts, rights, block_of=owner):
    pieces = [r for right in rights for r in right]
    wide = sum(r.shape[1] for r in rights[0])
    together = 2

    def kernel(order, *rest):
        left_refs, right_refs, out_ref = rest[: len(lefts)], rest[len(lefts) : -1], rest[-1]
        at = first + together * pl.program_id(0)
        left = [
            jnp.concatenate([lanes(ref, block_of(order, at + k)) for k in range(together)], axis=1)
            for ref in left_refs
        ]
        each = len(rights[0])
        start = 0
        for j in range(each):
            total = 0.0
            for i in range(len(lefts)):
                total = total + mm(left[i], right_refs[i * each + j][...], DOWN)
            width = total.shape[1]
            out_ref[:, :, start : start + width] = total.reshape(together, 128, width).astype(bf16)
            start += width

    return grid_call(
        "weight_grad",
        kernel,
        order,
        (count // together,),
        [(a, whole_block(a)) for a in lefts] + [(a, whole_block(a)) for a in pieces],
        [
            (
                shape_of((count, 128, wide), bf16),
                pl.BlockSpec((together, 128, wide), lambda i, o: (i, 0, 0)),
            )
        ],
    )[0]


def head_of(order, part):
    return member_of(order) * 8 + (pair_of(order) ^ part) * 4 + 2 * pl.program_id(0)


def team_attend_kernel(part, order, q_ref, k_ref, v_ref, o_ref, total_ref, vt, su):
    at = pl.program_id(1)
    block = q_ref.shape[0]

    @pl.when(at == 0)
    def _():
        vt[...] = v_ref[...].T
        set_bias(order[2], head_of(order, part), su)

    def branch(b):
        nk = (b + 1) * block
        q = q_ref[...]
        outs, totals = [], []
        for h in range(2):
            st = scores(k_ref, q, h, su, nk, block)
            m = jnp.max(st, axis=0, keepdims=True)
            p = jnp.exp(st - m)
            l = jnp.sum(p, axis=0, keepdims=True)
            ot = mm(vt[64 * h : 64 * h + 64, :nk], p.astype(bf16), PLAIN)
            outs.append(ot / l)
            totals.append(m + jnp.log(l))
        o_ref[...] = jnp.concatenate(outs, axis=0).T.astype(bf16)
        total_ref[0] = jnp.concatenate(totals + [jnp.zeros((6, block), f32)], axis=0)

    for b in range(k_ref.shape[0] // block):
        pl.when(at == b)(partial(branch, b))


def kept_place(i, o):
    return ((i % 2) ^ member_of(o)) * 2 + ((i // 2) ^ pair_of(o))


def team_attend(order, qkv, part, block):
    rows = qkv.shape[0]
    whole = lambda kind: pl.BlockSpec((rows, 128), lambda p, i, o: (0, 2 * kind + p))
    return pl.pallas_call(
        partial(team_attend_kernel, part),
        name="team_attend",
        grid_spec=pltpu.PrefetchScalarGridSpec(
            num_scalar_prefetch=1,
            grid=(2, rows // block),
            in_specs=[pl.BlockSpec((block, 128), lambda p, i, o: (i, p)), whole(1), whole(2)],
            out_specs=[
                pl.BlockSpec((block, 128), lambda p, i, o: (kept_place(i, o), p)),
                pl.BlockSpec((1, 8, block), lambda p, i, o: (p, 0, i)),
            ],
            scratch_shapes=[pltpu.VMEM((128, rows), bf16), pltpu.VMEM((2, rows, 128), f32)],
        ),
        out_shape=[shape_of((rows, 256), bf16), shape_of((2, 8, rows), f32)],
        compiler_params=pltpu.CompilerParams(vmem_limit_bytes=40 << 20),
        cost_estimate=BRIEF,
    )(order, qkv, qkv, qkv)


def team_back_kernel(
    part, order, q_ref, k_ref, v_ref, g_ref, total_ref, dq_ref, dk_ref, dv_ref, sum_ref,
    kt, su, dk, dv
):
    at = pl.program_id(1)
    block = q_ref.shape[0]
    blocks = k_ref.shape[0] // block

    @pl.when(at == 0)
    def _():
        kt[...] = k_ref[...].T
        set_bias(order[2], head_of(order, part), su)
        dk[...] = jnp.zeros_like(dk)
        dv[...] = jnp.zeros_like(dv)
        sum_ref[...] = jnp.zeros_like(sum_ref)

    def branch(b):
        nk = (b + 1) * block
        q, g = q_ref[...], g_ref[...]
        outs, dks, dvs = [], [], []
        for h in range(2):
            st = scores(k_ref, q, h, su, nk, block)
            p = jnp.exp(st - total_ref[0, h : h + 1])
            gm = half(g, h)
            dp = mm(v_ref[:nk], gm, ACROSS)
            inner = jnp.sum(p * dp, axis=0, keepdims=True)
            ds = (p * (dp - inner)).astype(bf16)
            outs.append(mm(kt[64 * h : 64 * h + 64, :nk], ds, PLAIN))
            dks.append(mm(ds, half(q, h), PLAIN))
            dvs.append(mm(p.astype(bf16), gm, PLAIN))
        low = (jnp.concatenate(outs, axis=0).T * 0.125).astype(bf16)
        dq_ref[...] = low
        sum_ref[0, 0] += rows_of_eight(low.astype(f32))
        dk[:nk] += dks[0] + dks[1]
        dv[:nk] += dvs[0] + dvs[1]

    for b in range(blocks):
        pl.when(at == b)(partial(branch, b))

    @pl.when(at == blocks - 1)
    def _():
        dk_ref[...] = (dk[...] * 0.125).astype(bf16)
        low = dv[...].astype(bf16)
        dv_ref[...] = low
        sum_ref[0, 1] = rows_of_eight(low.astype(f32))


def team_back(order, qkv, grad, totals, part, block):
    rows = qkv.shape[0]
    whole = lambda kind: pl.BlockSpec((rows, 128), lambda p, i, o: (0, 2 * kind + p))
    by_rows = pl.BlockSpec((block, 128), lambda p, i, o: (i, p))
    by_head = pl.BlockSpec((rows, 128), lambda p, i, o: (0, p))
    return pl.pallas_call(
        partial(team_back_kernel, part),
        name="team_back",
        grid_spec=pltpu.PrefetchScalarGridSpec(
            num_scalar_prefetch=1,
            grid=(2, rows // block),
            in_specs=[
                by_rows,
                whole(1),
                whole(2),
                pl.BlockSpec((block, 128), lambda p, i, o: (kept_place(i, o), 2 * part + p)),
                pl.BlockSpec((1, 8, block), lambda p, i, o: (p, 0, i)),
            ],
            out_specs=[
                by_rows,
                by_head,
                by_head,
                pl.BlockSpec((1, 2, 8, 128), lambda p, i, o: (p, 0, 0, 0)),
            ],
            scratch_shapes=[
                pltpu.VMEM((128, rows), bf16),
                pltpu.VMEM((2, rows, 128), f32),
                pltpu.VMEM((rows, 128), f32),
                pltpu.VMEM((rows, 128), f32),
            ],
        ),
        out_shape=[shape_of((rows, 256), bf16)] * 3 + [shape_of((2, 2, 8, 128), f32)],
        compiler_params=pltpu.CompilerParams(vmem_limit_bytes=48 << 20),
        cost_estimate=BRIEF,
    )(order, qkv, qkv, qkv, grad, totals)


def joined(arrays, rows=None):
    rows = rows or arrays[0].shape[0]
    width = arrays[0].shape[1]
    count = len(arrays)

    def kernel(*refs):
        for i in range(count):
            refs[-1][i] = refs[i][:rows]

    return pl.pallas_call(
        kernel,
        name="joined",
        out_shape=shape_of((count, rows, width), arrays[0].dtype),
        compiler_params=pltpu.CompilerParams(vmem_limit_bytes=32 << 20),
        cost_estimate=BRIEF,
    )(*arrays)


def units(order, qkv_weight, out_weight, up_weight, down_weight, packed):
    def kernel(order, qkv_ref, out_ref, up_ref, down_ref, packed_ref, q_unit, o_unit, u_first, u_second, d_unit):
        c, x = member_of(order), pair_of(order)
        heads = qkv_ref[:, pl.ds(pl.multiple_of((c * 2 + x) * 768, 128), 768)]
        q_unit[:128] = jnp.concatenate(
            [
                heads[:, n * 192 + kind * 64 : n * 192 + kind * 64 + 64]
                for kind in range(3)
                for n in range(4)
            ],
            axis=1,
        )
        q_unit[128:] = jnp.concatenate([packed_ref[...], jnp.zeros((16, 640), bf16)], axis=1)
        o_unit[...] = out_ref[:, pl.ds(pl.multiple_of(c * 512, 128), 512)]
        for i in range(8):
            u_first[:, 128 * i : 128 * i + 128] = lanes(up_ref, i * 4 + x * 2 + c)
            u_second[:, 128 * i : 128 * i + 128] = lanes(up_ref, i * 4 + (1 - x) * 2 + c)
        d_unit[...] = down_ref[...]

    shapes = [(144, 768), (128, 512), (128, 1024), (128, 1024), (128, 1024)]
    return grid_call(
        "units",
        kernel,
        order,
        (1,),
        [(a, whole_block(a)) for a in (qkv_weight, out_weight, up_weight)]
        + [(down_weight, pl.BlockSpec((128, 1024), lambda i, o: (o[1], 0)))]
        + [(packed, whole_block(packed))],
        [(shape_of(s, bf16), pl.BlockSpec(s, lambda i, o: (0, 0))) for s in shapes],
    )


def unpacked(order, mine, came):
    def kernel(order, mine_ref, came_ref, vec_ref, qkv_ref, up_ref, tmp):
        c, x = member_of(order), pair_of(order)
        for i in range(8):
            values = (mine_ref if i < 4 else came_ref)[i % 4].astype(f32)
            start = owner(order, i) * 128
            vec_ref[:, pl.ds(pl.multiple_of(start, 128), 128)] = values
            tmp[i] = values
            for part in range(2):
                row = tmp[i, pl.ds(8 + (x ^ part) * 2 + c, 1)]
                up_ref[part : part + 1, pl.ds(pl.multiple_of(start, 128), 128)] = row
        for part in range(2):
            here = pl.ds(pl.multiple_of(c * 512 + (x ^ part) * 256, 128), 256)
            qkv_ref[part : part + 1] = jnp.concatenate(
                [vec_ref[6:7, here], jnp.zeros((1, 256), f32), vec_ref[7:8, here]], axis=1
            )

    spec = pl.BlockSpec((4, 16, 128), lambda i, o: (0, 8, 0))
    shapes = [(16, 1024), (2, 768), (2, 1024)]
    return grid_call(
        "unpacked",
        kernel,
        order,
        (1,),
        [(mine, spec), (came, spec)],
        [(shape_of(s, f32), pl.BlockSpec(s, lambda i, o: (0, 0))) for s in shapes],
        scratch=[pltpu.VMEM((8, 16, 128), f32)],
    )


def one_of(pair, index):
    return lax.dynamic_index_in_dim(pair, index, 0, keepdims=False)


def flipped(pair, index):
    return jnp.where(index == 0, pair, pair[::-1])


def after(value, *earlier):
    return lax.optimization_barrier((value,) + earlier)[0]


def team_program(
    tokens,
    cotangent,
    lengths,
    first_gain,
    first_shift,
    qkv_weight,
    qv_bias,
    out_weight,
    out_bias,
    second_gain,
    second_shift,
    up_weight,
    up_bias,
    down_weight,
    down_bias,
):
    _, block, width = tokens.shape
    own_rows = 2 * block
    f, s = lax.axis_index("fsdp"), lax.axis_index("seq")
    x, c = s // 2, s % 2
    over_core = lambda v: exchange(v, "seq", 1)
    over_x = lambda v: exchange(v, "seq", 2)
    over_y = lambda v: exchange(v, "fsdp", 1)
    over_z = lambda v, k: exchange(v, "fsdp", 2 * k)
    along_z = lambda v: joined([v] + [over_z(v, k) for k in (1, 2, 3)])

    length = one_of(lengths, x)
    order = jnp.stack([f, s, length]).astype(jnp.int32)

    packed = jnp.concatenate(
        [
            first_gain, first_shift, second_gain, second_shift, out_bias, down_bias,
            qv_bias[0], qv_bias[1], up_bias, jnp.zeros((512,), bf16),
        ]
    ).reshape(16, 128)
    order = [jnp.stack([f, s, length]).astype(jnp.int32)]

    def wait_for(*values):
        order[0] = after(order[0], *values)

    def run(kernel, *operands, **options):
        result = kernel(order[0], *operands, **options)
        wait_for(result[0] if isinstance(result, (list, tuple)) else result)
        return result

    def along_z(unit):
        pieces = [unit] + [over_z(unit, k) for k in (1, 2, 3)]
        result = joined([after(pieces[0], order[0])] + pieces[1:])
        wait_for(result)
        return result

    full = lambda a, b: ((a, 0, a.shape[2], 0), (b, 0, b.shape[2], 0))

    unit_qkv, unit_out, unit_up, unit_up_other, unit_down = run(
        units, qkv_weight, out_weight, up_weight, down_weight, packed
    )
    tokens_came = over_x(one_of(tokens, 1 - x))
    other_mine = over_core(one_of(tokens, x))
    other_came = over_core(tokens_came)
    own_tokens = jnp.concatenate([one_of(tokens, x), tokens_came])
    z_qkv = along_z(unit_qkv)
    y_qkv, xz_qkv = over_y(z_qkv), over_x(z_qkv)
    xy_qkv = over_x(y_qkv)
    qkv_own, qkv_other = full(z_qkv, y_qkv), full(xz_qkv, xy_qkv)
    z_out = along_z(after(unit_out, z_qkv))
    y_out = over_y(z_out)
    out = Weight(full(z_out, y_out), full(over_core(z_out), over_core(y_out)))
    vectors, bias_qkv, bias_up = run(unpacked, z_qkv, y_qkv)

    blocks_at = (jnp.arange(2) ^ x) * 2 + c
    valid = ((blocks_at[:, None] * block + jnp.arange(block)) < length).reshape(own_rows, 1)
    normed = run(first_norm, tokens, tokens_came, other_mine, other_came, vectors)
    projected = [None, None]
    mixed, totals = [None, None], [None, None]
    projected[0] = run(project, normed, bias_qkv, 0, Weight(qkv_own))
    z_up = along_z(after(unit_up, z_out))
    y_up = over_y(z_up)
    mixed[0], totals[0] = run(team_attend, projected[0], 0, block)
    projected[1] = run(project, normed, bias_qkv, 1, Weight(qkv_other))
    mixed[1], totals[1] = run(team_attend, projected[1], 1, block)
    z_down = along_z(after(unit_down, z_up))
    y_down, xz_down = over_y(z_down), over_x(z_down)
    down = [full(z_down, y_down), full(xz_down, over_x(y_down))]
    sent = jnp.concatenate([m[own_rows:] for m in mixed], axis=1)
    mixed_rows = jnp.concatenate([m[:own_rows] for m in mixed] + [over_core(sent)], axis=1)
    middle, norm_own = run(out_and_norm, mixed_rows, own_tokens, vectors, out)
    norm_other = over_core(norm_own)
    grad_came = over_x(one_of(after(cotangent, xy_qkv), 1 - x))
    grad_own = jnp.concatenate([one_of(cotangent, x), grad_came])
    grad_own = jnp.where(valid, grad_own, jnp.zeros_like(grad_own))
    grad_other = over_core(grad_own)
    grad_all = jnp.concatenate([grad_own, grad_other])
    norm_all = jnp.concatenate([norm_own, norm_other])

    act, slope, grad_pre, pre_sums = ([None, None] for _ in range(4))
    up_sent, up_kept, up_came = ([None, None] for _ in range(3))

    def hidden_grad(part):
        up_sent[part] = run(weight_grad, 4, 4, [norm_all], [[grad_pre[part]]])
        up_came[part] = over_y(up_sent[part])

    act[0], slope[0] = run(feed_up, norm_own, norm_other, bias_up, 0, Weight(full(z_up, y_up)))
    down_kept = run(weight_grad, 0, 8, [act[0]], [[grad_all]])
    z_up_other = along_z(after(unit_up_other, z_down))
    y_up_other = over_y(z_up_other)
    up = [full(z_up, y_up), full(z_up_other, y_up_other)]
    grad_pre[0], pre_sums[0] = run(feed_down_back, grad_own, grad_other, slope[0], Weight(down[0]))
    hidden_grad(0)
    up_kept[0] = run(weight_grad, 0, 4, [norm_all], [[grad_pre[0]]])
    act[1], slope[1] = run(feed_up, norm_own, norm_other, bias_up, 1, Weight(up[1]))
    down_sent = [None, None]
    for i in (1, 0):
        down_sent[i] = run(weight_grad, 4 * i, 4, [act[1]], [[grad_all]])
    down_came = [over_x(sent) for sent in down_sent]
    grad_pre[1], pre_sums[1] = run(feed_down_back, grad_own, grad_other, slope[1], Weight(down[1]))
    hidden_grad(1)
    back_own, back_sent = run(feed_up_back, grad_pre, Weight(*up))
    back_came = over_core(back_sent)
    up_kept[1] = run(weight_grad, 0, 4, [norm_all], [[grad_pre[1]]])
    grad_middle, branch, mixed_kept, mixed_sent, middle_sums = run(
        middle_back, back_own, back_came, middle, grad_own, vectors, out
    )
    grad_mixed = jnp.concatenate([mixed_kept, over_core(mixed_sent)])

    def out_grad(i):
        columns = lax.dynamic_slice(branch, (0, i * 512), (own_rows, 512))
        return run(weight_grad, 0, 8, [mixed_rows], [[columns]], block_of=mixed_block)

    out_sent = out_grad(1 - c)
    out_came = over_core(out_sent)
    out_kept = out_grad(c)

    def added(kept, came):
        return kept.astype(f32) + came.astype(f32)

    def low_sum(kept, came):
        return added(kept, came).astype(bf16)

    def z_pieces(total):
        return [total[k].astype(bf16) for k in (1, 2, 3)]

    def sum_z(total, pieces):
        result = total[0]
        for k, piece in enumerate(pieces):
            result = result + over_z(piece, k + 1).astype(f32)
        return result

    up_x = low_sum(up_kept[1], up_came[1])
    up_x_came = over_x(up_x)
    down_y = low_sum(down_kept[4:], down_came[1])
    down_y_came = over_y(down_y)
    out_total = jnp.swapaxes(added(out_kept, out_came).reshape(2, 4, 128, 512), 0, 1)
    out_pieces = z_pieces(out_total)
    wait_for(up_x, down_y, *out_pieces)
    *heads_other, sums_other = run(team_back, projected[1], grad_mixed, totals[1], 1, block)
    other_sent = run(weight_grad, 4, 4, [normed], [heads_other])
    other_y_came = over_y(other_sent)
    other_kept = run(weight_grad, 0, 4, [normed], [heads_other])
    out_y = sum_z(out_total, out_pieces)
    out_y_sent = out_y[1].astype(bf16)
    wait_for(out_y_sent)
    *heads_own, sums_own = run(team_back, projected[0], grad_mixed, totals[0], 0, block)
    own_sent = run(weight_grad, 4, 4, [normed], [heads_own])
    own_y_came = over_y(own_sent)
    down_total = added(low_sum(down_kept[:4], down_came[0]), down_y_came)
    down_pieces = z_pieces(down_total)
    wait_for(*down_pieces)
    first_own, first_sent = run(
        project_back, [heads_own, heads_other], Weight(qkv_own, qkv_other)
    )
    first_came = over_core(first_sent)
    other_x = low_sum(other_kept, other_y_came)
    up_total = added(low_sum(up_kept[0], up_came[0]), up_x_came)
    up_pieces = z_pieces(up_total)
    wait_for(other_x, *up_pieces)
    own_kept = run(weight_grad, 0, 4, [normed], [heads_own])
    row_grad, first_sums = run(first_back, first_own, first_came, own_tokens, grad_middle, vectors)
    fed_own, fed_sent = run(feed_down, act, Weight(*down))
    block_own = jnp.where(
        valid, middle + (fed_own + over_core(fed_sent).astype(f32)) + vectors[5:6], 0.0
    ).astype(bf16)

    def to_devices(rows):
        return flipped(jnp.stack([rows[:block], over_x(rows[block:])]), x)

    tokens_grad = to_devices(row_grad)
    block_out = to_devices(block_own)

    def over_pair(total):
        pieces = total.reshape(2, 64, -1)
        rows = flipped(jnp.stack([one_of(pieces, x), over_x(one_of(pieces, 1 - x))]), x)
        return jnp.swapaxes(rows, 0, 1)

    def over_team(total):
        pieces = total.reshape((2, 32) + total.shape[1:])
        rows = flipped(jnp.stack([one_of(pieces, c), over_core(one_of(pieces, 1 - c))]), c)
        return jnp.swapaxes(rows, 0, 1)

    down_sum = sum_z(down_total, down_pieces)
    up_sum = over_team(over_pair(sum_z(up_total, up_pieces)))
    up_sum = up_sum.reshape(32, 2, 2, 8, 128).transpose(0, 3, 2, 1, 4).reshape(32, 4096)
    out_x = added(out_y[0], over_y(out_y_sent)).reshape(2, 64, 512)
    out_sum = added(one_of(out_x, x), over_x(one_of(out_x, 1 - x).astype(bf16)))
    out_sum = over_team(out_sum).reshape(32, width)
    qkv_total = added(own_kept, own_y_came) + over_x(other_x).astype(f32)
    qkv_sum = over_team(over_pair(sum_z(qkv_total, z_pieces(qkv_total))))
    qkv_sum = qkv_sum.reshape(32, 2, 2, 3, 4, 64)
    qkv_sum = jnp.transpose(qkv_sum, (0, 1, 2, 4, 3, 5)).reshape(32, 3 * width)

    places = f ^ jnp.array([0, 2, 4, 6, 1, 3, 5, 7], jnp.int32)

    def sum_vectors(buffer):
        buffer = buffer.reshape(8, 2, 2, -1)
        at_core = jnp.moveaxis(buffer, 2, 0)
        buffer = one_of(at_core, c) + over_core(one_of(at_core, 1 - c))
        at_x = jnp.moveaxis(buffer, 1, 0)
        buffer = one_of(at_x, x) + over_x(one_of(at_x, 1 - x))
        buffer = jnp.take(buffer, places, axis=0)
        buffer = buffer[:4] + over_y(buffer[4:])
        total = buffer[0]
        for k in (1, 2, 3):
            total = total + over_z(buffer[k], k)
        return total

    at_member = jnp.arange(2) == c
    up_vector = flipped(jnp.sum(jnp.stack(pre_sums), axis=1).reshape(2, 8, 128), x)
    up_vector = jnp.where(
        at_member[None, None, :, None], jnp.swapaxes(up_vector, 0, 1)[:, :, None], 0.0
    ).reshape(32, 128)
    middle_sums = jnp.sum(middle_sums, axis=1)
    early = sum_vectors(
        jnp.concatenate([middle_sums[i].reshape(32, 32) for i in range(4)] + [up_vector], axis=1)
    )
    head_sums = flipped(jnp.sum(jnp.stack([sums_own, sums_other]), axis=3), x)

    def head_vector(kind):
        return jnp.where(at_member[:, None], head_sums[:, :, kind].reshape(1, 512), 0.0).reshape(32, 32)

    first_sums = jnp.sum(first_sums, axis=1)
    late = sum_vectors(
        jnp.concatenate(
            [first_sums[i].reshape(32, 32) for i in range(2)] + [head_vector(0), head_vector(1)],
            axis=1,
        )
    )
    return (
        block_out,
        tokens_grad,
        late[:32],
        late[32:64],
        qkv_sum,
        jnp.stack([late[64:96], late[96:]]),
        out_sum,
        early[64:96],
        early[:32],
        early[32:64],
        up_sum,
        early[128:],
        down_sum,
        early[96:128],
    )


def local(tokens, *others):
    width = tokens.shape[2]
    shards = (lax.axis_size("fsdp"), lax.axis_size("seq"))
    hidden = others[10].shape[1]
    if tokens.shape[0] == 2 and tokens.shape[1] % 256 == 0 and shards == (8, 4) and tokens.shape[1] * 4 <= 1024 and (width, hidden) == (1024, 4096):
        return team_program(tokens, *others)
    return general_program(tokens, *others)


def solution(mesh):
    return jax.shard_map(
        local,
        mesh=mesh,
        in_specs=(
            P("fsdp", "seq", None),
            P("fsdp", "seq", None),
            P("fsdp"),
            P("fsdp"),
            P("fsdp"),
            P("fsdp", None),
            P(None, "fsdp"),
            P("fsdp", None),
            P("fsdp"),
            P("fsdp"),
            P("fsdp"),
            P("fsdp", None),
            P("fsdp"),
            P("fsdp", None),
            P("fsdp"),
        ),
        out_specs=(
            P("fsdp", "seq", None),
            P("fsdp", "seq", None),
            P(("fsdp", "seq")),
            P(("fsdp", "seq")),
            P(("fsdp", "seq"), None),
            P(None, ("fsdp", "seq")),
            P(("fsdp", "seq"), None),
            P(("fsdp", "seq")),
            P(("fsdp", "seq")),
            P(("fsdp", "seq")),
            P(("fsdp", "seq"), None),
            P(("fsdp", "seq")),
            P(("fsdp", "seq"), None),
            P(("fsdp", "seq")),
        ),
        check_vma=False,
    )
```

time: 1450 us -> 518 us (0.36)
  waiting for transfers between devices: 815 us -> 153 us
  matrix products: 211 us -> 0 us
  blocking collectives: 192 us -> 0 us
  Pallas kernels: 0 us -> 171 us
  starting transfers between devices: 33.5 us -> 83.6 us
  local copies, waits for them, and re-layouts: 105 us -> 64 us
  other arithmetic: 56.9 us -> 34.9 us
  loops' own time: 16.4 us -> 0 us
    reduce_scatter x4 -> x0, waiting for transfers between devices: 659 us -> none  [the longest x1 188 us: local(): lax.psum_scatter(summed[10], ('fsdp', 'seq'), scatter_dimension=0, tiled=...]
    dot_general x52 -> x0, matrix products: 211 us -> none  [the longest x8 54.7 us: contract_rows(): lax.dot_general(left_side, right_side, (((0,), (0,)), ((), ())), preferre...]
    pallas_call x0 -> x37, Pallas kernels: none -> 171 us  [the longest x28 116 us: grid_call(): pl.pallas_call(kernel, name=name, grid_spec=pltpu.PrefetchScalarGridSpec(...]
    all_gather x8 -> x0, blocking collectives: 155 us -> none  [the longest x1 26.4 us: local(): lax.all_gather(up_bias, 'fsdp', axis=0, tiled=True)]
    ppermute x0 -> x80, waiting for transfers between devices: none -> 153 us  [exchange(): lax.ppermute(value, axis, [(i, i ^ bit) for i in range(lax.axis_size(axis...]
    all_gather x4 -> x0, waiting for transfers between devices: 117 us -> none  [the longest x1 75.9 us: local(): lax.all_gather(down_weight, 'fsdp', axis=0, tiled=True)]
    ppermute x0 -> x80, starting transfers between devices: none -> 83.6 us  [exchange(): lax.ppermute(value, axis, [(i, i ^ bit) for i in range(lax.axis_size(axis...]
    unnamed x1 -> x0, blocking collectives: 37.6 us -> none
  transfers between devices with their start and end apart: 17 -> 80, of which waited for: 10 -> 23; matrix products, arithmetic and copies ran while one was open for 17% -> 11% of each run, Pallas kernels for 0% -> 30%
where the time goes in v1:
time: 518 us; the launch traced here: 509 us
  Pallas kernels  171 us (33%)
  waiting for transfers between devices  153 us (30%)
  starting transfers between devices  83.6 us (16%)
  local copies, waits for them, and re-layouts  64 us (12%)
  other arithmetic  34.9 us (7%)
    ppermute x80, waiting for transfers between devices, exchange(): lax.ppermute(value, axis, [(i, i ^ bit) for i in range(lax.axis_size(axis...  153 us
    pallas_call x28, Pallas kernels, grid_call(): pl.pallas_call(kernel, name=name, grid_spec=pltpu.PrefetchScalarGridSpec(...  116 us
    ppermute x80, starting transfers between devices, exchange(): lax.ppermute(value, axis, [(i, i ^ bit) for i in range(lax.axis_size(axis...  83.6 us
    unnamed x211, local copies, waits for them, and re-layouts  35.9 us
    pallas_call x2, Pallas kernels, team_back(): pl.pallas_call(partial(team_back_kernel, part), name='team_back', grid_sp...  28.7 us
    pallas_call x2, Pallas kernels, team_attend(): pl.pallas_call(partial(team_attend_kernel, part), name='team_attend', gri...  21.9 us
  transfers between devices with their start and end apart: 80, of which 23 were waited for; matrix products, arithmetic and copies ran while one was open for 11% of the time, Pallas kernels for 30%

profile of v1, /device:TPU:0, one launch (start us, length us, event | category | flops | bytes accessed | tf_op | source)
XLA Modules:
  0.0 508.8 jit_solution(3452812922657391368)
XLA Ops:
  16.0 5.0 collective-permute-start.2
  21.6 5.8 %collective-permute-done.2.refs_3_ = bf16[144,768]{1,0:T(8,128)(2,1)S(1)} collective-permute-done((bf16[144,768]{1,0:T(8,128)(2,1)S(1)}, bf16[144,768]{1,0:T(8,128)(2,1)S(1)}, u32[]{:S(2)}, u32[]{:S(2)}) %collective-permute-start.2) | collective-permute-done | bytes 221216 | tf_op jit(solution)/shard_map/ppermute | solution.py:151
  27.4 12.4 %collective-permute-done.1.refs_2_ = bf16[144,768]{1,0:T(8,128)(2,1)S(1)} collective-permute-done((bf16[144,768]{1,0:T(8,128)(2,1)S(1)}, bf16[144,768]{1,0:T(8,128)(2,1)S(1)}, u32[]{:S(2)}, u32[]{:S(2)}) %collective-permute-start.1) | collective-permute-done | bytes 221216 | tf_op jit(solution)/shard_map/ppermute | solution.py:151
  48.2 13.6 %collective-permute-done.6.came_ref.rest_1_.rest_7_ = bf16[4,144,768]{2,1,0:T(8,128)(2,1)} collective-permute-done((bf16[4,144,768]{2,1,0:T(8,128)(2,1)}, bf16[4,144,768]{2,1,0:T(8,128)(2,1)}, u32[]{:S(2)}, u32[]{:S(2)}) %collective-permute-start.6) | collective-permute-done | bytes 884768 | tf_op jit(solution)/shard_map/ppermute | solution.py:151
  64.1 5.9 %collective-permute-done.4.refs_2_ = bf16[128,512]{1,0:T(8,128)(2,1)S(1)} collective-permute-done((bf16[128,512]{1,0:T(8,128)(2,1)S(1)}, bf16[128,512]{1,0:T(8,128)(2,1)S(1)}, u32[]{:S(2)}, u32[]{:S(2)}) %collective-permute-start.4) | collective-permute-done | bytes 131104 | tf_op jit(solution)/shard_map/ppermute | solution.py:151
  70.0 5.0 collective-permute-done.3.refs_1_
  79.7 4.6 collective-permute-done.12.refs_3_
  85.0 6.8 %collective-permute-start.11 = (bf16[128,1024]{1,0:T(8,128)(2,1)}, bf16[128,1024]{1,0:T(8,128)(2,1)}, u32[]{:S(2)}, u32[]{:S(2)}) collective-permute-start(bf16[128,1024]{1,0:T(8,128)(2,1)} %get-tuple-element.122.refs_0_), channel_id=1, source_target_pairs={{0,16},{4,20},{8,24},{12,28},{16,0},{20,4},{24,8},{28,12},{1,17},{... | collective-permute-start | bytes 786440 | tf_op jit(solution)/shard_map/ppermute | solution.py:151
  97.4 4.4 project.2.q_ref.k_ref.v_ref
  106.0 10.8 %team_attend.2 = (bf16[1024,256]{1,0:T(8,128)(2,1)S(1)}, f32[2,8,1024]{2,1,0:T(8,128)S(1)}) custom-call(s32[3]{0:T(128)S(1)} %pad_add_fusion.order, bf16[1024,768]{1,0:T(8,128)(2,1)S(1)} %project.2.q_ref.k_ref.v_ref, bf16[1024,768]{1,0:T(8,128)(2,1)S(1)} %project.2.q_ref.k_ref.v_ref, bf16[1024,768]{1,0:T(8,128)(2,1)S(1)} %project.2.q_ref.k_ref.v_ref), custom_call_target="tpu_custom_call" | custom-call | flops 1 | bytes 1 | tf_op jit(solution)/shard_map/team_attend/pallas_call | solution.py:1033
  122.5 11.1 %team_attend.3 = (bf16[1024,256]{1,0:T(8,128)(2,1)S(1)}, f32[2,8,1024]{2,1,0:T(8,128)S(1)}) custom-call(s32[3]{0:T(128)S(1)} %pad_add_fusion.order, bf16[1024,768]{1,0:T(8,128)(2,1)S(1)} %project.3.q_ref.k_ref.v_ref, bf16[1024,768]{1,0:T(8,128)(2,1)S(1)} %project.3.q_ref.k_ref.v_ref, bf16[1024,768]{1,0:T(8,128)(2,1)S(1)} %project.3.q_ref.k_ref.v_ref), custom_call_target="tpu_custom_call" | custom-call | flops 1 | bytes 1 | tf_op jit(solution)/shard_map/team_attend/pallas_call | solution.py:1033
  141.8 6.3 %collective-permute-done.15.refs_1_ = bf16[128,1024]{1,0:T(8,128)(2,1)S(1)} collective-permute-done((bf16[128,1024]{1,0:T(8,128)(2,1)}, bf16[128,1024]{1,0:T(8,128)(2,1)S(1)}, u32[]{:S(2)}, u32[]{:S(2)}) %collective-permute-start.15) | collective-permute-done | bytes 262176 | tf_op jit(solution)/shard_map/ppermute | solution.py:151
  152.3 5.2 %out_and_norm.1 = (f32[512,1024]{1,0:T(8,128)}, bf16[512,1024]{1,0:T(8,128)(2,1)S(1)}) custom-call(s32[3]{0:T(128)S(1)} %pad_add_fusion.order, bf16[512,1024]{1,0:T(8,128)(2,1)S(1)} %pad_maximum_fusion.1.lhs_ref.rest_0_, bf16[512,1024]{1,0:T(8,128)(2,1)S(1)} %pad_maximum_fusion.2.tok_ref, f32[16,1024]{1,0:T(8,128)S(1)} %get-tuple-element.115.vec_ref, ...), custom_call_target="tpu_custom_call" | custom-call | flops 1 | bytes 1 | tf_op jit(solution)/shard_map/out_and_norm/pallas_call | solution.py:546
  162.2 11.9 %collective-permute-done.23.rest_1_.rest_3_ = bf16[4,128,1024]{2,1,0:T(8,128)(2,1)S(1)} collective-permute-done((bf16[4,128,1024]{2,1,0:T(8,128)(2,1)S(1)}, bf16[4,128,1024]{2,1,0:T(8,128)(2,1)S(1)}, u32[]{:S(2)}, u32[]{:S(2)}) %collective-permute-start.23) | collective-permute-done | bytes 1048608 | tf_op jit(solution)/shard_map/ppermute | solution.py:151
  177.1 6.7 %feed_up.2 = (bf16[1024,1024]{1,0:T(8,128)(2,1)}, bf16[1024,1024]{1,0:T(8,128)(2,1)}) custom-call(s32[3]{0:T(128)S(1)} %pad_add_fusion.order, bf16[512,1024]{1,0:T(8,128)(2,1)S(1)} %get-tuple-element.135.own_ref, bf16[512,1024]{1,0:T(8,128)(2,1)S(1)} %collective-permute-done.22.other_ref, f32[2,1024]{1,0:T(2,128)S(1)} %get-tuple-element.136.bias_ref, ...), custom_call_target="tpu_custom_call" | custom-call | flops 1 | bytes 1 | tf_op jit(solution)/shard_map/feed_up/pallas_call | solution.py:546
  186.5 5.2 %weight_grad.13 = bf16[8,128,1024]{2,1,0:T(8,128)(2,1)S(1)} custom-call(s32[3]{0:T(128)S(1)} %pad_add_fusion.order, bf16[1024,1024]{1,0:T(8,128)(2,1)S(1)} %copy-done.30, bf16[1024,1024]{1,0:T(8,128)(2,1)} %pad_maximum_fusion.rest_1_), custom_call_target="tpu_custom_call" | custom-call | flops 1 | bytes 1 | tf_op jit(solution)/shard_map/weight_grad/pallas_call | solution.py:546
  198.3 6.5 %feed_down_back.2 = (bf16[1024,1024]{1,0:T(8,128)(2,1)}, f32[8,1024]{1,0:T(8,128)S(1)}) custom-call(s32[3]{0:T(128)S(1)} %pad_add_fusion.order, bf16[512,1024]{1,0:T(8,128)(2,1)S(1)} %maximum_select_fusion.own_ref.dy_ref, bf16[512,1024]{1,0:T(8,128)(2,1)S(1)} %collective-permute-done.25.other_ref, bf16[1024,1024]{1,0:T(8,128)(2,1)} %get-tuple-element.145.slope_ref, ...), custom_call_target="tpu_custom_call" | custom-call | flops 1 | bytes 1 | tf_op jit(solution)/shard_map/feed_down_back/pallas_call | solution.py:546
  212.9 4.8 collective-permute-done.30.rest_1_.rest_5_
  219.0 7.9 %feed_up.3 = (bf16[1024,1024]{1,0:T(8,128)(2,1)}, bf16[1024,1024]{1,0:T(8,128)(2,1)}) custom-call(s32[3]{0:T(128)S(1)} %pad_add_fusion.order, bf16[512,1024]{1,0:T(8,128)(2,1)S(1)} %get-tuple-element.135.own_ref, bf16[512,1024]{1,0:T(8,128)(2,1)S(1)} %collective-permute-done.22.other_ref, f32[2,1024]{1,0:T(2,128)S(1)} %get-tuple-element.136.bias_ref, ...), custom_call_target="tpu_custom_call" | custom-call | flops 1 | bytes 1 | tf_op jit(solution)/shard_map/feed_up/pallas_call | solution.py:546
  237.2 6.5 %feed_down_back.3 = (bf16[1024,1024]{1,0:T(8,128)(2,1)}, f32[8,1024]{1,0:T(8,128)S(1)}) custom-call(s32[3]{0:T(128)S(1)} %pad_add_fusion.order, bf16[512,1024]{1,0:T(8,128)(2,1)S(1)} %maximum_select_fusion.own_ref.dy_ref, bf16[512,1024]{1,0:T(8,128)(2,1)S(1)} %copy-done.27, bf16[1024,1024]{1,0:T(8,128)(2,1)} %get-tuple-element.154.slope_ref, ...), custom_call_target="tpu_custom_call" | custom-call | flops 1 | bytes 1 | tf_op jit(solution)/shard_map/feed_down_back/pallas_call | solution.py:546
  248.5 9.1 %feed_up_back.1 = (f32[512,1024]{1,0:T(8,128)}, bf16[512,1024]{1,0:T(8,128)(2,1)}) custom-call(s32[3]{0:T(128)S(1)} %pad_add_fusion.order, bf16[1024,1024]{1,0:T(8,128)(2,1)} %get-tuple-element.146.rest_1_.rest_0_, bf16[1024,1024]{1,0:T(8,128)(2,1)} %get-tuple-element.155.rest_1_, bf16[4,128,1024]{2,1,0:T(8,128)(2,1)S(1)} %copy-done.22, ...), custom_call_target="tpu_custom_call" | custom-call | flops 1 | bytes 1 | tf_op jit(solution)/shard_map/feed_up_back/pallas_call | solution.py:546
  266.7 7.5 %middle_back.1 = (f32[512,1024]{1,0:T(8,128)}, bf16[512,1024]{1,0:T(8,128)(2,1)S(1)}, bf16[512,512]{1,0:T(8,128)(2,1)S(1)}, bf16[512,512]{1,0:T(8,128)(2,1)S(1)}, f32[4,8,1024]{2,1,0:T(8,128)S(1)}) custom-call(s32[3]{0:T(128)S(1)} %pad_add_fusion.order, f32[512,1024]{1,0:T(8,128)} %get-tuple-element.158.own_ref, ...), custom_call_target="tpu_custom_call" | custom-call | flops 1 | bytes 1 | tf_op jit(solution)/shard_map/middle_back/pallas_call | solution.py:546
  307.6 14.3 %team_back.2 = (bf16[1024,256]{1,0:T(8,128)(2,1)S(1)}, bf16[1024,256]{1,0:T(8,128)(2,1)S(1)}, bf16[1024,256]{1,0:T(8,128)(2,1)S(1)}, f32[2,2,8,128]{3,2,1,0:T(8,128)S(1)}) custom-call(s32[3]{0:T(128)S(1)} %pad_add_fusion.order, bf16[1024,768]{1,0:T(8,128)(2,1)S(1)} %copy-done.5, bf16[1024,768]{1,0:T(8,128)(2,1)S(1)} %copy-done.5, ...), custom_call_target="tpu_custom_call" | custom-call | flops 1 | bytes 1 | tf_op jit(solution)/shard_map/team_back/pallas_call | solution.py:1104
  324.6 20.0 %collective-permute-done.45 = bf16[4,128,1024]{2,1,0:T(8,128)(2,1)} collective-permute-done((bf16[4,128,1024]{2,1,0:T(8,128)(2,1)}, bf16[4,128,1024]{2,1,0:T(8,128)(2,1)}, u32[]{:S(2)}, u32[]{:S(2)}) %collective-permute-start.45) | collective-permute-done | bytes 1048608 | tf_op jit(solution)/shard_map/ppermute | solution.py:151
  361.0 14.5 %team_back.3 = (bf16[1024,256]{1,0:T(8,128)(2,1)S(1)}, bf16[1024,256]{1,0:T(8,128)(2,1)S(1)}, bf16[1024,256]{1,0:T(8,128)(2,1)S(1)}, f32[2,2,8,128]{3,2,1,0:T(8,128)S(1)}) custom-call(s32[3]{0:T(128)S(1)} %pad_add_fusion.order, bf16[1024,768]{1,0:T(8,128)(2,1)S(1)} %copy-done.3, bf16[1024,768]{1,0:T(8,128)(2,1)S(1)} %copy-done.3, ...), custom_call_target="tpu_custom_call" | custom-call | flops 1 | bytes 1 | tf_op jit(solution)/shard_map/team_back/pallas_call | solution.py:1104
  378.2 8.3 %project_back.1 = (f32[512,1024]{1,0:T(8,128)}, bf16[512,1024]{1,0:T(8,128)(2,1)}) custom-call(s32[3]{0:T(128)S(1)} %pad_add_fusion.order, bf16[1024,256]{1,0:T(8,128)(2,1)S(1)} %get-tuple-element.179.rest_1_.rest_0_, bf16[1024,256]{1,0:T(8,128)(2,1)S(1)} %get-tuple-element.181.rest_2_.rest_1_, bf16[1024,256]{1,0:T(8,128)(2,1)S(1)} %get-tuple-element.182.rest_3_.rest_2_, ...), custom_call_target="tpu_custom_call" | custom-call | flops 1 | bytes 1 | tf_op jit(solution)/shard_map/project_back/pallas_call | solution.py:546
  422.4 18.1 %collective-permute-done.51 = f32[8,128]{1,0:T(8,128)S(1)} collective-permute-done((f32[8,128]{1,0:T(8,128)S(1)}, f32[8,128]{1,0:T(8,128)S(1)}, u32[]{:S(2)}, u32[]{:S(2)}) %collective-permute-start.51) | collective-permute-done | bytes 4128 | tf_op jit(solution)/shard_map/ppermute | solution.py:151
  450.2 8.4 %feed_down.1 = (f32[512,1024]{1,0:T(8,128)}, bf16[512,1024]{1,0:T(8,128)(2,1)S(1)}) custom-call(s32[3]{0:T(128)S(1)} %pad_add_fusion.order, bf16[1024,1024]{1,0:T(8,128)(2,1)} %get-tuple-element.137.rest_0_, bf16[1024,1024]{1,0:T(8,128)(2,1)} %get-tuple-element.150.rest_0_.rest_1_, bf16[4,128,1024]{2,1,0:T(8,128)(2,1)S(1)} %copy-done.17, ...), custom_call_target="tpu_custom_call" | custom-call | flops 1 | bytes 1 | tf_op jit(solution)/shard_map/feed_down/pallas_call | solution.py:546
  469.3 5.3 %collective-permute-done.60 = bf16[128,768]{1,0:T(8,128)(2,1)S(1)} collective-permute-done((bf16[128,768]{1,0:T(8,128)(2,1)S(1)}, bf16[128,768]{1,0:T(8,128)(2,1)S(1)}, u32[]{:S(2)}, u32[]{:S(2)}) %collective-permute-start.60) | collective-permute-done | bytes 196640 | tf_op jit(solution)/shard_map/ppermute | solution.py:151
  474.6 8.5 %collective-permute-done.59 = bf16[128,768]{1,0:T(8,128)(2,1)S(1)} collective-permute-done((bf16[128,768]{1,0:T(8,128)(2,1)S(1)}, bf16[128,768]{1,0:T(8,128)(2,1)S(1)}, u32[]{:S(2)}, u32[]{:S(2)}) %collective-permute-start.59) | collective-permute-done | bytes 196640 | tf_op jit(solution)/shard_map/ppermute | solution.py:151
  484.4 5.1 %collective-permute-done.61 = f32[64,768]{1,0:T(8,128)S(1)} collective-permute-done((f32[64,768]{1,0:T(8,128)S(1)}, f32[64,768]{1,0:T(8,128)S(1)}, u32[]{:S(2)}, u32[]{:S(2)}) %collective-permute-start.61) | collective-permute-done | bytes 196640 | tf_op jit(solution)/shard_map/ppermute | solution.py:151
  495.0 10.9 %collective-permute-done.48 = bf16[256,1024]{1,0:T(8,128)(2,1)} collective-permute-done((bf16[256,1024]{1,0:T(8,128)(2,1)}, bf16[256,1024]{1,0:T(8,128)(2,1)}, u32[]{:S(2)}, u32[]{:S(2)}) %collective-permute-start.48) | collective-permute-done | bytes 524320 | tf_op jit(solution)/shard_map/ppermute | solution.py:151
  (503 shorter events, 229.7 us)
Async XLA Ops:
  45.2 32.2 %collective-permute-start.8 = (bf16[256,1024]{1,0:T(8,128)(2,1)S(1)}, bf16[256,1024]{1,0:T(8,128)(2,1)S(1)}, u32[]{:S(2)}, u32[]{:S(2)}) collective-permute-start(bf16[256,1024]{1,0:T(8,128)(2,1)S(1)} %get-tuple-element.231), channel_id=1, source_target_pairs={{0,1},{1,0},{2,3},{3,2},{4,5},{5,4},{6,7},{7,6},{8,9},{9,8},{10,11... | collective-permute-start | bytes 1572872 | tf_op jit(solution)/shard_map/ppermute | solution.py:151
  47.7 69.2 %collective-permute-start.13 = (bf16[4,144,768]{2,1,0:T(8,128)(2,1)}, bf16[4,144,768]{2,1,0:T(8,128)(2,1)}, u32[]{:S(2)}, u32[]{:S(2)}) collective-permute-start(bf16[4,144,768]{2,1,0:T(8,128)(2,1)} %joined.5.mine_ref.rest_0_.rest_6_), channel_id=1, source_target_pairs={{0,2},{1,3},{2,0},{3,1},{4,6},{5,7},{6,4},{7,5},{8,10},{9,11},{10,... | collective-permute-start | bytes 2654216 | tf_op jit(solution)/shard_map/ppermute | solution.py:151
  61.8 56.3 %collective-permute-start.14 = (bf16[4,144,768]{2,1,0:T(8,128)(2,1)}, bf16[4,144,768]{2,1,0:T(8,128)(2,1)}, u32[]{:S(2)}, u32[]{:S(2)}) collective-permute-start(bf16[4,144,768]{2,1,0:T(8,128)(2,1)} %collective-permute-done.6.came_ref.rest_1_.rest_7_), channel_id=1, source_target_pairs={{0,2},{1,3},{2,0},{3,1},{4,6},{5,7},{6,4},{7,5},{8,10},{9,11},{10,... | collective-permute-start | bytes 2654216 | tf_op jit(solution)/shard_map/ppermute | solution.py:151
  64.1 27.6 %collective-permute-start.9 = (bf16[256,1024]{1,0:T(8,128)(2,1)S(1)}, bf16[256,1024]{1,0:T(8,128)(2,1)S(1)}, u32[]{:S(2)}, u32[]{:S(2)}) collective-permute-start(bf16[256,1024]{1,0:T(8,128)(2,1)S(1)} %collective-permute-done.7.came_ref), channel_id=1, source_target_pairs={{0,1},{1,0},{2,3},{3,2},{4,5},{5,4},{6,7},{7,6},{8,9},{9,8},{10,11... | collective-permute-start | bytes 1572872 | tf_op jit(solution)/shard_map/ppermute | solution.py:151
  101.8 50.5 %collective-permute-start.20 = (bf16[4,128,512]{2,1,0:T(8,128)(2,1)}, bf16[4,128,512]{2,1,0:T(8,128)(2,1)}, u32[]{:S(2)}, u32[]{:S(2)}) collective-permute-start(bf16[4,128,512]{2,1,0:T(8,128)(2,1)} %joined.6.rest_0_), channel_id=1, source_target_pairs={{0,1},{1,0},{2,3},{3,2},{4,5},{5,4},{6,7},{7,6},{8,9},{9,8},{10,11... | collective-permute-start | bytes 1572872 | tf_op jit(solution)/shard_map/ppermute | solution.py:151
  101.9 50.4 %collective-permute-start.21 = (bf16[4,128,512]{2,1,0:T(8,128)(2,1)}, bf16[4,128,512]{2,1,0:T(8,128)(2,1)}, u32[]{:S(2)}, u32[]{:S(2)}) collective-permute-start(bf16[4,128,512]{2,1,0:T(8,128)(2,1)} %collective-permute-done.19.rest_1_), channel_id=1, source_target_pairs={{0,1},{1,0},{2,3},{3,2},{4,5},{5,4},{6,7},{7,6},{8,9},{9,8},{10,11... | collective-permute-start | bytes 1572872 | tf_op jit(solution)/shard_map/ppermute | solution.py:151
  103.6 32.5 %collective-permute-start.17 = (bf16[128,1024]{1,0:T(8,128)(2,1)}, bf16[128,1024]{1,0:T(8,128)(2,1)S(1)}, u32[]{:S(2)}, u32[]{:S(2)}) collective-permute-start(bf16[128,1024]{1,0:T(8,128)(2,1)} %get-tuple-element.131.refs_0_), channel_id=1, source_target_pairs={{0,24},{4,28},{8,16},{12,20},{16,8},{20,12},{24,0},{28,4},{1,25},{... | collective-permute-start | bytes 786440 | tf_op jit(solution)/shard_map/ppermute | solution.py:151
  148.1 26.1 %collective-permute-start.23 = (bf16[4,128,1024]{2,1,0:T(8,128)(2,1)S(1)}, bf16[4,128,1024]{2,1,0:T(8,128)(2,1)S(1)}, u32[]{:S(2)}, u32[]{:S(2)}) collective-permute-start(bf16[4,128,1024]{2,1,0:T(8,128)(2,1)S(1)} %copy-done.21), channel_id=1, source_target_pairs={{0,4},{4,0},{8,12},{12,8},{16,20},{20,16},{24,28},{28,24},{1,5},{5... | collective-permute-start | bytes 3145736 | tf_op jit(solution)/shard_map/ppermute | solution.py:151
  158.8 25.0 %collective-permute-start.25 = (bf16[512,1024]{1,0:T(8,128)(2,1)S(1)}, bf16[512,1024]{1,0:T(8,128)(2,1)S(1)}, u32[]{:S(2)}, u32[]{:S(2)}) collective-permute-start(bf16[512,1024]{1,0:T(8,128)(2,1)S(1)} %maximum_select_fusion.own_ref.dy_ref), channel_id=1, source_target_pairs={{0,1},{1,0},{2,3},{3,2},{4,5},{5,4},{6,7},{7,6},{8,9},{9,8},{10,11... | collective-permute-start | bytes 3145736 | tf_op jit(solution)/shard_map/ppermute | solution.py:151
  159.4 37.3 %collective-permute-start.29 = (bf16[4,128,1024]{2,1,0:T(8,128)(2,1)S(1)}, bf16[4,128,1024]{2,1,0:T(8,128)(2,1)S(1)}, u32[]{:S(2)}, u32[]{:S(2)}) collective-permute-start(bf16[4,128,1024]{2,1,0:T(8,128)(2,1)S(1)} %joined.8.rest_0_.rest_2_), channel_id=1, source_target_pairs={{0,4},{4,0},{8,12},{12,8},{16,20},{20,16},{24,28},{28,24},{1,5},{5... | collective-permute-start | bytes 3145736 | tf_op jit(solution)/shard_map/ppermute | solution.py:151
  159.9 31.9 %collective-permute-start.28 = (bf16[128,1024]{1,0:T(8,128)(2,1)S(1)}, bf16[128,1024]{1,0:T(8,128)(2,1)S(1)}, u32[]{:S(2)}, u32[]{:S(2)}) collective-permute-start(bf16[128,1024]{1,0:T(8,128)(2,1)S(1)} %get-tuple-element.143.refs_0_), channel_id=1, source_target_pairs={{0,24},{4,28},{8,16},{12,20},{16,8},{20,12},{24,0},{28,4},{1,25},{... | collective-permute-start | bytes 786440 | tf_op jit(solution)/shard_map/ppermute | solution.py:151
  191.9 25.8 %collective-permute-start.30 = (bf16[4,128,1024]{2,1,0:T(8,128)(2,1)S(1)}, bf16[4,128,1024]{2,1,0:T(8,128)(2,1)}, u32[]{:S(2)}, u32[]{:S(2)}) collective-permute-start(bf16[4,128,1024]{2,1,0:T(8,128)(2,1)S(1)} %joined.9.rest_0_.rest_4_), channel_id=1, source_target_pairs={{0,4},{4,0},{8,12},{12,8},{16,20},{20,16},{24,28},{28,24},{1,5},{5... | collective-permute-start | bytes 3145736 | tf_op jit(solution)/shard_map/ppermute | solution.py:151
  193.4 40.2 %collective-permute-start.31 = (bf16[4,128,1024]{2,1,0:T(8,128)(2,1)S(1)}, bf16[4,128,1024]{2,1,0:T(8,128)(2,1)S(1)}, u32[]{:S(2)}, u32[]{:S(2)}) collective-permute-start(bf16[4,128,1024]{2,1,0:T(8,128)(2,1)S(1)} %joined.8.rest_0_.rest_2_), channel_id=1, source_target_pairs={{0,2},{1,3},{2,0},{3,1},{4,6},{5,7},{6,4},{7,5},{8,10},{9,11},{10,... | collective-permute-start | bytes 3145736 | tf_op jit(solution)/shard_map/ppermute | solution.py:151
  196.7 40.5 %collective-permute-start.32 = (bf16[4,128,1024]{2,1,0:T(8,128)(2,1)S(1)}, bf16[4,128,1024]{2,1,0:T(8,128)(2,1)S(1)}, u32[]{:S(2)}, u32[]{:S(2)}) collective-permute-start(bf16[4,128,1024]{2,1,0:T(8,128)(2,1)S(1)} %collective-permute-done.29.rest_1_.rest_3_), channel_id=1, source_target_pairs={{0,2},{1,3},{2,0},{3,1},{4,6},{5,7},{6,4},{7,5},{8,10},{9,11},{10,... | collective-permute-start | bytes 3145736 | tf_op jit(solution)/shard_map/ppermute | solution.py:151
  258.3 26.0 %collective-permute-start.34 = (bf16[4,128,1024]{2,1,0:T(8,128)(2,1)}, bf16[4,128,1024]{2,1,0:T(8,128)(2,1)}, u32[]{:S(2)}, u32[]{:S(2)}) collective-permute-start(bf16[4,128,1024]{2,1,0:T(8,128)(2,1)} %copy-done.67), channel_id=1, source_target_pairs={{0,4},{4,0},{8,12},{12,8},{16,20},{20,16},{24,28},{28,24},{1,5},{5... | collective-permute-start | bytes 3145736 | tf_op jit(solution)/shard_map/ppermute | solution.py:151
  258.9 30.5 %collective-permute-start.35 = (bf16[4,128,1024]{2,1,0:T(8,128)(2,1)}, bf16[4,128,1024]{2,1,0:T(8,128)(2,1)}, u32[]{:S(2)}, u32[]{:S(2)}) collective-permute-start(bf16[4,128,1024]{2,1,0:T(8,128)(2,1)} %copy-done.66), channel_id=1, source_target_pairs={{0,2},{1,3},{2,0},{3,1},{4,6},{5,7},{6,4},{7,5},{8,10},{9,11},{10,... | collective-permute-start | bytes 3145736 | tf_op jit(solution)/shard_map/ppermute | solution.py:151
  277.4 25.2 %collective-permute-start.37 = (bf16[512,512]{1,0:T(8,128)(2,1)}, bf16[512,512]{1,0:T(8,128)(2,1)}, u32[]{:S(2)}, u32[]{:S(2)}) collective-permute-start(bf16[512,512]{1,0:T(8,128)(2,1)} %copy-done.85), channel_id=1, source_target_pairs={{0,1},{1,0},{2,3},{3,2},{4,5},{5,4},{6,7},{7,6},{8,9},{9,8},{10,11... | collective-permute-start | bytes 1572872 | tf_op jit(solution)/shard_map/ppermute | solution.py:151
  297.9 26.6 %collective-permute-start.44 = (bf16[4,128,1024]{2,1,0:T(8,128)(2,1)S(1)}, bf16[4,128,1024]{2,1,0:T(8,128)(2,1)}, u32[]{:S(2)}, u32[]{:S(2)}) collective-permute-start(bf16[4,128,1024]{2,1,0:T(8,128)(2,1)S(1)} %copy-done.65), channel_id=1, source_target_pairs={{0,4},{4,0},{8,12},{12,8},{16,20},{20,16},{24,28},{28,24},{1,5},{5... | collective-permute-start | bytes 3145736 | tf_op jit(solution)/shard_map/ppermute | solution.py:151
  299.5 49.9 %collective-permute-start.41 = (bf16[4,128,1024]{2,1,0:T(8,128)(2,1)S(1)}, bf16[4,128,1024]{2,1,0:T(8,128)(2,1)}, u32[]{:S(2)}, u32[]{:S(2)}) collective-permute-start(bf16[4,128,1024]{2,1,0:T(8,128)(2,1)S(1)} %copy-done.63), channel_id=1, source_target_pairs={{0,2},{1,3},{2,0},{3,1},{4,6},{5,7},{6,4},{7,5},{8,10},{9,11},{10,... | collective-permute-start | bytes 3145736 | tf_op jit(solution)/shard_map/ppermute | solution.py:151
  300.5 44.0 %collective-permute-start.45 = (bf16[4,128,1024]{2,1,0:T(8,128)(2,1)}, bf16[4,128,1024]{2,1,0:T(8,128)(2,1)}, u32[]{:S(2)}, u32[]{:S(2)}) collective-permute-start(bf16[4,128,1024]{2,1,0:T(8,128)(2,1)} %add_convert_fusion.3), channel_id=1, source_target_pairs={{0,2},{1,3},{2,0},{3,1},{4,6},{5,7},{6,4},{7,5},{8,10},{9,11},{10,... | collective-permute-start | bytes 3145736 | tf_op jit(solution)/shard_map/ppermute | solution.py:151
  302.7 48.3 %collective-permute-start.42 = (bf16[4,128,1024]{2,1,0:T(8,128)(2,1)S(1)}, bf16[4,128,1024]{2,1,0:T(8,128)(2,1)}, u32[]{:S(2)}, u32[]{:S(2)}) collective-permute-start(bf16[4,128,1024]{2,1,0:T(8,128)(2,1)S(1)} %add_convert_fusion.2), channel_id=1, source_target_pairs={{0,4},{4,0},{8,12},{12,8},{16,20},{20,16},{24,28},{28,24},{1,5},{5... | collective-permute-start | bytes 3145736 | tf_op jit(solution)/shard_map/ppermute | solution.py:151
  306.0 50.4 %collective-permute-start.40 = (bf16[2,128,512]{2,1,0:T(8,128)(2,1)S(1)}, bf16[2,128,512]{2,1,0:T(8,128)(2,1)S(1)}, u32[]{:S(2)}, u32[]{:S(2)}) collective-permute-start(bf16[2,128,512]{2,1,0:T(8,128)(2,1)S(1)} %get-tuple-element.226), channel_id=1, source_target_pairs={{0,24},{4,28},{8,16},{12,20},{16,8},{20,12},{24,0},{28,4},{1,25},{... | collective-permute-start | bytes 786440 | tf_op jit(solution)/shard_map/ppermute | solution.py:151
  324.6 33.6 %collective-permute-start.39 = (bf16[2,128,512]{2,1,0:T(8,128)(2,1)S(1)}, bf16[2,128,512]{2,1,0:T(8,128)(2,1)S(1)}, u32[]{:S(2)}, u32[]{:S(2)}) collective-permute-start(bf16[2,128,512]{2,1,0:T(8,128)(2,1)S(1)} %get-tuple-element.227), channel_id=1, source_target_pairs={{0,16},{4,20},{8,24},{12,28},{16,0},{20,4},{24,8},{28,12},{1,17},{... | collective-permute-start | bytes 786440 | tf_op jit(solution)/shard_map/ppermute | solution.py:151
  349.4 37.1 %collective-permute-start.74 = (bf16[128,1024]{1,0:T(8,128)(2,1)}, bf16[128,1024]{1,0:T(8,128)(2,1)S(1)}, u32[]{:S(2)}, u32[]{:S(2)}) collective-permute-start(bf16[128,1024]{1,0:T(8,128)(2,1)} %get-tuple-element.220), channel_id=1, source_target_pairs={{0,24},{4,28},{8,16},{12,20},{16,8},{20,12},{24,0},{28,4},{1,25},{... | collective-permute-start | bytes 786440 | tf_op jit(solution)/shard_map/ppermute | solution.py:151
  350.9 57.7 %collective-permute-start.43 = (bf16[4,128,768]{2,1,0:T(8,128)(2,1)}, bf16[4,128,768]{2,1,0:T(8,128)(2,1)}, u32[]{:S(2)}, u32[]{:S(2)}) collective-permute-start(bf16[4,128,768]{2,1,0:T(8,128)(2,1)} %weight_grad.22), channel_id=1, source_target_pairs={{0,4},{4,0},{8,12},{12,8},{16,20},{20,16},{24,28},{28,24},{1,5},{5... | collective-permute-start | bytes 2359304 | tf_op jit(solution)/shard_map/ppermute | solution.py:151
  356.4 31.0 %collective-permute-start.73 = (bf16[128,1024]{1,0:T(8,128)(2,1)}, bf16[128,1024]{1,0:T(8,128)(2,1)S(1)}, u32[]{:S(2)}, u32[]{:S(2)}) collective-permute-start(bf16[128,1024]{1,0:T(8,128)(2,1)} %get-tuple-element.221), channel_id=1, source_target_pairs={{0,16},{4,20},{8,24},{12,28},{16,0},{20,4},{24,8},{28,12},{1,17},{... | collective-permute-start | bytes 786440 | tf_op jit(solution)/shard_map/ppermute | solution.py:151
  358.2 31.3 %collective-permute-start.72 = (bf16[128,1024]{1,0:T(8,128)(2,1)}, bf16[128,1024]{1,0:T(8,128)(2,1)S(1)}, u32[]{:S(2)}, u32[]{:S(2)}) collective-permute-start(bf16[128,1024]{1,0:T(8,128)(2,1)} %get-tuple-element.222), channel_id=1, source_target_pairs={{0,8},{4,12},{8,0},{12,4},{16,24},{20,28},{24,16},{28,20},{1,9},{5... | collective-permute-start | bytes 786440 | tf_op jit(solution)/shard_map/ppermute | solution.py:151
  359.3 32.8 %collective-permute-start.79 = (bf16[128,1024]{1,0:T(8,128)(2,1)S(1)}, bf16[128,1024]{1,0:T(8,128)(2,1)S(1)}, u32[]{:S(2)}, u32[]{:S(2)}) collective-permute-start(bf16[128,1024]{1,0:T(8,128)(2,1)S(1)} %get-tuple-element.223), channel_id=1, source_target_pairs={{0,24},{4,28},{8,16},{12,20},{16,8},{20,12},{24,0},{28,4},{1,25},{... | collective-permute-start | bytes 786440 | tf_op jit(solution)/shard_map/ppermute | solution.py:151
  392.1 68.1 %collective-permute-start.56 = (bf16[4,128,768]{2,1,0:T(8,128)(2,1)}, bf16[4,128,768]{2,1,0:T(8,128)(2,1)}, u32[]{:S(2)}, u32[]{:S(2)}) collective-permute-start(bf16[4,128,768]{2,1,0:T(8,128)(2,1)} %weight_grad.24), channel_id=1, source_target_pairs={{0,4},{4,0},{8,12},{12,8},{16,20},{20,16},{24,28},{28,24},{1,5},{5... | collective-permute-start | bytes 2359304 | tf_op jit(solution)/shard_map/ppermute | solution.py:151
  420.2 40.0 %collective-permute-start.57 = (bf16[4,128,768]{2,1,0:T(8,128)(2,1)}, bf16[4,128,768]{2,1,0:T(8,128)(2,1)}, u32[]{:S(2)}, u32[]{:S(2)}) collective-permute-start(bf16[4,128,768]{2,1,0:T(8,128)(2,1)} %add_convert_fusion.4), channel_id=1, source_target_pairs={{0,2},{1,3},{2,0},{3,1},{4,6},{5,7},{6,4},{7,5},{8,10},{9,11},{10,... | collective-permute-start | bytes 2359304 | tf_op jit(solution)/shard_map/ppermute | solution.py:151
  458.5 25.8 %collective-permute-start.49 = (bf16[256,1024]{1,0:T(8,128)(2,1)S(1)}, bf16[256,1024]{1,0:T(8,128)(2,1)S(1)}, u32[]{:S(2)}, u32[]{:S(2)}) collective-permute-start(bf16[256,1024]{1,0:T(8,128)(2,1)S(1)} %get-tuple-element.217), channel_id=1, source_target_pairs={{0,2},{1,3},{2,0},{3,1},{4,6},{5,7},{6,4},{7,5},{8,10},{9,11},{10,... | collective-permute-start | bytes 1572872 | tf_op jit(solution)/shard_map/ppermute | solution.py:151
  460.2 29.6 %collective-permute-start.47 = (bf16[512,1024]{1,0:T(8,128)(2,1)S(1)}, bf16[512,1024]{1,0:T(8,128)(2,1)S(1)}, u32[]{:S(2)}, u32[]{:S(2)}) collective-permute-start(bf16[512,1024]{1,0:T(8,128)(2,1)S(1)} %get-tuple-element.193), channel_id=1, source_target_pairs={{0,1},{1,0},{2,3},{3,2},{4,5},{5,4},{6,7},{7,6},{8,9},{9,8},{10,11... | collective-permute-start | bytes 3145736 | tf_op jit(solution)/shard_map/ppermute | solution.py:151
  (147 other events, 1544.9 us)

commit v2 on v1

--- a/solution.py
+++ b/solution.py
@@ -472,7 +472,7 @@
     )
 
 
-BRIEF = pl.CostEstimate(flops=1, bytes_accessed=1, transcendentals=0)
+WORK = pl.CostEstimate(flops=10000000000, bytes_accessed=20000000, transcendentals=0)
 
 
 def whole_block(array):
@@ -497,6 +497,10 @@
 
 def mixed_block(order, i):
     return owner(order, i) ^ (member_of(order) * 4 + pair_of(order) * 2)
+
+
+def natural(order, i):
+    return i
 
 
 def picked(ref, order, first, block_of=owner):
@@ -509,8 +513,9 @@
 
 
 class Weight:
-    def __init__(self, *parts):
+    def __init__(self, *parts, orders=None):
         self.parts = parts
+        self.orders = orders or [owner] * len(parts)
 
     def slabs(self):
         found = []
@@ -542,7 +547,7 @@
         return [(find(pair[0]), find(pair[1])) for pair in self.parts]
 
 
-def grid_call(name, kernel, order, grid, inputs, outputs, scratch=(), limit=48):
+def grid_call(name, kernel, order, grid, inputs, outputs, scratch=(), limit=16):
     return pl.pallas_call(
         kernel,
         name=name,
@@ -555,7 +560,7 @@
         ),
         out_shape=[shape for shape, _ in outputs],
         compiler_params=pltpu.CompilerParams(vmem_limit_bytes=limit << 20),
-        cost_estimate=BRIEF,
+        cost_estimate=WORK,
     )(order, *[a for a, _ in inputs])
 
 
@@ -680,12 +685,14 @@
         act_ref, slope_ref = rest[-2:]
 
         def run(lhs_ref, _):
-            left = [picked(lhs_ref, order, 0), picked(lhs_ref, order, 4)]
-            (views,) = weight.views(rest[:-2])
-            total = sum(mm(l, flat(*view), PLAIN) for l, view in zip(left, views))
-            act, slope = gelu_and_slope(total + bias_ref[part : part + 1])
-            act_ref[...] = act.astype(bf16)
-            slope_ref[...] = slope.astype(bf16)
+            left = [picked(lhs_ref, order, i, weight.orders[0]) for i in (0, 4)]
+            step = columns // len(weight.parts)
+            for at, views in enumerate(weight.views(rest[:-2])):
+                total = sum(mm(l, flat(*view), PLAIN) for l, view in zip(left, views))
+                here = slice(at * step, (at + 1) * step)
+                act, slope = gelu_and_slope(total + bias_ref[part : part + 1, here])
+                act_ref[:, here] = act.astype(bf16)
+                slope_ref[:, here] = slope.astype(bf16)
 
         either(own_ref, other_ref, run)
 
@@ -721,9 +728,9 @@
     def kernel(order, *rest):
         own_ref, sent_ref = rest[-2:]
         total = 0.0
-        for part, views in zip(rest[:count], weight.views(rest[count:-2])):
+        for part, views, block_of in zip(rest[:count], weight.views(rest[count:-2]), weight.orders):
             for half, view in enumerate(views):
-                total = total + mm(picked(part, order, 4 * half), flat(*view), PLAIN)
+                total = total + mm(picked(part, order, 4 * half, block_of), flat(*view), PLAIN)
 
         def save(ref, _):
             ref[...] = total.astype(ref.dtype)
@@ -760,7 +767,7 @@
                 for half, view in enumerate(views):
                     total = mm(left, flat(*view), ACROSS)
                     for k in range(4):
-                        start = at * step + owner(order, 4 * half + k) * 128
+                        start = at * step + weight.orders[at](order, 4 * half + k) * 128
                         here = pl.ds(pl.multiple_of(start, 128), 128)
                         value = total[:, 128 * k : 128 * (k + 1)] * slope_ref[:, here].astype(f32)
                         low = value.astype(bf16)
@@ -794,17 +801,20 @@
     count = len(grads)
 
     def kernel(order, *rest):
-        own_ref, sent_ref = rest[-2:]
+        own_ref, sent_ref, tmp = rest[-3:]
+        each = len(weight.parts) // count
+        step = columns // each
+        for at, (pair, block_of) in enumerate(zip(weight.views(rest[count:-3]), weight.orders)):
+            grad = rest[at // each][:, (at % each) * step : (at % each + 1) * step]
+            for half in range(2):
+                total = mm(grad, flat(*pair[half]), ACROSS)
+                for k in range(4):
+                    here = pl.ds(pl.multiple_of(block_of(order, 4 * half + k) * 128, 128), 128)
+                    value = total[:, 128 * k : 128 * (k + 1)]
+                    tmp[:, here] = value if at == 0 else tmp[:, here] + value
 
         def save(ref, _):
-            views = weight.views(rest[count:-2])
-            for half in range(2):
-                total = 0.0
-                for grad_ref, pair in zip(rest[:count], views):
-                    total = total + mm(grad_ref[...], flat(*pair[half]), ACROSS)
-                for k in range(4):
-                    here = pl.ds(pl.multiple_of(owner(order, 4 * half + k) * 128, 128), 128)
-                    ref[:, here] = total[:, 128 * k : 128 * (k + 1)].astype(ref.dtype)
+            ref[...] = tmp[...].astype(ref.dtype)
 
         either(own_ref, sent_ref, save)
 
@@ -816,6 +826,7 @@
         [(grad, pl.BlockSpec((block, columns), lambda i, o: (i, 0))) for grad in grads]
         + weight.inputs(),
         own_and_sent(rows // 2, width),
+        scratch=[pltpu.VMEM((block, width), f32)],
     )
 
 
@@ -837,7 +848,7 @@
     half_width = width // 2
 
     def kernel(order, own_ref, came_ref, middle_ref, dy_ref, vec_ref, *rest):
-        grad_ref, low_ref, keep_ref, sent_ref, sum_ref, tmp = rest[-6:]
+        grad_ref, branch_ref, keep_ref, sent_ref, sum_ref, tmp, low_ref = rest[-7:]
 
         @pl.when(pl.program_id(0) == 0)
         def _():
@@ -854,8 +865,11 @@
         sum_ref[1] += rows_of_eight(grad_norm)
         sum_ref[2] += rows_of_eight(low.astype(f32))
         sum_ref[3] += rows_of_eight(grad_out)
-        views = weight.views(rest[:-6])
+        views = weight.views(rest[:-7])
         member = member_of(order)
+        for i in range(4):
+            from_ = i ^ (member * 2 + pair_of(order))
+            branch_ref[:, 256 * i : 256 * i + 256] = low_ref[:, pl.ds(pl.multiple_of(from_ * 256, 128), 256)]
         for half in range(2):
             total = 0.0
             for at, pair in enumerate(views):
@@ -883,7 +897,7 @@
             (shape_of((rows, half_width), bf16), part),
             (shape_of((4, 8, width), f32), pl.BlockSpec((4, 8, width), lambda i, o: (0, 0, 0))),
         ],
-        scratch=[pltpu.VMEM((block, width), bf16)],
+        scratch=[pltpu.VMEM((block, width), bf16)] * 2,
     )
 
 
@@ -954,38 +968,49 @@
     )
 
 
-def weight_grad(order, first, count, lefts, rights, block_of=owner):
-    pieces = [r for right in rights for r in right]
-    wide = sum(r.shape[1] for r in rights[0])
+def weight_grad(order, first, count, left, rights, block_of=owner, extra=None):
+    wide = sum(columns for _, columns, _ in rights)
+    extra = extra or ()
+    more = extra[0].shape[2] if extra else 0
     together = 2
 
-    def kernel(order, *rest):
-        left_refs, right_refs, out_ref = rest[: len(lefts)], rest[len(lefts) : -1], rest[-1]
+    def kernel(order, left_ref, *rest):
+        right_refs, out_ref = rest[: len(rights)], rest[-1]
         at = first + together * pl.program_id(0)
-        left = [
-            jnp.concatenate([lanes(ref, block_of(order, at + k)) for k in range(together)], axis=1)
-            for ref in left_refs
-        ]
-        each = len(rights[0])
+        lefts = [lanes(left_ref, block_of(order, at + k)) for k in range(together)]
+        picked_left = jnp.concatenate(lefts, axis=1)
         start = 0
-        for j in range(each):
-            total = 0.0
-            for i in range(len(lefts)):
-                total = total + mm(left[i], right_refs[i * each + j][...], DOWN)
+        for ref in right_refs:
+            total = mm(picked_left, ref[...], DOWN)
             width = total.shape[1]
             out_ref[:, :, start : start + width] = total.reshape(together, 128, width).astype(bf16)
             start += width
+        if extra:
+            kept, came = rest[len(rights) : -1]
+            out_ref[:, :, start:] = (kept[...].astype(f32) + came[...].astype(f32)).astype(bf16)
+
+    def right_spec(array, columns, which):
+        return pl.BlockSpec(
+            (array.shape[0], columns), lambda *_: (0, which), pipeline_mode=pl.Buffered(1)
+        )
+
+    def extra_spec(array, which):
+        return pl.BlockSpec(
+            (together, 128, more // 2), lambda i, o: (first // together + i, 0, which)
+        )
 
     return grid_call(
         "weight_grad",
         kernel,
         order,
         (count // together,),
-        [(a, whole_block(a)) for a in lefts] + [(a, whole_block(a)) for a in pieces],
+        [(left, whole_block(left))]
+        + [(right[0], right_spec(*right)) for right in rights]
+        + [(a, extra_spec(a, extra[2])) for a in extra[:2]],
         [
             (
-                shape_of((count, 128, wide), bf16),
-                pl.BlockSpec((together, 128, wide), lambda i, o: (i, 0, 0)),
+                shape_of((count, 128, wide + more // 2), bf16),
+                pl.BlockSpec((together, 128, wide + more // 2), lambda i, o: (i, 0, 0)),
             )
         ],
     )[0]
@@ -1044,8 +1069,8 @@
             scratch_shapes=[pltpu.VMEM((128, rows), bf16), pltpu.VMEM((2, rows, 128), f32)],
         ),
         out_shape=[shape_of((rows, 256), bf16), shape_of((2, 8, rows), f32)],
-        compiler_params=pltpu.CompilerParams(vmem_limit_bytes=40 << 20),
-        cost_estimate=BRIEF,
+        compiler_params=pltpu.CompilerParams(vmem_limit_bytes=16 << 20),
+        cost_estimate=WORK,
     )(order, qkv, qkv, qkv)
 
 
@@ -1128,58 +1153,71 @@
             ],
         ),
         out_shape=[shape_of((rows, 256), bf16)] * 3 + [shape_of((2, 2, 8, 128), f32)],
-        compiler_params=pltpu.CompilerParams(vmem_limit_bytes=48 << 20),
-        cost_estimate=BRIEF,
+        compiler_params=pltpu.CompilerParams(vmem_limit_bytes=24 << 20),
+        cost_estimate=WORK,
     )(order, qkv, qkv, qkv, grad, totals)
 
 
-def joined(arrays, rows=None):
-    rows = rows or arrays[0].shape[0]
-    width = arrays[0].shape[1]
-    count = len(arrays)
-
-    def kernel(*refs):
-        for i in range(count):
-            refs[-1][i] = refs[i][:rows]
+def joined(first, second):
+    count, rows, width = first.shape
+
+    def kernel(first_ref, second_ref, out_ref):
+        out_ref[:count] = first_ref[...]
+        out_ref[count:] = second_ref[...]
 
     return pl.pallas_call(
         kernel,
         name="joined",
-        out_shape=shape_of((count, rows, width), arrays[0].dtype),
-        compiler_params=pltpu.CompilerParams(vmem_limit_bytes=32 << 20),
-        cost_estimate=BRIEF,
-    )(*arrays)
-
-
-def units(order, qkv_weight, out_weight, up_weight, down_weight, packed):
-    def kernel(order, qkv_ref, out_ref, up_ref, down_ref, packed_ref, q_unit, o_unit, u_first, u_second, d_unit):
-        c, x = member_of(order), pair_of(order)
-        heads = qkv_ref[:, pl.ds(pl.multiple_of((c * 2 + x) * 768, 128), 768)]
-        q_unit[:128] = jnp.concatenate(
+        out_shape=shape_of((2 * count, rows, width), first.dtype),
+        compiler_params=pltpu.CompilerParams(vmem_limit_bytes=12 << 20),
+        cost_estimate=WORK,
+    )(first, second)
+
+
+def qkv_unit(order, qkv_weight, packed):
+    def kernel(order, qkv_ref, packed_ref, unit_ref):
+        unit_ref[0, :128] = jnp.concatenate(
             [
-                heads[:, n * 192 + kind * 64 : n * 192 + kind * 64 + 64]
+                qkv_ref[:, n * 192 + kind * 64 : n * 192 + kind * 64 + 64]
                 for kind in range(3)
                 for n in range(4)
             ],
             axis=1,
         )
-        q_unit[128:] = jnp.concatenate([packed_ref[...], jnp.zeros((16, 640), bf16)], axis=1)
-        o_unit[...] = out_ref[:, pl.ds(pl.multiple_of(c * 512, 128), 512)]
-        for i in range(8):
-            u_first[:, 128 * i : 128 * i + 128] = lanes(up_ref, i * 4 + x * 2 + c)
-            u_second[:, 128 * i : 128 * i + 128] = lanes(up_ref, i * 4 + (1 - x) * 2 + c)
-        d_unit[...] = down_ref[...]
-
-    shapes = [(144, 768), (128, 512), (128, 1024), (128, 1024), (128, 1024)]
+        unit_ref[0, 128:] = jnp.concatenate([packed_ref[...], jnp.zeros((16, 640), bf16)], axis=1)
+
+    share = lambda i, o: (0, member_of(o) * 2 + pair_of(o))
     return grid_call(
-        "units",
+        "qkv_unit",
         kernel,
         order,
         (1,),
-        [(a, whole_block(a)) for a in (qkv_weight, out_weight, up_weight)]
-        + [(down_weight, pl.BlockSpec((128, 1024), lambda i, o: (o[1], 0)))]
-        + [(packed, whole_block(packed))],
-        [(shape_of(s, bf16), pl.BlockSpec(s, lambda i, o: (0, 0))) for s in shapes],
+        [(qkv_weight, pl.BlockSpec((128, 768), share)), (packed, whole_block(packed))],
+        [(shape_of((1, 144, 768), bf16), pl.BlockSpec((1, 144, 768), lambda i, o: (0, 0, 0)))],
+    )[0]
+
+
+def other_units(order, out_weight, up_weight, down_weight):
+    def kernel(order, out_ref, up_ref, down_ref, out_unit, own_unit, other_unit, down_unit):
+        c, x = member_of(order), pair_of(order)
+        out_unit[0] = out_ref[...]
+        for i in range(8):
+            own_unit[0, :, 128 * i : 128 * i + 128] = lanes(up_ref, i * 4 + x * 2 + c)
+            other_unit[0, :, 128 * i : 128 * i + 128] = lanes(up_ref, i * 4 + (1 - x) * 2 + c)
+        down_unit[0] = down_ref[...]
+
+    shapes = [(1, 128, 512), (1, 128, 1024), (1, 128, 1024), (1, 128, 1024)]
+    return grid_call(
+        "other_units",
+        kernel,
+        order,
+        (1,),
+        [
+            (out_weight, pl.BlockSpec((128, 512), lambda i, o: (0, member_of(o)))),
+            (up_weight, whole_block(up_weight)),
+            (down_weight, pl.BlockSpec((128, 1024), lambda i, o: (o[1], 0))),
+        ],
+        [(shape_of(s, bf16), pl.BlockSpec(s, lambda i, o: (0, 0, 0))) for s in shapes],
     )
 
 
@@ -1246,21 +1284,17 @@
     own_rows = 2 * block
     f, s = lax.axis_index("fsdp"), lax.axis_index("seq")
     x, c = s // 2, s % 2
-    over_core = lambda v: exchange(v, "seq", 1)
     over_x = lambda v: exchange(v, "seq", 2)
     over_y = lambda v: exchange(v, "fsdp", 1)
     over_z = lambda v, k: exchange(v, "fsdp", 2 * k)
-    along_z = lambda v: joined([v] + [over_z(v, k) for k in (1, 2, 3)])
 
     length = one_of(lengths, x)
+
+    def over_core(value):
+        return lax.cond(length > 0, lambda v: exchange(v, "seq", 1), lambda v: v, value)
+
     order = jnp.stack([f, s, length]).astype(jnp.int32)
 
-    packed = jnp.concatenate(
-        [
-            first_gain, first_shift, second_gain, second_shift, out_bias, down_bias,
-            qv_bias[0], qv_bias[1], up_bias, jnp.zeros((512,), bf16),
-        ]
-    ).reshape(16, 128)
     order = [jnp.stack([f, s, length]).astype(jnp.int32)]
 
     def wait_for(*values):
@@ -1271,92 +1305,124 @@
         wait_for(result[0] if isinstance(result, (list, tuple)) else result)
         return result
 
-    def along_z(unit):
-        pieces = [unit] + [over_z(unit, k) for k in (1, 2, 3)]
-        result = joined([after(pieces[0], order[0])] + pieces[1:])
+    def join(first, second):
+        result = joined(after(first, order[0]), second)
         wait_for(result)
         return result
 
     full = lambda a, b: ((a, 0, a.shape[2], 0), (b, 0, b.shape[2], 0))
 
-    unit_qkv, unit_out, unit_up, unit_up_other, unit_down = run(
-        units, qkv_weight, out_weight, up_weight, down_weight, packed
-    )
+    packed = [first_gain, first_shift, second_gain, second_shift, out_bias, down_bias, qv_bias, up_bias]
+    packed = jnp.concatenate([v.reshape(-1, 128) for v in packed] + [jnp.zeros((4, 128), bf16)])
+    unit_qkv = run(qkv_unit, qkv_weight, packed)
     tokens_came = over_x(one_of(tokens, 1 - x))
-    other_mine = over_core(one_of(tokens, x))
-    other_came = over_core(tokens_came)
-    own_tokens = jnp.concatenate([one_of(tokens, x), tokens_came])
-    z_qkv = along_z(unit_qkv)
+    unit_out, unit_up, unit_up_other, unit_down = run(
+        other_units, out_weight, up_weight, down_weight
+    )
+    own_mine = one_of(tokens, x)
+    other_mine, other_came = over_core(own_mine), over_core(tokens_came)
+    grad_came = over_x(one_of(after(cotangent, tokens_came), 1 - x))
+    z_qkv = join(unit_qkv, over_z(unit_qkv, 1))
+    z_out = over_z(after(unit_out, z_qkv), 1)
+    own_tokens = jnp.concatenate([own_mine, tokens_came])
+    wait_for(other_mine, other_came)
+    z_qkv = join(z_qkv, over_z(z_qkv, 2))
     y_qkv, xz_qkv = over_y(z_qkv), over_x(z_qkv)
+    z_out = join(unit_out, z_out)
+    z_out_came = over_z(z_out, 2)
+    z_up = over_z(after(unit_up, z_out), 1)
+
+    blocks_at = (jnp.arange(2) ^ x) * 2 + c
+    valid = ((blocks_at[:, None] * block + jnp.arange(block)) < length).reshape(own_rows, 1)
+    grad_own = jnp.concatenate([one_of(cotangent, x), grad_came])
+    grad_own = jnp.where(valid, grad_own, jnp.zeros_like(grad_own))
+    grad_other = over_core(grad_own)
+    grad_all = jnp.concatenate([grad_own, grad_other])
+    wait_for(grad_all)
+    z_up = join(unit_up, z_up)
+    z_up_came = over_z(z_up, 2)
+    z_out = join(z_out, z_out_came)
+    y_out = over_y(z_out)
+    z_down = over_z(after(unit_down, z_up), 1)
     xy_qkv = over_x(y_qkv)
     qkv_own, qkv_other = full(z_qkv, y_qkv), full(xz_qkv, xy_qkv)
-    z_out = along_z(after(unit_out, z_qkv))
-    y_out = over_y(z_out)
-    out = Weight(full(z_out, y_out), full(over_core(z_out), over_core(y_out)))
     vectors, bias_qkv, bias_up = run(unpacked, z_qkv, y_qkv)
-
-    blocks_at = (jnp.arange(2) ^ x) * 2 + c
-    valid = ((blocks_at[:, None] * block + jnp.arange(block)) < length).reshape(own_rows, 1)
     normed = run(first_norm, tokens, tokens_came, other_mine, other_came, vectors)
     projected = [None, None]
     mixed, totals = [None, None], [None, None]
     projected[0] = run(project, normed, bias_qkv, 0, Weight(qkv_own))
-    z_up = along_z(after(unit_up, z_out))
+    mixed[0], totals[0] = run(team_attend, projected[0], 0, block)
+    z_up = join(z_up, z_up_came)
     y_up = over_y(z_up)
-    mixed[0], totals[0] = run(team_attend, projected[0], 0, block)
+    z_down = join(unit_down, z_down)
+    z_down_came = over_z(z_down, 2)
+    z_up_other = over_z(after(unit_up_other, z_down), 1)
+    out_other = over_core(jnp.concatenate([z_out, y_out]))
     projected[1] = run(project, normed, bias_qkv, 1, Weight(qkv_other))
+    wait_for(out_other)
     mixed[1], totals[1] = run(team_attend, projected[1], 1, block)
-    z_down = along_z(after(unit_down, z_up))
-    y_down, xz_down = over_y(z_down), over_x(z_down)
-    down = [full(z_down, y_down), full(xz_down, over_x(y_down))]
+    out = Weight(full(z_out, y_out), ((out_other, 0, 512, 0), (out_other, 4, 512, 0)))
     sent = jnp.concatenate([m[own_rows:] for m in mixed], axis=1)
     mixed_rows = jnp.concatenate([m[:own_rows] for m in mixed] + [over_core(sent)], axis=1)
     middle, norm_own = run(out_and_norm, mixed_rows, own_tokens, vectors, out)
     norm_other = over_core(norm_own)
-    grad_came = over_x(one_of(after(cotangent, xy_qkv), 1 - x))
-    grad_own = jnp.concatenate([one_of(cotangent, x), grad_came])
-    grad_own = jnp.where(valid, grad_own, jnp.zeros_like(grad_own))
-    grad_other = over_core(grad_own)
-    grad_all = jnp.concatenate([grad_own, grad_other])
+    wait_for(norm_other)
+    z_down = join(z_down, z_down_came)
+    y_down, xz_down = over_y(z_down), over_x(z_down)
+    z_up_other = join(unit_up_other, z_up_other)
+    z_up_other_came = over_z(z_up_other, 2)
     norm_all = jnp.concatenate([norm_own, norm_other])
 
     act, slope, grad_pre, pre_sums = ([None, None] for _ in range(4))
     up_sent, up_kept, up_came = ([None, None] for _ in range(3))
 
-    def hidden_grad(part):
-        up_sent[part] = run(weight_grad, 4, 4, [norm_all], [[grad_pre[part]]])
-        up_came[part] = over_y(up_sent[part])
+    def up_grad(part, first):
+        return run(weight_grad, first, 4, norm_all, [(grad_pre[part], 1024, 0)])
+
+    def down_grad(part, first, count):
+        return run(weight_grad, first, count, act[part], [(grad_all, 1024, 0)])
 
     act[0], slope[0] = run(feed_up, norm_own, norm_other, bias_up, 0, Weight(full(z_up, y_up)))
-    down_kept = run(weight_grad, 0, 8, [act[0]], [[grad_all]])
-    z_up_other = along_z(after(unit_up_other, z_down))
+    down_kept = down_grad(0, 0, 8)
+    z_up_other = join(z_up_other, z_up_other_came)
     y_up_other = over_y(z_up_other)
     up = [full(z_up, y_up), full(z_up_other, y_up_other)]
-    grad_pre[0], pre_sums[0] = run(feed_down_back, grad_own, grad_other, slope[0], Weight(down[0]))
-    hidden_grad(0)
-    up_kept[0] = run(weight_grad, 0, 4, [norm_all], [[grad_pre[0]]])
+    xy_down = over_x(y_down)
+    down = [full(z_down, y_down), full(xz_down, xy_down)]
+    grad_pre[0], pre_sums[0] = run(
+        feed_down_back, grad_own, grad_other, slope[0], Weight(down[0])
+    )
+    up_sent[0] = up_grad(0, 4)
+    up_came[0] = over_y(up_sent[0])
+    up_kept[0] = up_grad(0, 0)
     act[1], slope[1] = run(feed_up, norm_own, norm_other, bias_up, 1, Weight(up[1]))
     down_sent = [None, None]
     for i in (1, 0):
-        down_sent[i] = run(weight_grad, 4 * i, 4, [act[1]], [[grad_all]])
+        down_sent[i] = down_grad(1, 4 * i, 4)
     down_came = [over_x(sent) for sent in down_sent]
-    grad_pre[1], pre_sums[1] = run(feed_down_back, grad_own, grad_other, slope[1], Weight(down[1]))
-    hidden_grad(1)
-    back_own, back_sent = run(feed_up_back, grad_pre, Weight(*up))
+    wait_for(up_came[0])
+    grad_pre[1], pre_sums[1] = run(
+        feed_down_back, grad_own, grad_other, slope[1], Weight(down[1])
+    )
+    up_sent[1] = up_grad(1, 4)
+    up_came[1] = over_y(up_sent[1])
+    back_own, back_sent = run(
+        feed_up_back,
+        grad_pre,
+        Weight(*up),
+    )
     back_came = over_core(back_sent)
-    up_kept[1] = run(weight_grad, 0, 4, [norm_all], [[grad_pre[1]]])
+    up_kept[1] = up_grad(1, 0)
     grad_middle, branch, mixed_kept, mixed_sent, middle_sums = run(
         middle_back, back_own, back_came, middle, grad_own, vectors, out
     )
     grad_mixed = jnp.concatenate([mixed_kept, over_core(mixed_sent)])
-
-    def out_grad(i):
-        columns = lax.dynamic_slice(branch, (0, i * 512), (own_rows, 512))
-        return run(weight_grad, 0, 8, [mixed_rows], [[columns]], block_of=mixed_block)
-
-    out_sent = out_grad(1 - c)
+    out_grad = lambda which: run(
+        weight_grad, 0, 8, mixed_rows, [(branch, 512, which)], block_of=mixed_block
+    )
+    out_sent = out_grad(1)
     out_came = over_core(out_sent)
-    out_kept = out_grad(c)
+    out_kept = out_grad(0)
 
     def added(kept, came):
         return kept.astype(f32) + came.astype(f32)
@@ -1373,36 +1439,53 @@
             result = result + over_z(piece, k + 1).astype(f32)
         return result
 
+    def qkv_grad(grads, first, part):
+        rights = [(grad, 256, 0) for grad in grads]
+        return run(weight_grad, first, 4, normed, rights, extra=(out_kept, out_came, part))
+
+    def z_far(total):
+        return total[2:].astype(bf16)
+
+    def z_near(total, far_came):
+        total = added(total[:2], far_came)
+        return total[0], total[1].astype(bf16)
+
     up_x = low_sum(up_kept[1], up_came[1])
     up_x_came = over_x(up_x)
     down_y = low_sum(down_kept[4:], down_came[1])
     down_y_came = over_y(down_y)
-    out_total = jnp.swapaxes(added(out_kept, out_came).reshape(2, 4, 128, 512), 0, 1)
-    out_pieces = z_pieces(out_total)
-    wait_for(up_x, down_y, *out_pieces)
+    wait_for(up_x, down_y)
     *heads_other, sums_other = run(team_back, projected[1], grad_mixed, totals[1], 1, block)
-    other_sent = run(weight_grad, 4, 4, [normed], [heads_other])
-    other_y_came = over_y(other_sent)
-    other_kept = run(weight_grad, 0, 4, [normed], [heads_other])
-    out_y = sum_z(out_total, out_pieces)
-    out_y_sent = out_y[1].astype(bf16)
-    wait_for(out_y_sent)
+    other_y_came = over_y(qkv_grad(heads_other, 4, 1))
+    down_total = added(low_sum(after(down_kept[:4], order[0]), down_came[0]), down_y_came)
+    down_far = z_far(down_total)
+    down_far_came = over_z(down_far, 2)
+    wait_for(down_far)
+    other_kept = qkv_grad(heads_other, 0, 1)
+    up_total = added(low_sum(after(up_kept[0], order[0]), up_came[0]), up_x_came)
+    up_far = z_far(up_total)
+    up_far_came = over_z(up_far, 2)
+    wait_for(up_far)
     *heads_own, sums_own = run(team_back, projected[0], grad_mixed, totals[0], 0, block)
-    own_sent = run(weight_grad, 4, 4, [normed], [heads_own])
-    own_y_came = over_y(own_sent)
-    down_total = added(low_sum(down_kept[:4], down_came[0]), down_y_came)
-    down_pieces = z_pieces(down_total)
-    wait_for(*down_pieces)
+    other_x = low_sum(other_kept, other_y_came)
+    other_x_came = over_x(other_x)
+    wait_for(other_x)
+    own_y_came = over_y(qkv_grad(heads_own, 4, 0))
+    down_sum, down_near = z_near(down_total, down_far_came)
+    down_near_came = over_z(down_near, 1)
+    wait_for(down_near)
     first_own, first_sent = run(
         project_back, [heads_own, heads_other], Weight(qkv_own, qkv_other)
     )
     first_came = over_core(first_sent)
-    other_x = low_sum(other_kept, other_y_came)
-    up_total = added(low_sum(up_kept[0], up_came[0]), up_x_came)
-    up_pieces = z_pieces(up_total)
-    wait_for(other_x, *up_pieces)
-    own_kept = run(weight_grad, 0, 4, [normed], [heads_own])
+    up_sum, up_near = z_near(up_total, up_far_came)
+    up_near_came = over_z(up_near, 1)
+    wait_for(up_near, down_near_came)
+    own_kept = qkv_grad(heads_own, 0, 0)
     row_grad, first_sums = run(first_back, first_own, first_came, own_tokens, grad_middle, vectors)
+    qkv_total = added(own_kept, own_y_came) + other_x_came.astype(f32)
+    qkv_pieces = z_pieces(qkv_total)
+    wait_for(*qkv_pieces)
     fed_own, fed_sent = run(feed_down, act, Weight(*down))
     block_own = jnp.where(
         valid, middle + (fed_own + over_core(fed_sent).astype(f32)) + vectors[5:6], 0.0
@@ -1424,68 +1507,56 @@
         rows = flipped(jnp.stack([one_of(pieces, c), over_core(one_of(pieces, 1 - c))]), c)
         return jnp.swapaxes(rows, 0, 1)
 
-    down_sum = sum_z(down_total, down_pieces)
-    up_sum = over_team(over_pair(sum_z(up_total, up_pieces)))
+    down_sum = added(down_sum, down_near_came)
+    up_sum = over_team(over_pair(added(up_sum, up_near_came)))
     up_sum = up_sum.reshape(32, 2, 2, 8, 128).transpose(0, 3, 2, 1, 4).reshape(32, 4096)
-    out_x = added(out_y[0], over_y(out_y_sent)).reshape(2, 64, 512)
-    out_sum = added(one_of(out_x, x), over_x(one_of(out_x, 1 - x).astype(bf16)))
-    out_sum = over_team(out_sum).reshape(32, width)
-    qkv_total = added(own_kept, own_y_came) + over_x(other_x).astype(f32)
-    qkv_sum = over_team(over_pair(sum_z(qkv_total, z_pieces(qkv_total))))
-    qkv_sum = qkv_sum.reshape(32, 2, 2, 3, 4, 64)
+    qkv_sum = over_team(over_pair(sum_z(qkv_total, qkv_pieces)))
+    out_sum = qkv_sum[..., 768:].reshape(32, width)
+    qkv_sum = qkv_sum[..., :768].reshape(32, 2, 2, 3, 4, 64)
     qkv_sum = jnp.transpose(qkv_sum, (0, 1, 2, 4, 3, 5)).reshape(32, 3 * width)
-
-    places = f ^ jnp.array([0, 2, 4, 6, 1, 3, 5, 7], jnp.int32)
-
-    def sum_vectors(buffer):
-        buffer = buffer.reshape(8, 2, 2, -1)
-        at_core = jnp.moveaxis(buffer, 2, 0)
-        buffer = one_of(at_core, c) + over_core(one_of(at_core, 1 - c))
-        at_x = jnp.moveaxis(buffer, 1, 0)
-        buffer = one_of(at_x, x) + over_x(one_of(at_x, 1 - x))
-        buffer = jnp.take(buffer, places, axis=0)
-        buffer = buffer[:4] + over_y(buffer[4:])
-        total = buffer[0]
-        for k in (1, 2, 3):
-            total = total + over_z(buffer[k], k)
-        return total
 
     at_member = jnp.arange(2) == c
     up_vector = flipped(jnp.sum(jnp.stack(pre_sums), axis=1).reshape(2, 8, 128), x)
     up_vector = jnp.where(
         at_member[None, None, :, None], jnp.swapaxes(up_vector, 0, 1)[:, :, None], 0.0
     ).reshape(32, 128)
-    middle_sums = jnp.sum(middle_sums, axis=1)
-    early = sum_vectors(
-        jnp.concatenate([middle_sums[i].reshape(32, 32) for i in range(4)] + [up_vector], axis=1)
-    )
+    middle_sums = jnp.sum(middle_sums, axis=1).reshape(4, 32, 32)
+    first_sums = jnp.sum(first_sums, axis=1).reshape(2, 32, 32)
     head_sums = flipped(jnp.sum(jnp.stack([sums_own, sums_other]), axis=3), x)
 
     def head_vector(kind):
         return jnp.where(at_member[:, None], head_sums[:, :, kind].reshape(1, 512), 0.0).reshape(32, 32)
 
-    first_sums = jnp.sum(first_sums, axis=1)
-    late = sum_vectors(
-        jnp.concatenate(
-            [first_sums[i].reshape(32, 32) for i in range(2)] + [head_vector(0), head_vector(1)],
-            axis=1,
-        )
-    )
+    totals = jnp.concatenate(
+        [middle_sums[i] for i in range(4)]
+        + [up_vector, head_vector(0), head_vector(1), first_sums[0], first_sums[1]],
+        axis=1,
+    )
+    totals = after(totals, *qkv_pieces)
+
+    def summed(value):
+        for axis, bit in (("seq", 1), ("seq", 2), ("fsdp", 1), ("fsdp", 2), ("fsdp", 4)):
+            value = value + exchange(value, axis, bit)
+        return value
+
+    totals = lax.cond(length > 0, summed, lambda v: v, totals)
+    totals = one_of(totals, f * 4 + s)
+    piece = lambda i: totals[i * 32 : (i + 1) * 32]
     return (
         block_out,
         tokens_grad,
-        late[:32],
-        late[32:64],
+        piece(10),
+        piece(11),
         qkv_sum,
-        jnp.stack([late[64:96], late[96:]]),
+        jnp.stack([piece(8), piece(9)]),
         out_sum,
-        early[64:96],
-        early[:32],
-        early[32:64],
+        piece(2),
+        piece(0),
+        piece(1),
         up_sum,
-        early[128:],
+        totals[128:256],
         down_sum,
-        early[96:128],
+        piece(3),
     )
 
 

time: 518 us -> 449 us (0.87)
  waiting for transfers between devices: 153 us -> 124 us
  starting transfers between devices: 83.6 us -> 56.6 us
  local copies, waits for them, and re-layouts: 64 us -> 49.3 us
    ppermute x80 -> x59, waiting for transfers between devices: 153 us -> 124 us  [exchange(): lax.ppermute(value, axis, [(i, i ^ bit) for i in range(lax.axis_size(axis...]
    ppermute x80 -> x59, starting transfers between devices: 83.6 us -> 56.6 us  [exchange(): lax.ppermute(value, axis, [(i, i ^ bit) for i in range(lax.axis_size(axis...]
    unnamed x211 -> x214, local copies, waits for them, and re-layouts: 35.9 us -> 21.7 us
    add x3 -> x6, other arithmetic: 1.68 us -> 7.16 us  [added(): return kept.astype(f32) + came.astype(f32)]
    pallas_call x28 -> x29, Pallas kernels: 116 us -> 111 us  [grid_call(): pl.pallas_call(kernel, name=name, grid_spec=pltpu.PrefetchScalarGridSpec(...]
  transfers between devices with their start and end apart: 80 -> 59, of which waited for: 23 -> 29; matrix products, arithmetic and copies ran while one was open for 11% -> 14% of each run, Pallas kernels for 30% -> 38%
where the time goes in v2:
time: 449 us; the launch traced here: 441 us
  Pallas kernels  168 us (37%)
  waiting for transfers between devices  124 us (28%)
  starting transfers between devices  56.6 us (13%)
  local copies, waits for them, and re-layouts  49.3 us (11%)
  other arithmetic  39.9 us (9%)
    ppermute x59, waiting for transfers between devices, exchange(): lax.ppermute(value, axis, [(i, i ^ bit) for i in range(lax.axis_size(axis...  124 us
    pallas_call x29, Pallas kernels, grid_call(): pl.pallas_call(kernel, name=name, grid_spec=pltpu.PrefetchScalarGridSpec(...  111 us
    ppermute x59, starting transfers between devices, exchange(): lax.ppermute(value, axis, [(i, i ^ bit) for i in range(lax.axis_size(axis...  56.6 us
    pallas_call x2, Pallas kernels, team_back(): pl.pallas_call(partial(team_back_kernel, part), name='team_back', grid_sp...  28.7 us
    unnamed x214, local copies, waits for them, and re-layouts  21.7 us
    pallas_call x2, Pallas kernels, team_attend(): pl.pallas_call(partial(team_attend_kernel, part), name='team_attend', gri...  21.7 us
  transfers between devices with their start and end apart: 59, of which 29 were waited for; matrix products, arithmetic and copies ran while one was open for 14% of the time, Pallas kernels for 38%

profile of v2, /device:TPU:0, one launch (start us, length us, event | category | flops | bytes accessed | tf_op | source)
XLA Modules:
  0.0 441.1 jit_solution(18244416180433409299)
XLA Ops:
  31.4 8.1 %collective-permute-done.20.second_ref = bf16[2,144,768]{2,1,0:T(8,128)(2,1)S(1)} collective-permute-done((bf16[2,144,768]{2,1,0:T(8,128)(2,1)S(1)}, bf16[2,144,768]{2,1,0:T(8,128)(2,1)S(1)}, u32[]{:S(2)}, u32[]{:S(2)}) %collective-permute-start.20) | collective-permute-done | bytes 442400 | tf_op jit(solution)/shard_map/ppermute | solution.py:151
  42.8 3.9 collective-permute-start.23
  69.2 4.5 %project.2.q_ref.k_ref.v_ref = bf16[1024,768]{1,0:T(8,128)(2,1)S(1)} custom-call(s32[3]{0:T(128)S(1)} %pad_add_fusion.order, bf16[1024,1024]{1,0:T(8,128)(2,1)S(1)} %first_norm.1.lhs_ref.left_ref, f32[2,768]{1,0:T(2,128)S(1)} %get-tuple-element.262.bias_ref, bf16[4,144,768]{2,1,0:T(8,128)(2,1)} %joined.11.mine_ref.rest_0_.rest_6_, ...), custom_call_target="tpu_custom_call" | custom-call | flops 10000000000 | bytes 20000000 | tf_op jit(solution)/shard_map/project/pallas_call | solution.py:551
  73.7 10.8 %team_attend.2 = (bf16[1024,256]{1,0:T(8,128)(2,1)S(1)}, f32[2,8,1024]{2,1,0:T(8,128)S(1)}) custom-call(s32[3]{0:T(128)S(1)} %pad_add_fusion.order, bf16[1024,768]{1,0:T(8,128)(2,1)S(1)} %project.2.q_ref.k_ref.v_ref, bf16[1024,768]{1,0:T(8,128)(2,1)S(1)} %project.2.q_ref.k_ref.v_ref, bf16[1024,768]{1,0:T(8,128)(2,1)S(1)} %project.2.q_ref.k_ref.v_ref), custom_call_target="tpu_custom_call" | custom-call | flops 10000000000 | bytes 20000000 | tf_op jit(solution)/shard_map/team_attend/pallas_call | solution.py:1058
  91.9 4.0 conditional.17
  97.0 5.3 %collective-permute-done.29.rest_1_.rest_9_ = bf16[4,144,768]{2,1,0:T(8,128)(2,1)} collective-permute-done((bf16[4,144,768]{2,1,0:T(8,128)(2,1)}, bf16[4,144,768]{2,1,0:T(8,128)(2,1)}, u32[]{:S(2)}, u32[]{:S(2)}) %collective-permute-start.29) | collective-permute-done | bytes 884768 | tf_op jit(solution)/shard_map/ppermute | solution.py:151
  103.9 4.4 project.3.q_ref.k_ref.v_ref
  108.4 10.8 %team_attend.3 = (bf16[1024,256]{1,0:T(8,128)(2,1)S(1)}, f32[2,8,1024]{2,1,0:T(8,128)S(1)}) custom-call(s32[3]{0:T(128)S(1)} %pad_add_fusion.order, bf16[1024,768]{1,0:T(8,128)(2,1)S(1)} %project.3.q_ref.k_ref.v_ref, bf16[1024,768]{1,0:T(8,128)(2,1)S(1)} %project.3.q_ref.k_ref.v_ref, bf16[1024,768]{1,0:T(8,128)(2,1)S(1)} %project.3.q_ref.k_ref.v_ref), custom_call_target="tpu_custom_call" | custom-call | flops 10000000000 | bytes 20000000 | tf_op jit(solution)/shard_map/team_attend/pallas_call | solution.py:1058
  139.8 8.2 %feed_up.2 = (bf16[1024,1024]{1,0:T(8,128)(2,1)S(1)}, bf16[1024,1024]{1,0:T(8,128)(2,1)S(1)}) custom-call(s32[3]{0:T(128)S(1)} %pad_add_fusion.order, bf16[512,1024]{1,0:T(8,128)(2,1)S(1)} %copy-done.76, bf16[512,1024]{1,0:T(8,128)(2,1)} %get-tuple-element.398.other_ref, f32[2,1024]{1,0:T(2,128)S(1)} %get-tuple-element.286.bias_ref, ...), custom_call_target="tpu_custom_call" | custom-call | flops 10000000000 | bytes 20000000 | tf_op jit(solution)/shard_map/feed_up/pallas_call | solution.py:551
  148.0 3.6 weight_grad.13
  151.6 8.6 %collective-permute-done.34.second_ref = bf16[2,128,1024]{2,1,0:T(8,128)(2,1)S(1)} collective-permute-done((bf16[2,128,1024]{2,1,0:T(8,128)(2,1)S(1)}, bf16[2,128,1024]{2,1,0:T(8,128)(2,1)S(1)}, u32[]{:S(2)}, u32[]{:S(2)}) %collective-permute-start.34) | collective-permute-done | bytes 524320 | tf_op jit(solution)/shard_map/ppermute | solution.py:151
  161.7 5.5 %feed_down_back.2 = (bf16[1024,1024]{1,0:T(8,128)(2,1)S(1)}, f32[8,1024]{1,0:T(8,128)S(1)}) custom-call(s32[3]{0:T(128)S(1)} %pad_add_fusion.order, bf16[512,1024]{1,0:T(8,128)(2,1)S(1)} %copy-done.71, bf16[512,1024]{1,0:T(8,128)(2,1)} %get-tuple-element.395.other_ref, bf16[1024,1024]{1,0:T(8,128)(2,1)S(1)} %get-tuple-element.292.slope_ref, ...), custom_call_target="tpu_custom_call" | custom-call | flops 10000000000 | bytes 20000000 | tf_op jit(solution)/shard_map/feed_down_back/pallas_call | solution.py:551
  173.2 13.2 %collective-permute-done.36.rest_1_.rest_5_ = bf16[4,128,1024]{2,1,0:T(8,128)(2,1)S(1)} collective-permute-done((bf16[4,128,1024]{2,1,0:T(8,128)(2,1)S(1)}, bf16[4,128,1024]{2,1,0:T(8,128)(2,1)S(1)}, u32[]{:S(2)}, u32[]{:S(2)}) %collective-permute-start.36) | collective-permute-done | bytes 1048608 | tf_op jit(solution)/shard_map/ppermute | solution.py:151
  186.5 6.6 %feed_up.3 = (bf16[1024,1024]{1,0:T(8,128)(2,1)S(1)}, bf16[1024,1024]{1,0:T(8,128)(2,1)S(1)}) custom-call(s32[3]{0:T(128)S(1)} %pad_add_fusion.order, bf16[512,1024]{1,0:T(8,128)(2,1)S(1)} %copy-done.76, bf16[512,1024]{1,0:T(8,128)(2,1)} %get-tuple-element.398.other_ref, f32[2,1024]{1,0:T(2,128)S(1)} %get-tuple-element.286.bias_ref, ...), custom_call_target="tpu_custom_call" | custom-call | flops 10000000000 | bytes 20000000 | tf_op jit(solution)/shard_map/feed_up/pallas_call | solution.py:551
  200.9 6.3 %collective-permute-done.37 = bf16[4,128,1024]{2,1,0:T(8,128)(2,1)S(1)} collective-permute-done((bf16[4,128,1024]{2,1,0:T(8,128)(2,1)S(1)}, bf16[4,128,1024]{2,1,0:T(8,128)(2,1)S(1)}, u32[]{:S(2)}, u32[]{:S(2)}) %collective-permute-start.37) | collective-permute-done | bytes 1048608 | tf_op jit(solution)/shard_map/ppermute | solution.py:151
  207.2 5.9 %feed_down_back.3 = (bf16[1024,1024]{1,0:T(8,128)(2,1)S(1)}, f32[8,1024]{1,0:T(8,128)S(1)}) custom-call(s32[3]{0:T(128)S(1)} %pad_add_fusion.order, bf16[512,1024]{1,0:T(8,128)(2,1)S(1)} %copy-done.71, bf16[512,1024]{1,0:T(8,128)(2,1)} %get-tuple-element.395.other_ref, bf16[1024,1024]{1,0:T(8,128)(2,1)S(1)} %get-tuple-element.302.slope_ref, ...), custom_call_target="tpu_custom_call" | custom-call | flops 10000000000 | bytes 20000000 | tf_op jit(solution)/shard_map/feed_down_back/pallas_call | solution.py:551
  217.4 9.8 %feed_up_back.1 = (f32[512,1024]{1,0:T(8,128)S(1)}, bf16[512,1024]{1,0:T(8,128)(2,1)}) custom-call(s32[3]{0:T(128)S(1)} %pad_add_fusion.order, bf16[1024,1024]{1,0:T(8,128)(2,1)S(1)} %get-tuple-element.293.rest_0_, bf16[1024,1024]{1,0:T(8,128)(2,1)S(1)} %get-tuple-element.303.rest_0_.rest_1_, bf16[4,128,1024]{2,1,0:T(8,128)(2,1)} %joined.15.rest_0_.rest_2_, ...), custom_call_target="tpu_custom_call" | custom-call | flops 10000000000 | bytes 20000000 | tf_op jit(solution)/shard_map/feed_up_back/pallas_call | solution.py:551
  228.6 3.9 conditional.20
  239.4 5.2 %middle_back.1 = (f32[512,1024]{1,0:T(8,128)S(1)}, bf16[512,1024]{1,0:T(8,128)(2,1)S(1)}, bf16[512,512]{1,0:T(8,128)(2,1)S(1)}, bf16[512,512]{1,0:T(8,128)(2,1)}, f32[4,8,1024]{2,1,0:T(8,128)S(1)}) custom-call(s32[3]{0:T(128)S(1)} %pad_add_fusion.order, f32[512,1024]{1,0:T(8,128)S(1)} %copy-done.45, bf16[512,1024]{1,0:T(8,128)(2,1)S(1)} %copy-done.105, ...), custom_call_target="tpu_custom_call" | custom-call | flops 10000000000 | bytes 20000000 | tf_op jit(solution)/shard_map/middle_back/pallas_call | solution.py:551
  264.0 14.3 %team_back.2 = (bf16[1024,256]{1,0:T(8,128)(2,1)S(1)}, bf16[1024,256]{1,0:T(8,128)(2,1)S(1)}, bf16[1024,256]{1,0:T(8,128)(2,1)S(1)}, f32[2,2,8,128]{3,2,1,0:T(8,128)S(1)}) custom-call(s32[3]{0:T(128)S(1)} %pad_add_fusion.order, bf16[1024,768]{1,0:T(8,128)(2,1)S(1)} %copy-done.61, bf16[1024,768]{1,0:T(8,128)(2,1)S(1)} %copy-done.61, ...), custom_call_target="tpu_custom_call" | custom-call | flops 10000000000 | bytes 20000000 | tf_op jit(solution)/shard_map/team_back/pallas_call | solution.py:1129
  282.6 4.1 collective-permute-done.43
  296.1 14.4 %team_back.3 = (bf16[1024,256]{1,0:T(8,128)(2,1)S(1)}, bf16[1024,256]{1,0:T(8,128)(2,1)S(1)}, bf16[1024,256]{1,0:T(8,128)(2,1)S(1)}, f32[2,2,8,128]{3,2,1,0:T(8,128)S(1)}) custom-call(s32[3]{0:T(128)S(1)} %pad_add_fusion.order, bf16[1024,768]{1,0:T(8,128)(2,1)S(1)} %copy-done.59, bf16[1024,768]{1,0:T(8,128)(2,1)S(1)} %copy-done.59, ...), custom_call_target="tpu_custom_call" | custom-call | flops 10000000000 | bytes 20000000 | tf_op jit(solution)/shard_map/team_back/pallas_call | solution.py:1129
  316.6 10.4 %collective-permute-done.46 = bf16[2,128,1024]{2,1,0:T(8,128)(2,1)S(1)} collective-permute-done((bf16[2,128,1024]{2,1,0:T(8,128)(2,1)S(1)}, bf16[2,128,1024]{2,1,0:T(8,128)(2,1)S(1)}, u32[]{:S(2)}, u32[]{:S(2)}) %collective-permute-start.46) | collective-permute-done | bytes 524320 | tf_op jit(solution)/shard_map/ppermute | solution.py:151
  328.0 7.9 %project_back.1 = (f32[512,1024]{1,0:T(8,128)S(1)}, bf16[512,1024]{1,0:T(8,128)(2,1)}) custom-call(s32[3]{0:T(128)S(1)} %pad_add_fusion.order, bf16[1024,256]{1,0:T(8,128)(2,1)S(1)} %get-tuple-element.330.rest_0_, bf16[1024,256]{1,0:T(8,128)(2,1)S(1)} %get-tuple-element.333.rest_1_, bf16[1024,256]{1,0:T(8,128)(2,1)S(1)} %get-tuple-element.334.rest_2_, ...), custom_call_target="tpu_custom_call" | custom-call | flops 10000000000 | bytes 20000000 | tf_op jit(solution)/shard_map/project_back/pallas_call | solution.py:551
  337.5 3.8 conditional.23
  359.0 3.6 fusion.12
  364.0 24.8 %conditional.25 = (f32[32,384]{1,0:T(8,128)S(1)}) conditional(s32[]{:T(128)} %convert_element_type.137, f32[32,384]{1,0:T(8,128)S(1)} %concatenate.51, f32[32,384]{1,0:T(8,128)S(1)} %concatenate.51), branch_computations={%region_26.27_spmd, %region_27.28_spmd} | conditional | flops 61440 | bytes 1720528 | solution.py:1542
  366.6 8.9 %collective-permute-done.12 = f32[32,384]{1,0:T(8,128)S(1)} collective-permute-done((f32[32,384]{1,0:T(8,128)S(1)}, f32[32,384]{1,0:T(8,128)S(1)}, u32[]{:S(2)}, u32[]{:S(2)}) %collective-permute-start.12) | collective-permute-done | bytes 49184 | tf_op jit(solution)/shard_map/cond/branch_1_fun/ppermute | solution.py:151
  383.9 5.0 %collective-permute-done.15 = f32[32,384]{1,0:T(8,128)S(1)} collective-permute-done((f32[32,384]{1,0:T(8,128)S(1)}, f32[32,384]{1,0:T(8,128)S(1)}, u32[]{:S(2)}, u32[]{:S(2)}) %collective-permute-start.15) | collective-permute-done | bytes 49184 | tf_op jit(solution)/shard_map/cond/branch_1_fun/ppermute | solution.py:151
  393.3 6.8 %feed_down.1 = (f32[512,1024]{1,0:T(8,128)S(1)}, bf16[512,1024]{1,0:T(8,128)(2,1)}) custom-call(s32[3]{0:T(128)S(1)} %pad_add_fusion.order, bf16[1024,1024]{1,0:T(8,128)(2,1)S(1)} %copy-done.47, bf16[1024,1024]{1,0:T(8,128)(2,1)S(1)} %copy-done.49, bf16[4,128,1024]{2,1,0:T(8,128)(2,1)S(1)} %copy-done.27, bf16[4,128,1024]{2,1,0:T(8,128)(2,1)S(1)} %copy-done.29, ...), custom_call_target="tpu_custom_call" | custom-call | flops 10000000000 | bytes 20000000 | tf_op jit(solution)/shard_map/feed_down/pallas_call | solution.py:551
  401.5 3.8 conditional.24
  425.6 6.9 %collective-permute-done.56 = f32[64,1024]{1,0:T(8,128)S(1)} collective-permute-done((f32[64,1024]{1,0:T(8,128)S(1)}, f32[64,1024]{1,0:T(8,128)S(1)}, u32[]{:S(2)}, u32[]{:S(2)}) %collective-permute-start.56) | collective-permute-done | bytes 262176 | tf_op jit(solution)/shard_map/ppermute | solution.py:151
  (469 shorter events, 255.5 us)
Async XLA Ops:
  3.1 24.3 %collective-permute-start.19 = (bf16[256,1024]{1,0:T(8,128)(2,1)}, bf16[256,1024]{1,0:T(8,128)(2,1)}, u32[]{:S(2)}, u32[]{:S(2)}) collective-permute-start(bf16[256,1024]{1,0:T(8,128)(2,1)} %get-tuple-element.371), channel_id=1, source_target_pairs={{0,2},{1,3},{2,0},{3,1},{4,6},{5,7},{6,4},{7,5},{8,10},{9,11},{10,... | collective-permute-start | bytes 1572872 | tf_op jit(solution)/shard_map/ppermute | solution.py:151
  18.3 21.3 %collective-permute-start.20 = (bf16[2,144,768]{2,1,0:T(8,128)(2,1)S(1)}, bf16[2,144,768]{2,1,0:T(8,128)(2,1)S(1)}, u32[]{:S(2)}, u32[]{:S(2)}) collective-permute-start(bf16[2,144,768]{2,1,0:T(8,128)(2,1)S(1)} %joined.10.first_ref), channel_id=1, source_target_pairs={{0,16},{4,20},{8,24},{12,28},{16,0},{20,4},{24,8},{28,12},{1,17},{... | collective-permute-start | bytes 1327112 | tf_op jit(solution)/shard_map/ppermute | solution.py:151
  27.4 19.2 %collective-permute-start.22 = (bf16[256,1024]{1,0:T(8,128)(2,1)S(1)}, bf16[256,1024]{1,0:T(8,128)(2,1)}, u32[]{:S(2)}, u32[]{:S(2)}) collective-permute-start(bf16[256,1024]{1,0:T(8,128)(2,1)S(1)} %dynamic-slice_bitcast_fusion.2), channel_id=1, source_target_pairs={{0,2},{1,3},{2,0},{3,1},{4,6},{5,7},{6,4},{7,5},{8,10},{9,11},{10,... | collective-permute-start | bytes 1572872 | tf_op jit(solution)/shard_map/ppermute | solution.py:151
  40.7 23.0 %collective-permute-start.25 = (bf16[4,144,768]{2,1,0:T(8,128)(2,1)}, bf16[4,144,768]{2,1,0:T(8,128)(2,1)}, u32[]{:S(2)}, u32[]{:S(2)}) collective-permute-start(bf16[4,144,768]{2,1,0:T(8,128)(2,1)} %joined.11.mine_ref.rest_0_.rest_6_), channel_id=1, source_target_pairs={{0,4},{4,0},{8,12},{12,8},{16,20},{20,16},{24,28},{28,24},{1,5},{5... | collective-permute-start | bytes 2654216 | tf_op jit(solution)/shard_map/ppermute | solution.py:151
  42.2 54.8 %collective-permute-start.28 = (bf16[4,144,768]{2,1,0:T(8,128)(2,1)}, bf16[4,144,768]{2,1,0:T(8,128)(2,1)}, u32[]{:S(2)}, u32[]{:S(2)}) collective-permute-start(bf16[4,144,768]{2,1,0:T(8,128)(2,1)} %joined.11.mine_ref.rest_0_.rest_6_), channel_id=1, source_target_pairs={{0,2},{1,3},{2,0},{3,1},{4,6},{5,7},{6,4},{7,5},{8,10},{9,11},{10,... | collective-permute-start | bytes 2654216 | tf_op jit(solution)/shard_map/ppermute | solution.py:151
  56.0 34.7 %collective-permute-start.30 = (bf16[4,128,512]{2,1,0:T(8,128)(2,1)S(1)}, bf16[4,128,512]{2,1,0:T(8,128)(2,1)S(1)}, u32[]{:S(2)}, u32[]{:S(2)}) collective-permute-start(bf16[4,128,512]{2,1,0:T(8,128)(2,1)S(1)} %joined.14.rest_0_), channel_id=1, source_target_pairs={{0,4},{4,0},{8,12},{12,8},{16,20},{20,16},{24,28},{28,24},{1,5},{5... | collective-permute-start | bytes 1572872 | tf_op jit(solution)/shard_map/ppermute | solution.py:151
  56.6 28.8 %collective-permute-start.26 = (bf16[2,128,1024]{2,1,0:T(8,128)(2,1)S(1)}, bf16[2,128,1024]{2,1,0:T(8,128)(2,1)S(1)}, u32[]{:S(2)}, u32[]{:S(2)}) collective-permute-start(bf16[2,128,1024]{2,1,0:T(8,128)(2,1)S(1)} %joined.13.first_ref), channel_id=1, source_target_pairs={{0,16},{4,20},{8,24},{12,28},{16,0},{20,4},{24,8},{28,12},{1,17},{... | collective-permute-start | bytes 1572872 | tf_op jit(solution)/shard_map/ppermute | solution.py:151
  58.5 27.9 %collective-permute-start.27 = (bf16[1,128,1024]{2,1,0:T(8,128)(2,1)S(1)}, bf16[1,128,1024]{2,1,0:T(8,128)(2,1)S(1)}, u32[]{:S(2)}, u32[]{:S(2)}) collective-permute-start(bf16[1,128,1024]{2,1,0:T(8,128)(2,1)S(1)} %copy-done.39), channel_id=1, source_target_pairs={{0,8},{4,12},{8,0},{12,4},{16,24},{20,28},{24,16},{28,20},{1,9},{5... | collective-permute-start | bytes 786440 | tf_op jit(solution)/shard_map/ppermute | solution.py:151
  86.5 45.1 %collective-permute-start.31 = (bf16[2,128,1024]{2,1,0:T(8,128)(2,1)S(1)}, bf16[2,128,1024]{2,1,0:T(8,128)(2,1)}, u32[]{:S(2)}, u32[]{:S(2)}) collective-permute-start(bf16[2,128,1024]{2,1,0:T(8,128)(2,1)S(1)} %joined.16.first_ref), channel_id=1, source_target_pairs={{0,16},{4,20},{8,24},{12,28},{16,0},{20,4},{24,8},{28,12},{1,17},{... | collective-permute-start | bytes 1572872 | tf_op jit(solution)/shard_map/ppermute | solution.py:151
  89.3 50.4 %collective-permute-start.33 = (bf16[4,128,1024]{2,1,0:T(8,128)(2,1)}, bf16[4,128,1024]{2,1,0:T(8,128)(2,1)}, u32[]{:S(2)}, u32[]{:S(2)}) collective-permute-start(bf16[4,128,1024]{2,1,0:T(8,128)(2,1)} %joined.15.rest_0_.rest_2_), channel_id=1, source_target_pairs={{0,4},{4,0},{8,12},{12,8},{16,20},{20,16},{24,28},{28,24},{1,5},{5... | collective-permute-start | bytes 3145736 | tf_op jit(solution)/shard_map/ppermute | solution.py:151
  95.9 36.8 %collective-permute-start.32 = (bf16[1,128,1024]{2,1,0:T(8,128)(2,1)}, bf16[1,128,1024]{2,1,0:T(8,128)(2,1)}, u32[]{:S(2)}, u32[]{:S(2)}) collective-permute-start(bf16[1,128,1024]{2,1,0:T(8,128)(2,1)} %copy-done.36), channel_id=1, source_target_pairs={{0,8},{4,12},{8,0},{12,4},{16,24},{20,28},{24,16},{28,20},{1,9},{5... | collective-permute-start | bytes 786440 | tf_op jit(solution)/shard_map/ppermute | solution.py:151
  134.1 26.2 %collective-permute-start.34 = (bf16[2,128,1024]{2,1,0:T(8,128)(2,1)S(1)}, bf16[2,128,1024]{2,1,0:T(8,128)(2,1)S(1)}, u32[]{:S(2)}, u32[]{:S(2)}) collective-permute-start(bf16[2,128,1024]{2,1,0:T(8,128)(2,1)S(1)} %joined.18.first_ref), channel_id=1, source_target_pairs={{0,16},{4,20},{8,24},{12,28},{16,0},{20,4},{24,8},{28,12},{1,17},{... | collective-permute-start | bytes 1572872 | tf_op jit(solution)/shard_map/ppermute | solution.py:151
  136.3 25.4 %collective-permute-start.35 = (bf16[4,128,1024]{2,1,0:T(8,128)(2,1)S(1)}, bf16[4,128,1024]{2,1,0:T(8,128)(2,1)S(1)}, u32[]{:S(2)}, u32[]{:S(2)}) collective-permute-start(bf16[4,128,1024]{2,1,0:T(8,128)(2,1)S(1)} %joined.17.rest_0_.rest_2_), channel_id=1, source_target_pairs={{0,4},{4,0},{8,12},{12,8},{16,20},{20,16},{24,28},{28,24},{1,5},{5... | collective-permute-start | bytes 3145736 | tf_op jit(solution)/shard_map/ppermute | solution.py:151
  137.8 69.4 %collective-permute-start.38 = (bf16[4,128,1024]{2,1,0:T(8,128)(2,1)S(1)}, bf16[4,128,1024]{2,1,0:T(8,128)(2,1)S(1)}, u32[]{:S(2)}, u32[]{:S(2)}) collective-permute-start(bf16[4,128,1024]{2,1,0:T(8,128)(2,1)S(1)} %joined.17.rest_0_.rest_2_), channel_id=1, source_target_pairs={{0,2},{1,3},{2,0},{3,1},{4,6},{5,7},{6,4},{7,5},{8,10},{9,11},{10,... | collective-permute-start | bytes 3145736 | tf_op jit(solution)/shard_map/ppermute | solution.py:151
  160.3 26.2 %collective-permute-start.36 = (bf16[4,128,1024]{2,1,0:T(8,128)(2,1)S(1)}, bf16[4,128,1024]{2,1,0:T(8,128)(2,1)S(1)}, u32[]{:S(2)}, u32[]{:S(2)}) collective-permute-start(bf16[4,128,1024]{2,1,0:T(8,128)(2,1)S(1)} %joined.19.rest_0_.rest_4_), channel_id=1, source_target_pairs={{0,4},{4,0},{8,12},{12,8},{16,20},{20,16},{24,28},{28,24},{1,5},{5... | collective-permute-start | bytes 3145736 | tf_op jit(solution)/shard_map/ppermute | solution.py:151
  169.3 37.9 %collective-permute-start.37 = (bf16[4,128,1024]{2,1,0:T(8,128)(2,1)S(1)}, bf16[4,128,1024]{2,1,0:T(8,128)(2,1)S(1)}, u32[]{:S(2)}, u32[]{:S(2)}) collective-permute-start(bf16[4,128,1024]{2,1,0:T(8,128)(2,1)S(1)} %weight_grad.14), channel_id=1, source_target_pairs={{0,4},{4,0},{8,12},{12,8},{16,20},{20,16},{24,28},{28,24},{1,5},{5... | collective-permute-start | bytes 3145736 | tf_op jit(solution)/shard_map/ppermute | solution.py:151
  172.5 34.7 %collective-permute-start.39 = (bf16[4,128,1024]{2,1,0:T(8,128)(2,1)S(1)}, bf16[4,128,1024]{2,1,0:T(8,128)(2,1)S(1)}, u32[]{:S(2)}, u32[]{:S(2)}) collective-permute-start(bf16[4,128,1024]{2,1,0:T(8,128)(2,1)S(1)} %collective-permute-done.35.rest_1_.rest_3_), channel_id=1, source_target_pairs={{0,2},{1,3},{2,0},{3,1},{4,6},{5,7},{6,4},{7,5},{8,10},{9,11},{10,... | collective-permute-start | bytes 3145736 | tf_op jit(solution)/shard_map/ppermute | solution.py:151
  196.0 63.0 %collective-permute-start.41 = (bf16[4,128,1024]{2,1,0:T(8,128)(2,1)}, bf16[4,128,1024]{2,1,0:T(8,128)(2,1)}, u32[]{:S(2)}, u32[]{:S(2)}) collective-permute-start(bf16[4,128,1024]{2,1,0:T(8,128)(2,1)} %weight_grad.16), channel_id=1, source_target_pairs={{0,2},{1,3},{2,0},{3,1},{4,6},{5,7},{6,4},{7,5},{8,10},{9,11},{10,... | collective-permute-start | bytes 3145736 | tf_op jit(solution)/shard_map/ppermute | solution.py:151
  199.9 82.7 %collective-permute-start.42 = (bf16[4,128,1024]{2,1,0:T(8,128)(2,1)}, bf16[4,128,1024]{2,1,0:T(8,128)(2,1)}, u32[]{:S(2)}, u32[]{:S(2)}) collective-permute-start(bf16[4,128,1024]{2,1,0:T(8,128)(2,1)} %weight_grad.17), channel_id=1, source_target_pairs={{0,2},{1,3},{2,0},{3,1},{4,6},{5,7},{6,4},{7,5},{8,10},{9,11},{10,... | collective-permute-start | bytes 3145736 | tf_op jit(solution)/shard_map/ppermute | solution.py:151
  216.1 45.3 %collective-permute-start.40 = (bf16[4,128,1024]{2,1,0:T(8,128)(2,1)}, bf16[4,128,1024]{2,1,0:T(8,128)(2,1)}, u32[]{:S(2)}, u32[]{:S(2)}) collective-permute-start(bf16[4,128,1024]{2,1,0:T(8,128)(2,1)} %weight_grad.18), channel_id=1, source_target_pairs={{0,4},{4,0},{8,12},{12,8},{16,20},{20,16},{24,28},{28,24},{1,5},{5... | collective-permute-start | bytes 3145736 | tf_op jit(solution)/shard_map/ppermute | solution.py:151
  260.6 26.1 %collective-permute-start.43 = (bf16[4,128,1024]{2,1,0:T(8,128)(2,1)S(1)}, bf16[4,128,1024]{2,1,0:T(8,128)(2,1)S(1)}, u32[]{:S(2)}, u32[]{:S(2)}) collective-permute-start(bf16[4,128,1024]{2,1,0:T(8,128)(2,1)S(1)} %add_convert_fusion.3), channel_id=1, source_target_pairs={{0,4},{4,0},{8,12},{12,8},{16,20},{20,16},{24,28},{28,24},{1,5},{5... | collective-permute-start | bytes 3145736 | tf_op jit(solution)/shard_map/ppermute | solution.py:151
  263.0 28.6 %collective-permute-start.44 = (bf16[4,128,1024]{2,1,0:T(8,128)(2,1)S(1)}, bf16[4,128,1024]{2,1,0:T(8,128)(2,1)S(1)}, u32[]{:S(2)}, u32[]{:S(2)}) collective-permute-start(bf16[4,128,1024]{2,1,0:T(8,128)(2,1)S(1)} %add_convert_fusion.4), channel_id=1, source_target_pairs={{0,2},{1,3},{2,0},{3,1},{4,6},{5,7},{6,4},{7,5},{8,10},{9,11},{10,... | collective-permute-start | bytes 3145736 | tf_op jit(solution)/shard_map/ppermute | solution.py:151
  281.2 29.4 %collective-permute-start.45 = (bf16[4,128,1024]{2,1,0:T(8,128)(2,1)S(1)}, bf16[4,128,1024]{2,1,0:T(8,128)(2,1)S(1)}, u32[]{:S(2)}, u32[]{:S(2)}) collective-permute-start(bf16[4,128,1024]{2,1,0:T(8,128)(2,1)S(1)} %weight_grad.22), channel_id=1, source_target_pairs={{0,4},{4,0},{8,12},{12,8},{16,20},{20,16},{24,28},{28,24},{1,5},{5... | collective-permute-start | bytes 3145736 | tf_op jit(solution)/shard_map/ppermute | solution.py:151
  288.6 38.4 %collective-permute-start.46 = (bf16[2,128,1024]{2,1,0:T(8,128)(2,1)S(1)}, bf16[2,128,1024]{2,1,0:T(8,128)(2,1)S(1)}, u32[]{:S(2)}, u32[]{:S(2)}) collective-permute-start(bf16[2,128,1024]{2,1,0:T(8,128)(2,1)S(1)} %slice.275), channel_id=1, source_target_pairs={{0,16},{4,20},{8,24},{12,28},{16,0},{20,4},{24,8},{28,12},{1,17},{... | collective-permute-start | bytes 1572872 | tf_op jit(solution)/shard_map/ppermute | solution.py:151
  293.2 50.2 %collective-permute-start.47 = (bf16[2,128,1024]{2,1,0:T(8,128)(2,1)}, bf16[2,128,1024]{2,1,0:T(8,128)(2,1)}, u32[]{:S(2)}, u32[]{:S(2)}) collective-permute-start(bf16[2,128,1024]{2,1,0:T(8,128)(2,1)} %slice.274), channel_id=1, source_target_pairs={{0,16},{4,20},{8,24},{12,28},{16,0},{20,4},{24,8},{28,12},{1,17},{... | collective-permute-start | bytes 1572872 | tf_op jit(solution)/shard_map/ppermute | solution.py:151
  314.9 44.1 %collective-permute-start.49 = (bf16[4,128,1024]{2,1,0:T(8,128)(2,1)S(1)}, bf16[4,128,1024]{2,1,0:T(8,128)(2,1)}, u32[]{:S(2)}, u32[]{:S(2)}) collective-permute-start(bf16[4,128,1024]{2,1,0:T(8,128)(2,1)S(1)} %weight_grad.24), channel_id=1, source_target_pairs={{0,4},{4,0},{8,12},{12,8},{16,20},{20,16},{24,28},{28,24},{1,5},{5... | collective-permute-start | bytes 3145736 | tf_op jit(solution)/shard_map/ppermute | solution.py:151
  315.6 43.4 %collective-permute-start.50 = (bf16[4,128,1024]{2,1,0:T(8,128)(2,1)}, bf16[4,128,1024]{2,1,0:T(8,128)(2,1)}, u32[]{:S(2)}, u32[]{:S(2)}) collective-permute-start(bf16[4,128,1024]{2,1,0:T(8,128)(2,1)} %add_convert_fusion), channel_id=1, source_target_pairs={{0,2},{1,3},{2,0},{3,1},{4,6},{5,7},{6,4},{7,5},{8,10},{9,11},{10,... | collective-permute-start | bytes 3145736 | tf_op jit(solution)/shard_map/ppermute | solution.py:151
  354.9 65.5 %collective-permute-start.52 = (bf16[256,1024]{1,0:T(8,128)(2,1)}, bf16[256,1024]{1,0:T(8,128)(2,1)}, u32[]{:S(2)}, u32[]{:S(2)}) collective-permute-start(bf16[256,1024]{1,0:T(8,128)(2,1)} %get-tuple-element.365), channel_id=1, source_target_pairs={{0,2},{1,3},{2,0},{3,1},{4,6},{5,7},{6,4},{7,5},{8,10},{9,11},{10,... | collective-permute-start | bytes 1572872 | tf_op jit(solution)/shard_map/ppermute | solution.py:151
  357.8 51.0 %collective-permute-start.58 = (f32[64,1024]{1,0:T(8,128)}, f32[64,1024]{1,0:T(8,128)}, u32[]{:S(2)}, u32[]{:S(2)}) collective-permute-start(f32[64,1024]{1,0:T(8,128)} %get-tuple-element.374), channel_id=1, source_target_pairs={{0,2},{1,3},{2,0},{3,1},{4,6},{5,7},{6,4},{7,5},{8,10},{9,11},{10,... | collective-permute-start | bytes 786440 | tf_op jit(solution)/shard_map/ppermute | solution.py:151
  363.6 58.0 %collective-permute-start.53 = (bf16[128,1024]{1,0:T(8,128)(2,1)}, bf16[128,1024]{1,0:T(8,128)(2,1)}, u32[]{:S(2)}, u32[]{:S(2)}) collective-permute-start(bf16[128,1024]{1,0:T(8,128)(2,1)} %get-tuple-element.370), channel_id=1, source_target_pairs={{0,8},{4,12},{8,0},{12,4},{16,24},{20,28},{24,16},{28,20},{1,9},{5... | collective-permute-start | bytes 786440 | tf_op jit(solution)/shard_map/ppermute | solution.py:151
  364.0 57.5 %collective-permute-start.54 = (bf16[128,1024]{1,0:T(8,128)(2,1)}, bf16[128,1024]{1,0:T(8,128)(2,1)}, u32[]{:S(2)}, u32[]{:S(2)}) collective-permute-start(bf16[128,1024]{1,0:T(8,128)(2,1)} %get-tuple-element.369), channel_id=1, source_target_pairs={{0,16},{4,20},{8,24},{12,28},{16,0},{20,4},{24,8},{28,12},{1,17},{... | collective-permute-start | bytes 786440 | tf_op jit(solution)/shard_map/ppermute | solution.py:151
  412.9 26.5 %collective-permute-start.51 = (bf16[256,1024]{1,0:T(8,128)(2,1)S(1)}, bf16[256,1024]{1,0:T(8,128)(2,1)S(1)}, u32[]{:S(2)}, u32[]{:S(2)}) collective-permute-start(bf16[256,1024]{1,0:T(8,128)(2,1)S(1)} %get-tuple-element.367), channel_id=1, source_target_pairs={{0,2},{1,3},{2,0},{3,1},{4,6},{5,7},{6,4},{7,5},{8,10},{9,11},{10,... | collective-permute-start | bytes 1572872 | tf_op jit(solution)/shard_map/ppermute | solution.py:151
  (135 other events, 1244.7 us)

commit v3 on v2

--- a/solution.py
+++ b/solution.py
@@ -1361,16 +1361,16 @@
     projected[1] = run(project, normed, bias_qkv, 1, Weight(qkv_other))
     wait_for(out_other)
     mixed[1], totals[1] = run(team_attend, projected[1], 1, block)
+    z_down = join(z_down, z_down_came)
+    y_down, xz_down = over_y(z_down), over_x(z_down)
+    z_up_other = join(unit_up_other, z_up_other)
+    z_up_other_came = over_z(z_up_other, 2)
     out = Weight(full(z_out, y_out), ((out_other, 0, 512, 0), (out_other, 4, 512, 0)))
     sent = jnp.concatenate([m[own_rows:] for m in mixed], axis=1)
     mixed_rows = jnp.concatenate([m[:own_rows] for m in mixed] + [over_core(sent)], axis=1)
     middle, norm_own = run(out_and_norm, mixed_rows, own_tokens, vectors, out)
     norm_other = over_core(norm_own)
     wait_for(norm_other)
-    z_down = join(z_down, z_down_came)
-    y_down, xz_down = over_y(z_down), over_x(z_down)
-    z_up_other = join(unit_up_other, z_up_other)
-    z_up_other_came = over_z(z_up_other, 2)
     norm_all = jnp.concatenate([norm_own, norm_other])
 
     act, slope, grad_pre, pre_sums = ([None, None] for _ in range(4))
@@ -1383,9 +1383,9 @@
         return run(weight_grad, first, count, act[part], [(grad_all, 1024, 0)])
 
     act[0], slope[0] = run(feed_up, norm_own, norm_other, bias_up, 0, Weight(full(z_up, y_up)))
-    down_kept = down_grad(0, 0, 8)
     z_up_other = join(z_up_other, z_up_other_came)
     y_up_other = over_y(z_up_other)
+    down_kept = down_grad(0, 0, 8)
     up = [full(z_up, y_up), full(z_up_other, y_up_other)]
     xy_down = over_x(y_down)
     down = [full(z_down, y_down), full(xz_down, xy_down)]
@@ -1400,10 +1400,10 @@
     for i in (1, 0):
         down_sent[i] = down_grad(1, 4 * i, 4)
     down_came = [over_x(sent) for sent in down_sent]
-    wait_for(up_came[0])
     grad_pre[1], pre_sums[1] = run(
         feed_down_back, grad_own, grad_other, slope[1], Weight(down[1])
     )
+    wait_for(up_came[0])
     up_sent[1] = up_grad(1, 4)
     up_came[1] = over_y(up_sent[1])
     back_own, back_sent = run(
@@ -1462,16 +1462,20 @@
     down_far_came = over_z(down_far, 2)
     wait_for(down_far)
     other_kept = qkv_grad(heads_other, 0, 1)
-    up_total = added(low_sum(after(up_kept[0], order[0]), up_came[0]), up_x_came)
-    up_far = z_far(up_total)
-    up_far_came = over_z(up_far, 2)
-    wait_for(up_far)
     *heads_own, sums_own = run(team_back, projected[0], grad_mixed, totals[0], 0, block)
     other_x = low_sum(other_kept, other_y_came)
     other_x_came = over_x(other_x)
     wait_for(other_x)
     own_y_came = over_y(qkv_grad(heads_own, 4, 0))
-    down_sum, down_near = z_near(down_total, down_far_came)
+    up_total = added(low_sum(after(up_kept[0], order[0]), up_came[0]), up_x_came)
+    up_far = z_far(up_total)
+    up_far_came = over_z(up_far, 2)
+    wait_for(up_far)
+    fed_own, fed_sent = run(feed_down, act, Weight(*down))
+    block_own = jnp.where(
+        valid, middle + (fed_own + over_core(fed_sent).astype(f32)) + vectors[5:6], 0.0
+    ).astype(bf16)
+    down_sum, down_near = z_near(down_total, after(down_far_came, fed_own))
     down_near_came = over_z(down_near, 1)
     wait_for(down_near)
     first_own, first_sent = run(
@@ -1482,14 +1486,10 @@
     up_near_came = over_z(up_near, 1)
     wait_for(up_near, down_near_came)
     own_kept = qkv_grad(heads_own, 0, 0)
-    row_grad, first_sums = run(first_back, first_own, first_came, own_tokens, grad_middle, vectors)
     qkv_total = added(own_kept, own_y_came) + other_x_came.astype(f32)
     qkv_pieces = z_pieces(qkv_total)
     wait_for(*qkv_pieces)
-    fed_own, fed_sent = run(feed_down, act, Weight(*down))
-    block_own = jnp.where(
-        valid, middle + (fed_own + over_core(fed_sent).astype(f32)) + vectors[5:6], 0.0
-    ).astype(bf16)
+    row_grad, first_sums = run(first_back, first_own, first_came, own_tokens, grad_middle, vectors)
 
     def to_devices(rows):
         return flipped(jnp.stack([rows[:block], over_x(rows[block:])]), x)
@@ -1532,14 +1532,8 @@
         + [up_vector, head_vector(0), head_vector(1), first_sums[0], first_sums[1]],
         axis=1,
     )
-    totals = after(totals, *qkv_pieces)
-
-    def summed(value):
-        for axis, bit in (("seq", 1), ("seq", 2), ("fsdp", 1), ("fsdp", 2), ("fsdp", 4)):
-            value = value + exchange(value, axis, bit)
-        return value
-
-    totals = lax.cond(length > 0, summed, lambda v: v, totals)
+    for step in (over_core, over_x, over_y, partial(over_z, k=1), partial(over_z, k=2)):
+        totals = totals + step(totals)
     totals = one_of(totals, f * 4 + s)
     piece = lambda i: totals[i * 32 : (i + 1) * 32]
     return (

time: 449 us -> 431 us (0.960)
  waiting for transfers between devices: 124 us -> 85.3 us
  starting transfers between devices: 56.6 us -> 62.4 us
  local copies, waits for them, and re-layouts: 49.3 us -> 54.7 us
  Pallas kernels: 168 us -> 173 us
    ppermute x59, waiting for transfers between devices: 124 us -> 85.3 us  [exchange(): lax.ppermute(value, axis, [(i, i ^ bit) for i in range(lax.axis_size(axis...]
    unnamed x214 -> x222, local copies, waits for them, and re-layouts: 21.7 us -> 28.9 us
    ppermute x59, starting transfers between devices: 56.6 us -> 62.4 us  [exchange(): lax.ppermute(value, axis, [(i, i ^ bit) for i in range(lax.axis_size(axis...]
  transfers between devices with their start and end apart: 59 -> 59, of which waited for: 29 -> 27; matrix products, arithmetic and copies ran while one was open for 14% -> 16% of each run, Pallas kernels for 38% -> 41%
where the time goes in v3:
time: 431 us; the launch traced here: 422 us
  Pallas kernels  173 us (40%)
  waiting for transfers between devices  85.3 us (20%)
  starting transfers between devices  62.4 us (14%)
  local copies, waits for them, and re-layouts  54.7 us (13%)
  other arithmetic  43.6 us (10%)
    pallas_call x29, Pallas kernels, grid_call(): pl.pallas_call(kernel, name=name, grid_spec=pltpu.PrefetchScalarGridSpec(...  114 us
    ppermute x59, waiting for transfers between devices, exchange(): lax.ppermute(value, axis, [(i, i ^ bit) for i in range(lax.axis_size(axis...  85.3 us
    ppermute x59, starting transfers between devices, exchange(): lax.ppermute(value, axis, [(i, i ^ bit) for i in range(lax.axis_size(axis...  62.4 us
    unnamed x222, local copies, waits for them, and re-layouts  28.9 us
    pallas_call x2, Pallas kernels, team_back(): pl.pallas_call(partial(team_back_kernel, part), name='team_back', grid_sp...  28.7 us
    pallas_call x2, Pallas kernels, team_attend(): pl.pallas_call(partial(team_attend_kernel, part), name='team_attend', gri...  21.7 us
  transfers between devices with their start and end apart: 59, of which 27 were waited for; matrix products, arithmetic and copies ran while one was open for 16% of the time, Pallas kernels for 41%

profile of v3, /device:TPU:0, one launch (start us, length us, event | category | flops | bytes accessed | tf_op | source)
XLA Modules:
  0.0 422.2 jit_solution(12449628423702651735)
XLA Ops:
  31.4 8.1 %collective-permute-done.16.second_ref = bf16[2,144,768]{2,1,0:T(8,128)(2,1)S(1)} collective-permute-done((bf16[2,144,768]{2,1,0:T(8,128)(2,1)S(1)}, bf16[2,144,768]{2,1,0:T(8,128)(2,1)S(1)}, u32[]{:S(2)}, u32[]{:S(2)}) %collective-permute-start.16) | collective-permute-done | bytes 442400 | tf_op jit(solution)/shard_map/ppermute | solution.py:151
  42.8 3.9 collective-permute-start.19
  65.5 3.6 first_norm.1.lhs_ref.left_ref
  69.1 4.5 %project.2.q_ref.k_ref.v_ref = bf16[1024,768]{1,0:T(8,128)(2,1)S(1)} custom-call(s32[3]{0:T(128)S(1)} %pad_add_fusion.order, bf16[1024,1024]{1,0:T(8,128)(2,1)S(1)} %first_norm.1.lhs_ref.left_ref, f32[2,768]{1,0:T(2,128)S(1)} %get-tuple-element.262.bias_ref, bf16[4,144,768]{2,1,0:T(8,128)(2,1)} %joined.11.mine_ref.rest_0_.rest_6_, ...), custom_call_target="tpu_custom_call" | custom-call | flops 10000000000 | bytes 20000000 | tf_op jit(solution)/shard_map/project/pallas_call | solution.py:551
  73.7 10.8 %team_attend.2 = (bf16[1024,256]{1,0:T(8,128)(2,1)S(1)}, f32[2,8,1024]{2,1,0:T(8,128)S(1)}) custom-call(s32[3]{0:T(128)S(1)} %pad_add_fusion.order, bf16[1024,768]{1,0:T(8,128)(2,1)S(1)} %project.2.q_ref.k_ref.v_ref, bf16[1024,768]{1,0:T(8,128)(2,1)S(1)} %project.2.q_ref.k_ref.v_ref, bf16[1024,768]{1,0:T(8,128)(2,1)S(1)} %project.2.q_ref.k_ref.v_ref), custom_call_target="tpu_custom_call" | custom-call | flops 10000000000 | bytes 20000000 | tf_op jit(solution)/shard_map/team_attend/pallas_call | solution.py:1058
  91.9 4.0 conditional.17
  97.0 5.3 %collective-permute-done.25.rest_1_.rest_9_ = bf16[4,144,768]{2,1,0:T(8,128)(2,1)} collective-permute-done((bf16[4,144,768]{2,1,0:T(8,128)(2,1)}, bf16[4,144,768]{2,1,0:T(8,128)(2,1)}, u32[]{:S(2)}, u32[]{:S(2)}) %collective-permute-start.25) | collective-permute-done | bytes 884768 | tf_op jit(solution)/shard_map/ppermute | solution.py:151
  103.9 4.4 %project.3.q_ref.k_ref.v_ref = bf16[1024,768]{1,0:T(8,128)(2,1)S(1)} custom-call(s32[3]{0:T(128)S(1)} %pad_add_fusion.order, bf16[1024,1024]{1,0:T(8,128)(2,1)S(1)} %copy-done.47, f32[2,768]{1,0:T(2,128)S(1)} %get-tuple-element.262.bias_ref, bf16[4,144,768]{2,1,0:T(8,128)(2,1)} %collective-permute-done.24.rest_0_.rest_8_, ...), custom_call_target="tpu_custom_call" | custom-call | flops 10000000000 | bytes 20000000 | tf_op jit(solution)/shard_map/project/pallas_call | solution.py:551
  108.3 10.9 %team_attend.3 = (bf16[1024,256]{1,0:T(8,128)(2,1)S(1)}, f32[2,8,1024]{2,1,0:T(8,128)S(1)}) custom-call(s32[3]{0:T(128)S(1)} %pad_add_fusion.order, bf16[1024,768]{1,0:T(8,128)(2,1)S(1)} %project.3.q_ref.k_ref.v_ref, bf16[1024,768]{1,0:T(8,128)(2,1)S(1)} %project.3.q_ref.k_ref.v_ref, bf16[1024,768]{1,0:T(8,128)(2,1)S(1)} %project.3.q_ref.k_ref.v_ref), custom_call_target="tpu_custom_call" | custom-call | flops 10000000000 | bytes 20000000 | tf_op jit(solution)/shard_map/team_attend/pallas_call | solution.py:1058
  142.5 7.7 %feed_up.2 = (bf16[1024,1024]{1,0:T(8,128)(2,1)S(1)}, bf16[1024,1024]{1,0:T(8,128)(2,1)S(1)}) custom-call(s32[3]{0:T(128)S(1)} %pad_add_fusion.order, bf16[512,1024]{1,0:T(8,128)(2,1)S(1)} %copy-done.86, bf16[512,1024]{1,0:T(8,128)(2,1)} %get-tuple-element.398.other_ref, f32[2,1024]{1,0:T(2,128)S(1)} %get-tuple-element.286.bias_ref, ...), custom_call_target="tpu_custom_call" | custom-call | flops 10000000000 | bytes 20000000 | tf_op jit(solution)/shard_map/feed_up/pallas_call | solution.py:551
  153.3 3.6 weight_grad.13
  159.0 5.8 %feed_down_back.2 = (bf16[1024,1024]{1,0:T(8,128)(2,1)S(1)}, f32[8,1024]{1,0:T(8,128)S(1)}) custom-call(s32[3]{0:T(128)S(1)} %pad_add_fusion.order, bf16[512,1024]{1,0:T(8,128)(2,1)S(1)} %copy-done.78, bf16[512,1024]{1,0:T(8,128)(2,1)} %get-tuple-element.395.other_ref, bf16[1024,1024]{1,0:T(8,128)(2,1)S(1)} %get-tuple-element.292.slope_ref, ...), custom_call_target="tpu_custom_call" | custom-call | flops 10000000000 | bytes 20000000 | tf_op jit(solution)/shard_map/feed_down_back/pallas_call | solution.py:551
  171.8 6.6 %collective-permute-done.32.rest_1_.rest_5_ = bf16[4,128,1024]{2,1,0:T(8,128)(2,1)S(1)} collective-permute-done((bf16[4,128,1024]{2,1,0:T(8,128)(2,1)S(1)}, bf16[4,128,1024]{2,1,0:T(8,128)(2,1)S(1)}, u32[]{:S(2)}, u32[]{:S(2)}) %collective-permute-start.32) | collective-permute-done | bytes 1048608 | tf_op jit(solution)/shard_map/ppermute | solution.py:151
  178.4 6.6 %feed_up.3 = (bf16[1024,1024]{1,0:T(8,128)(2,1)S(1)}, bf16[1024,1024]{1,0:T(8,128)(2,1)S(1)}) custom-call(s32[3]{0:T(128)S(1)} %pad_add_fusion.order, bf16[512,1024]{1,0:T(8,128)(2,1)S(1)} %copy-done.86, bf16[512,1024]{1,0:T(8,128)(2,1)} %get-tuple-element.398.other_ref, f32[2,1024]{1,0:T(2,128)S(1)} %get-tuple-element.286.bias_ref, ...), custom_call_target="tpu_custom_call" | custom-call | flops 10000000000 | bytes 20000000 | tf_op jit(solution)/shard_map/feed_up/pallas_call | solution.py:551
  192.9 3.5 collective-permute-done.34.rest_1_.rest_5_
  196.4 5.9 %feed_down_back.3 = (bf16[1024,1024]{1,0:T(8,128)(2,1)S(1)}, f32[8,1024]{1,0:T(8,128)S(1)}) custom-call(s32[3]{0:T(128)S(1)} %pad_add_fusion.order, bf16[512,1024]{1,0:T(8,128)(2,1)S(1)} %copy-done.78, bf16[512,1024]{1,0:T(8,128)(2,1)} %get-tuple-element.395.other_ref, bf16[1024,1024]{1,0:T(8,128)(2,1)S(1)} %get-tuple-element.301.slope_ref, ...), custom_call_target="tpu_custom_call" | custom-call | flops 10000000000 | bytes 20000000 | tf_op jit(solution)/shard_map/feed_down_back/pallas_call | solution.py:551
  206.1 9.8 %feed_up_back.1 = (f32[512,1024]{1,0:T(8,128)S(1)}, bf16[512,1024]{1,0:T(8,128)(2,1)}) custom-call(s32[3]{0:T(128)S(1)} %pad_add_fusion.order, bf16[1024,1024]{1,0:T(8,128)(2,1)S(1)} %get-tuple-element.293.rest_0_, bf16[1024,1024]{1,0:T(8,128)(2,1)S(1)} %get-tuple-element.302.rest_0_.rest_1_, bf16[4,128,1024]{2,1,0:T(8,128)(2,1)} %joined.15.rest_0_.rest_2_, ...), custom_call_target="tpu_custom_call" | custom-call | flops 10000000000 | bytes 20000000 | tf_op jit(solution)/shard_map/feed_up_back/pallas_call | solution.py:551
  217.2 3.9 conditional.20
  228.1 5.2 %middle_back.1 = (f32[512,1024]{1,0:T(8,128)S(1)}, bf16[512,1024]{1,0:T(8,128)(2,1)S(1)}, bf16[512,512]{1,0:T(8,128)(2,1)S(1)}, bf16[512,512]{1,0:T(8,128)(2,1)}, f32[4,8,1024]{2,1,0:T(8,128)S(1)}) custom-call(s32[3]{0:T(128)S(1)} %pad_add_fusion.order, f32[512,1024]{1,0:T(8,128)S(1)} %copy-done.39, bf16[512,1024]{1,0:T(8,128)(2,1)S(1)} %copy-done.109, ...), custom_call_target="tpu_custom_call" | custom-call | flops 10000000000 | bytes 20000000 | tf_op jit(solution)/shard_map/middle_back/pallas_call | solution.py:551
  251.4 14.3 %team_back.2 = (bf16[1024,256]{1,0:T(8,128)(2,1)S(1)}, bf16[1024,256]{1,0:T(8,128)(2,1)S(1)}, bf16[1024,256]{1,0:T(8,128)(2,1)S(1)}, f32[2,2,8,128]{3,2,1,0:T(8,128)S(1)}) custom-call(s32[3]{0:T(128)S(1)} %pad_add_fusion.order, bf16[1024,768]{1,0:T(8,128)(2,1)S(1)} %copy-done.56, bf16[1024,768]{1,0:T(8,128)(2,1)S(1)} %copy-done.56, ...), custom_call_target="tpu_custom_call" | custom-call | flops 10000000000 | bytes 20000000 | tf_op jit(solution)/shard_map/team_back/pallas_call | solution.py:1129
  265.7 3.2 weight_grad.22
  281.2 14.4 %team_back.3 = (bf16[1024,256]{1,0:T(8,128)(2,1)S(1)}, bf16[1024,256]{1,0:T(8,128)(2,1)S(1)}, bf16[1024,256]{1,0:T(8,128)(2,1)S(1)}, f32[2,2,8,128]{3,2,1,0:T(8,128)S(1)}) custom-call(s32[3]{0:T(128)S(1)} %pad_add_fusion.order, bf16[1024,768]{1,0:T(8,128)(2,1)S(1)} %copy-done.54, bf16[1024,768]{1,0:T(8,128)(2,1)S(1)} %copy-done.54, ...), custom_call_target="tpu_custom_call" | custom-call | flops 10000000000 | bytes 20000000 | tf_op jit(solution)/shard_map/team_back/pallas_call | solution.py:1129
  304.2 3.6 weight_grad.24
  315.6 8.3 %feed_down.1 = (f32[512,1024]{1,0:T(8,128)S(1)}, bf16[512,1024]{1,0:T(8,128)(2,1)}) custom-call(s32[3]{0:T(128)S(1)} %pad_add_fusion.order, bf16[1024,1024]{1,0:T(8,128)(2,1)S(1)} %copy-done.41, bf16[1024,1024]{1,0:T(8,128)(2,1)S(1)} %copy-done.43, bf16[4,128,1024]{2,1,0:T(8,128)(2,1)} %joined.17.rest_0_.rest_2_, bf16[4,128,1024]{2,1,0:T(8,128)(2,1)S(1)} %copy-done.25, ...), custom_call_target="tpu_custom_call" | custom-call | flops 10000000000 | bytes 20000000 | tf_op jit(solution)/shard_map/feed_down/pallas_call | solution.py:551
  326.9 4.1 collective-permute-start.45
  331.0 3.8 conditional.23
  339.1 8.2 %project_back.1 = (f32[512,1024]{1,0:T(8,128)S(1)}, bf16[512,1024]{1,0:T(8,128)(2,1)}) custom-call(s32[3]{0:T(128)S(1)} %pad_add_fusion.order, bf16[1024,256]{1,0:T(8,128)(2,1)S(1)} %copy-done.63, bf16[1024,256]{1,0:T(8,128)(2,1)S(1)} %copy-done.66, bf16[1024,256]{1,0:T(8,128)(2,1)S(1)} %copy-done.69, bf16[1024,256]{1,0:T(8,128)(2,1)S(1)} %copy-done.72, ...), custom_call_target="tpu_custom_call" | custom-call | flops 10000000000 | bytes 20000000 | tf_op jit(solution)/shard_map/project_back/pallas_call | solution.py:551
  350.0 3.9 conditional.24
  362.6 6.7 %collective-permute-done.42 = bf16[256,1024]{1,0:T(8,128)(2,1)S(1)} collective-permute-done((bf16[256,1024]{1,0:T(8,128)(2,1)S(1)}, bf16[256,1024]{1,0:T(8,128)(2,1)S(1)}, u32[]{:S(2)}, u32[]{:S(2)}) %collective-permute-start.42) | collective-permute-done | bytes 524320 | tf_op jit(solution)/shard_map/ppermute | solution.py:151
  372.2 3.9 fusion.12
  392.2 3.6 collective-permute-done.50
  409.7 3.8 collective-permute-done.56
  (477 shorter events, 261.8 us)
Async XLA Ops:
  3.1 24.3 %collective-permute-start.15 = (bf16[256,1024]{1,0:T(8,128)(2,1)}, bf16[256,1024]{1,0:T(8,128)(2,1)}, u32[]{:S(2)}, u32[]{:S(2)}) collective-permute-start(bf16[256,1024]{1,0:T(8,128)(2,1)} %get-tuple-element.371), channel_id=1, source_target_pairs={{0,2},{1,3},{2,0},{3,1},{4,6},{5,7},{6,4},{7,5},{8,10},{9,11},{10,... | collective-permute-start | bytes 1572872 | tf_op jit(solution)/shard_map/ppermute | solution.py:151
  18.3 21.3 %collective-permute-start.16 = (bf16[2,144,768]{2,1,0:T(8,128)(2,1)S(1)}, bf16[2,144,768]{2,1,0:T(8,128)(2,1)S(1)}, u32[]{:S(2)}, u32[]{:S(2)}) collective-permute-start(bf16[2,144,768]{2,1,0:T(8,128)(2,1)S(1)} %joined.10.first_ref), channel_id=1, source_target_pairs={{0,16},{4,20},{8,24},{12,28},{16,0},{20,4},{24,8},{28,12},{1,17},{... | collective-permute-start | bytes 1327112 | tf_op jit(solution)/shard_map/ppermute | solution.py:151
  27.4 19.2 %collective-permute-start.18 = (bf16[256,1024]{1,0:T(8,128)(2,1)S(1)}, bf16[256,1024]{1,0:T(8,128)(2,1)}, u32[]{:S(2)}, u32[]{:S(2)}) collective-permute-start(bf16[256,1024]{1,0:T(8,128)(2,1)S(1)} %dynamic-slice_bitcast_fusion.2), channel_id=1, source_target_pairs={{0,2},{1,3},{2,0},{3,1},{4,6},{5,7},{6,4},{7,5},{8,10},{9,11},{10,... | collective-permute-start | bytes 1572872 | tf_op jit(solution)/shard_map/ppermute | solution.py:151
  40.6 23.0 %collective-permute-start.21 = (bf16[4,144,768]{2,1,0:T(8,128)(2,1)}, bf16[4,144,768]{2,1,0:T(8,128)(2,1)}, u32[]{:S(2)}, u32[]{:S(2)}) collective-permute-start(bf16[4,144,768]{2,1,0:T(8,128)(2,1)} %joined.11.mine_ref.rest_0_.rest_6_), channel_id=1, source_target_pairs={{0,4},{4,0},{8,12},{12,8},{16,20},{20,16},{24,28},{28,24},{1,5},{5... | collective-permute-start | bytes 2654216 | tf_op jit(solution)/shard_map/ppermute | solution.py:151
  42.2 54.8 %collective-permute-start.24 = (bf16[4,144,768]{2,1,0:T(8,128)(2,1)}, bf16[4,144,768]{2,1,0:T(8,128)(2,1)}, u32[]{:S(2)}, u32[]{:S(2)}) collective-permute-start(bf16[4,144,768]{2,1,0:T(8,128)(2,1)} %joined.11.mine_ref.rest_0_.rest_6_), channel_id=1, source_target_pairs={{0,2},{1,3},{2,0},{3,1},{4,6},{5,7},{6,4},{7,5},{8,10},{9,11},{10,... | collective-permute-start | bytes 2654216 | tf_op jit(solution)/shard_map/ppermute | solution.py:151
  56.0 34.7 %collective-permute-start.26 = (bf16[4,128,512]{2,1,0:T(8,128)(2,1)S(1)}, bf16[4,128,512]{2,1,0:T(8,128)(2,1)S(1)}, u32[]{:S(2)}, u32[]{:S(2)}) collective-permute-start(bf16[4,128,512]{2,1,0:T(8,128)(2,1)S(1)} %joined.14.rest_0_), channel_id=1, source_target_pairs={{0,4},{4,0},{8,12},{12,8},{16,20},{20,16},{24,28},{28,24},{1,5},{5... | collective-permute-start | bytes 1572872 | tf_op jit(solution)/shard_map/ppermute | solution.py:151
  56.6 28.8 %collective-permute-start.22 = (bf16[2,128,1024]{2,1,0:T(8,128)(2,1)S(1)}, bf16[2,128,1024]{2,1,0:T(8,128)(2,1)S(1)}, u32[]{:S(2)}, u32[]{:S(2)}) collective-permute-start(bf16[2,128,1024]{2,1,0:T(8,128)(2,1)S(1)} %joined.13.first_ref), channel_id=1, source_target_pairs={{0,16},{4,20},{8,24},{12,28},{16,0},{20,4},{24,8},{28,12},{1,17},{... | collective-permute-start | bytes 1572872 | tf_op jit(solution)/shard_map/ppermute | solution.py:151
  58.5 27.9 %collective-permute-start.23 = (bf16[1,128,1024]{2,1,0:T(8,128)(2,1)S(1)}, bf16[1,128,1024]{2,1,0:T(8,128)(2,1)S(1)}, u32[]{:S(2)}, u32[]{:S(2)}) collective-permute-start(bf16[1,128,1024]{2,1,0:T(8,128)(2,1)S(1)} %copy-done.33), channel_id=1, source_target_pairs={{0,8},{4,12},{8,0},{12,4},{16,24},{20,28},{24,16},{28,20},{1,9},{5... | collective-permute-start | bytes 786440 | tf_op jit(solution)/shard_map/ppermute | solution.py:151
  86.5 32.7 %collective-permute-start.27 = (bf16[2,128,1024]{2,1,0:T(8,128)(2,1)S(1)}, bf16[2,128,1024]{2,1,0:T(8,128)(2,1)}, u32[]{:S(2)}, u32[]{:S(2)}) collective-permute-start(bf16[2,128,1024]{2,1,0:T(8,128)(2,1)S(1)} %joined.16.first_ref), channel_id=1, source_target_pairs={{0,16},{4,20},{8,24},{12,28},{16,0},{20,4},{24,8},{28,12},{1,17},{... | collective-permute-start | bytes 1572872 | tf_op jit(solution)/shard_map/ppermute | solution.py:151
  89.3 53.1 %collective-permute-start.29 = (bf16[4,128,1024]{2,1,0:T(8,128)(2,1)}, bf16[4,128,1024]{2,1,0:T(8,128)(2,1)}, u32[]{:S(2)}, u32[]{:S(2)}) collective-permute-start(bf16[4,128,1024]{2,1,0:T(8,128)(2,1)} %joined.15.rest_0_.rest_2_), channel_id=1, source_target_pairs={{0,4},{4,0},{8,12},{12,8},{16,20},{20,16},{24,28},{28,24},{1,5},{5... | collective-permute-start | bytes 3145736 | tf_op jit(solution)/shard_map/ppermute | solution.py:151
  95.9 26.2 %collective-permute-start.28 = (bf16[1,128,1024]{2,1,0:T(8,128)(2,1)}, bf16[1,128,1024]{2,1,0:T(8,128)(2,1)S(1)}, u32[]{:S(2)}, u32[]{:S(2)}) collective-permute-start(bf16[1,128,1024]{2,1,0:T(8,128)(2,1)} %copy-done.30), channel_id=1, source_target_pairs={{0,8},{4,12},{8,0},{12,4},{16,24},{20,28},{24,16},{28,20},{1,9},{5... | collective-permute-start | bytes 786440 | tf_op jit(solution)/shard_map/ppermute | solution.py:151
  123.1 27.2 %collective-permute-start.30 = (bf16[2,128,1024]{2,1,0:T(8,128)(2,1)}, bf16[2,128,1024]{2,1,0:T(8,128)(2,1)}, u32[]{:S(2)}, u32[]{:S(2)}) collective-permute-start(bf16[2,128,1024]{2,1,0:T(8,128)(2,1)} %joined.18.first_ref), channel_id=1, source_target_pairs={{0,16},{4,20},{8,24},{12,28},{16,0},{20,4},{24,8},{28,12},{1,17},{... | collective-permute-start | bytes 1572872 | tf_op jit(solution)/shard_map/ppermute | solution.py:151
  125.3 31.7 %collective-permute-start.31 = (bf16[4,128,1024]{2,1,0:T(8,128)(2,1)}, bf16[4,128,1024]{2,1,0:T(8,128)(2,1)S(1)}, u32[]{:S(2)}, u32[]{:S(2)}) collective-permute-start(bf16[4,128,1024]{2,1,0:T(8,128)(2,1)} %joined.17.rest_0_.rest_2_), channel_id=1, source_target_pairs={{0,4},{4,0},{8,12},{12,8},{16,20},{20,16},{24,28},{28,24},{1,5},{5... | collective-permute-start | bytes 3145736 | tf_op jit(solution)/shard_map/ppermute | solution.py:151
  126.8 66.0 %collective-permute-start.33 = (bf16[4,128,1024]{2,1,0:T(8,128)(2,1)}, bf16[4,128,1024]{2,1,0:T(8,128)(2,1)}, u32[]{:S(2)}, u32[]{:S(2)}) collective-permute-start(bf16[4,128,1024]{2,1,0:T(8,128)(2,1)} %joined.17.rest_0_.rest_2_), channel_id=1, source_target_pairs={{0,2},{1,3},{2,0},{3,1},{4,6},{5,7},{6,4},{7,5},{8,10},{9,11},{10,... | collective-permute-start | bytes 3145736 | tf_op jit(solution)/shard_map/ppermute | solution.py:151
  152.3 26.1 %collective-permute-start.32 = (bf16[4,128,1024]{2,1,0:T(8,128)(2,1)S(1)}, bf16[4,128,1024]{2,1,0:T(8,128)(2,1)S(1)}, u32[]{:S(2)}, u32[]{:S(2)}) collective-permute-start(bf16[4,128,1024]{2,1,0:T(8,128)(2,1)S(1)} %joined.19.rest_0_.rest_4_), channel_id=1, source_target_pairs={{0,4},{4,0},{8,12},{12,8},{16,20},{20,16},{24,28},{28,24},{1,5},{5... | collective-permute-start | bytes 3145736 | tf_op jit(solution)/shard_map/ppermute | solution.py:151
  166.9 35.4 %collective-permute-start.35 = (bf16[4,128,1024]{2,1,0:T(8,128)(2,1)S(1)}, bf16[4,128,1024]{2,1,0:T(8,128)(2,1)S(1)}, u32[]{:S(2)}, u32[]{:S(2)}) collective-permute-start(bf16[4,128,1024]{2,1,0:T(8,128)(2,1)S(1)} %weight_grad.14), channel_id=1, source_target_pairs={{0,4},{4,0},{8,12},{12,8},{16,20},{20,16},{24,28},{28,24},{1,5},{5... | collective-permute-start | bytes 3145736 | tf_op jit(solution)/shard_map/ppermute | solution.py:151
  170.2 26.1 %collective-permute-start.34 = (bf16[4,128,1024]{2,1,0:T(8,128)(2,1)S(1)}, bf16[4,128,1024]{2,1,0:T(8,128)(2,1)S(1)}, u32[]{:S(2)}, u32[]{:S(2)}) collective-permute-start(bf16[4,128,1024]{2,1,0:T(8,128)(2,1)S(1)} %copy-done.24), channel_id=1, source_target_pairs={{0,2},{1,3},{2,0},{3,1},{4,6},{5,7},{6,4},{7,5},{8,10},{9,11},{10,... | collective-permute-start | bytes 3145736 | tf_op jit(solution)/shard_map/ppermute | solution.py:151
  187.9 57.9 %collective-permute-start.37 = (bf16[4,128,1024]{2,1,0:T(8,128)(2,1)}, bf16[4,128,1024]{2,1,0:T(8,128)(2,1)}, u32[]{:S(2)}, u32[]{:S(2)}) collective-permute-start(bf16[4,128,1024]{2,1,0:T(8,128)(2,1)} %weight_grad.16), channel_id=1, source_target_pairs={{0,2},{1,3},{2,0},{3,1},{4,6},{5,7},{6,4},{7,5},{8,10},{9,11},{10,... | collective-permute-start | bytes 3145736 | tf_op jit(solution)/shard_map/ppermute | solution.py:151
  192.3 78.6 %collective-permute-start.38 = (bf16[4,128,1024]{2,1,0:T(8,128)(2,1)}, bf16[4,128,1024]{2,1,0:T(8,128)(2,1)}, u32[]{:S(2)}, u32[]{:S(2)}) collective-permute-start(bf16[4,128,1024]{2,1,0:T(8,128)(2,1)} %weight_grad.17), channel_id=1, source_target_pairs={{0,2},{1,3},{2,0},{3,1},{4,6},{5,7},{6,4},{7,5},{8,10},{9,11},{10,... | collective-permute-start | bytes 3145736 | tf_op jit(solution)/shard_map/ppermute | solution.py:151
  205.2 43.5 %collective-permute-start.36 = (bf16[4,128,1024]{2,1,0:T(8,128)(2,1)}, bf16[4,128,1024]{2,1,0:T(8,128)(2,1)}, u32[]{:S(2)}, u32[]{:S(2)}) collective-permute-start(bf16[4,128,1024]{2,1,0:T(8,128)(2,1)} %weight_grad.18), channel_id=1, source_target_pairs={{0,4},{4,0},{8,12},{12,8},{16,20},{20,16},{24,28},{28,24},{1,5},{5... | collective-permute-start | bytes 3145736 | tf_op jit(solution)/shard_map/ppermute | solution.py:151
  247.6 26.1 %collective-permute-start.39 = (bf16[4,128,1024]{2,1,0:T(8,128)(2,1)S(1)}, bf16[4,128,1024]{2,1,0:T(8,128)(2,1)S(1)}, u32[]{:S(2)}, u32[]{:S(2)}) collective-permute-start(bf16[4,128,1024]{2,1,0:T(8,128)(2,1)S(1)} %add_convert_fusion.3), channel_id=1, source_target_pairs={{0,4},{4,0},{8,12},{12,8},{16,20},{20,16},{24,28},{28,24},{1,5},{5... | collective-permute-start | bytes 3145736 | tf_op jit(solution)/shard_map/ppermute | solution.py:151
  268.9 29.4 %collective-permute-start.40 = (bf16[4,128,1024]{2,1,0:T(8,128)(2,1)S(1)}, bf16[4,128,1024]{2,1,0:T(8,128)(2,1)}, u32[]{:S(2)}, u32[]{:S(2)}) collective-permute-start(bf16[4,128,1024]{2,1,0:T(8,128)(2,1)S(1)} %weight_grad.22), channel_id=1, source_target_pairs={{0,4},{4,0},{8,12},{12,8},{16,20},{20,16},{24,28},{28,24},{1,5},{5... | collective-permute-start | bytes 3145736 | tf_op jit(solution)/shard_map/ppermute | solution.py:151
  269.9 38.0 %collective-permute-start.41 = (bf16[4,128,1024]{2,1,0:T(8,128)(2,1)}, bf16[4,128,1024]{2,1,0:T(8,128)(2,1)}, u32[]{:S(2)}, u32[]{:S(2)}) collective-permute-start(bf16[4,128,1024]{2,1,0:T(8,128)(2,1)} %add_convert_fusion.4), channel_id=1, source_target_pairs={{0,2},{1,3},{2,0},{3,1},{4,6},{5,7},{6,4},{7,5},{8,10},{9,11},{10,... | collective-permute-start | bytes 3145736 | tf_op jit(solution)/shard_map/ppermute | solution.py:151
  277.6 46.3 %collective-permute-start.43 = (bf16[2,128,1024]{2,1,0:T(8,128)(2,1)}, bf16[2,128,1024]{2,1,0:T(8,128)(2,1)}, u32[]{:S(2)}, u32[]{:S(2)}) collective-permute-start(bf16[2,128,1024]{2,1,0:T(8,128)(2,1)} %slice.291), channel_id=1, source_target_pairs={{0,16},{4,20},{8,24},{12,28},{16,0},{20,4},{24,8},{28,12},{1,17},{... | collective-permute-start | bytes 1572872 | tf_op jit(solution)/shard_map/ppermute | solution.py:151
  310.7 47.5 %collective-permute-start.44 = (bf16[2,128,1024]{2,1,0:T(8,128)(2,1)}, bf16[2,128,1024]{2,1,0:T(8,128)(2,1)}, u32[]{:S(2)}, u32[]{:S(2)}) collective-permute-start(bf16[2,128,1024]{2,1,0:T(8,128)(2,1)} %slice.290), channel_id=1, source_target_pairs={{0,16},{4,20},{8,24},{12,28},{16,0},{20,4},{24,8},{28,12},{1,17},{... | collective-permute-start | bytes 1572872 | tf_op jit(solution)/shard_map/ppermute | solution.py:151
  313.0 59.3 %collective-permute-start.46 = (bf16[4,128,1024]{2,1,0:T(8,128)(2,1)}, bf16[4,128,1024]{2,1,0:T(8,128)(2,1)}, u32[]{:S(2)}, u32[]{:S(2)}) collective-permute-start(bf16[4,128,1024]{2,1,0:T(8,128)(2,1)} %weight_grad.24), channel_id=1, source_target_pairs={{0,4},{4,0},{8,12},{12,8},{16,20},{20,16},{24,28},{28,24},{1,5},{5... | collective-permute-start | bytes 3145736 | tf_op jit(solution)/shard_map/ppermute | solution.py:151
  314.1 58.1 %collective-permute-start.47 = (bf16[4,128,1024]{2,1,0:T(8,128)(2,1)}, bf16[4,128,1024]{2,1,0:T(8,128)(2,1)}, u32[]{:S(2)}, u32[]{:S(2)}) collective-permute-start(bf16[4,128,1024]{2,1,0:T(8,128)(2,1)} %add_convert_fusion.1), channel_id=1, source_target_pairs={{0,2},{1,3},{2,0},{3,1},{4,6},{5,7},{6,4},{7,5},{8,10},{9,11},{10,... | collective-permute-start | bytes 3145736 | tf_op jit(solution)/shard_map/ppermute | solution.py:151
  326.9 29.0 %collective-permute-start.45 = (bf16[128,1024]{1,0:T(8,128)(2,1)}, bf16[128,1024]{1,0:T(8,128)(2,1)}, u32[]{:S(2)}, u32[]{:S(2)}) collective-permute-start(bf16[128,1024]{1,0:T(8,128)(2,1)} %fusion.9), channel_id=1, source_target_pairs={{0,8},{4,12},{8,0},{12,4},{16,24},{20,28},{24,16},{28,20},{1,9},{5... | collective-permute-start | bytes 786440 | tf_op jit(solution)/shard_map/ppermute | solution.py:151
  377.0 28.6 %collective-permute-start.53 = (bf16[128,1024]{1,0:T(8,128)(2,1)}, bf16[128,1024]{1,0:T(8,128)(2,1)}, u32[]{:S(2)}, u32[]{:S(2)}) collective-permute-start(bf16[128,1024]{1,0:T(8,128)(2,1)} %get-tuple-element.368), channel_id=1, source_target_pairs={{0,8},{4,12},{8,0},{12,4},{16,24},{20,28},{24,16},{28,20},{1,9},{5... | collective-permute-start | bytes 786440 | tf_op jit(solution)/shard_map/ppermute | solution.py:151
  377.0 28.6 %collective-permute-start.54 = (bf16[128,1024]{1,0:T(8,128)(2,1)}, bf16[128,1024]{1,0:T(8,128)(2,1)}, u32[]{:S(2)}, u32[]{:S(2)}) collective-permute-start(bf16[128,1024]{1,0:T(8,128)(2,1)} %get-tuple-element.367), channel_id=1, source_target_pairs={{0,16},{4,20},{8,24},{12,28},{16,0},{20,4},{24,8},{28,12},{1,17},{... | collective-permute-start | bytes 786440 | tf_op jit(solution)/shard_map/ppermute | solution.py:151
  379.3 26.4 %collective-permute-start.55 = (bf16[128,1024]{1,0:T(8,128)(2,1)}, bf16[128,1024]{1,0:T(8,128)(2,1)}, u32[]{:S(2)}, u32[]{:S(2)}) collective-permute-start(bf16[128,1024]{1,0:T(8,128)(2,1)} %get-tuple-element.366), channel_id=1, source_target_pairs={{0,24},{4,28},{8,16},{12,20},{16,8},{20,12},{24,0},{28,4},{1,25},{... | collective-permute-start | bytes 786440 | tf_op jit(solution)/shard_map/ppermute | solution.py:151
  391.1 29.3 %collective-permute-start.48 = (bf16[256,1024]{1,0:T(8,128)(2,1)S(1)}, bf16[256,1024]{1,0:T(8,128)(2,1)S(1)}, u32[]{:S(2)}, u32[]{:S(2)}) collective-permute-start(bf16[256,1024]{1,0:T(8,128)(2,1)S(1)} %get-tuple-element.365), channel_id=1, source_target_pairs={{0,2},{1,3},{2,0},{3,1},{4,6},{5,7},{6,4},{7,5},{8,10},{9,11},{10,... | collective-permute-start | bytes 1572872 | tf_op jit(solution)/shard_map/ppermute | solution.py:151
  (139 other events, 1121.1 us)
